TPU v7x, 32 devices: a whole 2x2x4 slice. The times are simulated.
32 devices in a mesh: dp: 8 (over y, x, core), tensor: 4 (over z).
Axes of the slice: x: 2, y: 2, z: 4, core: 2. Of those that a mesh axis runs over, the one named last changes fastest.
Arguments:
- inputs: bfloat16 [4096, 1024], P(('dp', 'tensor')), may hold values from -6 to 6
- segments: int32 [4096], P('dp'), may hold values from 0 to 7, never falling along the last dimension, each value on 1 to 2000 neighbouring positions
- mixers_norm_gain: float32 [1024], replicated, may hold values from 0.5 to 1.5
- query_weight: bfloat16 [1024, 512], P(None, 'tensor'), may hold values from -0.1875 to 0.1875
- key_weight: bfloat16 [1024, 128], replicated, may hold values from -0.1875 to 0.1875
- value_weight: bfloat16 [1024, 128], replicated, may hold values from -0.1875 to 0.1875
- attention_out: bfloat16 [512, 1024], P('tensor'), may hold values from -2 to 2
- mamba_gate: bfloat16 [1024, 1536], P(None, 'tensor'), may hold values from -0.1875 to 0.1875
- mamba_input: bfloat16 [1024, 1536], P(None, 'tensor'), may hold values from -0.1875 to 0.1875
- state_weight: bfloat16 [1024, 256], replicated, may hold values from -0.1875 to 0.1875
- step_weight: bfloat16 [1024, 24], P(None, 'tensor'), may hold values from -0.1875 to 0.1875
- kernel_input: float32 [4, 1536], P(None, 'tensor'), may hold values from -3 to 3
- kernel_state: float32 [4, 256], replicated, may hold values from -3 to 3
- offset_input: float32 [1536], P('tensor'), may hold values from -3 to 3
- offset_state: float32 [256], replicated, may hold values from -3 to 3
- step_bias: float32 [24], P('tensor'), may hold values from -6 to -1
- decay_log: float32 [24], P('tensor'), may hold values from -3 to 1.5
- skip_gain: float32 [24], P('tensor'), may hold values from 0.5 to 2
- mamba_out: bfloat16 [1536, 1024], P('tensor'), may hold values from -0.15625 to 0.15625
- feedforward_norm_gain: float32 [1024], replicated, may hold values from 0.5 to 1.5
- gate_weight: bfloat16 [1024, 2048], P(None, 'tensor'), may hold values from -0.1875 to 0.1875
- up_weight: bfloat16 [1024, 2048], P(None, 'tensor'), may hold values from -0.1875 to 0.1875
- down_weight: bfloat16 [2048, 1024], P('tensor'), may hold values from -0.125 to 0.125
- cotangent: bfloat16 [4096, 1024], P(('dp', 'tensor')), may hold values from -6 to 6
Outputs:
- output: bfloat16 [4096, 1024], P(('dp', 'tensor'))
- block_input_gradient: float32 [4096, 1024], P(('dp', 'tensor'))
- grad_mixer_gain: float32 [1024], replicated
- grad_query_weight: float32 [1024, 512], P(None, 'tensor')
- grad_key_weight: float32 [1024, 128], replicated
- grad_value_weight: float32 [1024, 128], replicated
- grad_attention_out: float32 [512, 1024], P('tensor')
- grad_mamba_gate: float32 [1024, 1536], P(None, 'tensor')
- grad_mamba_input: float32 [1024, 1536], P(None, 'tensor')
- grad_state_weight: float32 [1024, 256], replicated
- grad_step_weight: float32 [1024, 24], P(None, 'tensor')
- grad_kernel_input: float32 [4, 1536], P(None, 'tensor')
- grad_kernel_state: float32 [4, 256], replicated
- grad_offset_input: float32 [1536], P('tensor')
- grad_offset_state: float32 [256], replicated
- grad_step_bias: float32 [24], P('tensor')
- grad_decay_log: float32 [24], P('tensor')
- grad_skip_gain: float32 [24], P('tensor')
- grad_mamba_out: float32 [1536, 1024], P('tensor')
- grad_feed_gain: float32 [1024], replicated
- grad_gate_weight: float32 [1024, 2048], P(None, 'tensor')
- grad_up_weight: float32 [1024, 2048], P(None, 'tensor')
- grad_down_weight: float32 [2048, 1024], P('tensor')
Inputs may be any that keep to these rules, and one draw needn't show every extreme that they name: `segments`: segment numbers never fall along the tokens; each segment holds 1 to 2000 tokens and one holds exactly 2000.
All inputs are finite; a program needn't handle non-finite values.
Results may differ from a plain program's by a relative error of at most 0.018.
Values may be sent and summed in bfloat16 or wider, within the bound.
No kernel may reach another device: no remote copies, remote signals or barrier semaphores. Data moves between devices by JAX's collectives and lax.ppermute only.
A program may use at most 192 MiB of HBM per device.

v0:
```python
import functools

import jax
import jax.numpy as jnp
from jax import lax
from jax.experimental import pallas as pl
from jax.experimental.pallas import tpu as pltpu
from jax.sharding import PartitionSpec as P


QH = 8
KVH = 2
HD = 64
LANES = 128

eps = 1e-05
big_negative = -1e30
f32 = jnp.float32
bf16 = jnp.bfloat16


def dot(left, right):
    return jnp.dot(left, right, preferred_element_type=f32)


def tdot(left, right):
    return lax.dot_general(left, right, (((0,), (0,)), ((), ())), preferred_element_type=f32)


def dot_t(left, right):
    return lax.dot_general(left, right, (((1,), (1,)), ((), ())), preferred_element_type=f32)


def split3(value):
    high = value.astype(bf16)
    rest = value - high.astype(f32)
    mid = rest.astype(bf16)
    return high, mid, (rest - mid.astype(f32)).astype(bf16)


def exact_left(mask, value):
    high, mid, low = split3(value)
    return dot(mask, high) + (dot(mask, mid) + dot(mask, low))


def rms_recip(values):
    return lax.rsqrt(jnp.mean(values * values, axis=-1, keepdims=True) + eps)


def sigmoid(value):
    return 1.0 / (1.0 + jnp.exp(-value))


def lane_ids(rows, width):
    return lax.broadcasted_iota(jnp.int32, (rows, width), 1)


def pair_columns(values, pair, lanes):
    first = values[:, 2 * pair : 2 * pair + 1]
    second = values[:, 2 * pair + 1 : 2 * pair + 2]
    return jnp.where(lanes < HD, first, second)


def fwd_body(widths, taps_count, heads, tensor, *refs):
    (t_ref,) = refs[:1]
    parts = refs[1 : 1 + tensor]
    (
        seg_ref,
        gain_ref,
        query_w_ref,
        kv_w_ref,
        gate_w_ref,
        input_w_ref,
        state_w_ref,
        step_w_ref,
        taps_ref,
        offs_ref,
        bias_ref,
        nega_ref,
        skip_ref,
        att_w_ref,
        mam_w_ref,
        n1_ref,
        qkv_ref,
        att_ref,
        stat_ref,
        z_ref,
        u_ref,
        acc_ref,
        ysum_ref,
        gated_ref,
        raw_ref,
        mask_ref,
        g_ref,
        run_ref,
        run_t_ref,
        dt_ref,
        link_ref,
        *mixed_refs,
        mixed_ref,
        query_v,
        att_v,
        mam_v,
        sems,
    ) = refs[1 + tensor :]
    wq, _, _, wx, wbc, _ = widths
    copies = Copies(sems)
    for source, target in (
        (query_w_ref, query_v),
        (att_w_ref, att_v),
        (mam_w_ref, mam_v),
    ):
        copies.start(source, target)
    t = t_ref[0]
    rows = parts[0].shape[0]
    length = rows * tensor
    state = wbc // 2
    for k in range(tensor):
        xf = parts[k][...].astype(f32)
        normed = (xf * rms_recip(xf) * gain_ref[...]).astype(bf16)
        n1_ref[pl.ds(pl.multiple_of((t ^ k) * rows, rows), rows), :] = normed
    n1 = n1_ref[...]
    seg_row = seg_ref[0:1, :].astype(f32)
    seg_col = jnp.broadcast_to(seg_row, (LANES, length)).T
    row_pos = lax.broadcasted_iota(jnp.int32, (length, length), 0)
    col_pos = lax.broadcasted_iota(jnp.int32, (length, length), 1)
    allowed = (row_pos >= col_pos) & (seg_col[:, 0:1] == seg_row)
    mask_ref[...] = jnp.where(allowed, 0.0, big_negative)
    copies.wait(0, 1)
    query = dot(n1, query_v[...]).astype(bf16)
    kv = dot(n1, kv_w_ref[...])
    lanes = lane_ids(length, LANES)
    kv_swap = pltpu.roll(kv, HD, 1)
    keys2 = jnp.where(lanes < HD, kv, kv_swap).astype(bf16)
    values2 = jnp.where(lanes < HD, kv_swap, kv).astype(bf16)
    qkv_ref[:, 0:wq] = query
    qkv_ref[:, wq : wq + LANES] = keys2
    qkv_ref[:, wq + LANES :] = values2
    z_ref[...] = dot(n1, gate_w_ref[...])
    u_ref[:, :wx] = dot(n1, input_w_ref[...])
    u_ref[:, wx:] = dot(n1, state_w_ref[...])
    raw = dot_t(n1, step_w_ref[...]) + bias_ref[...]
    raw_ref[...] = raw

    lane_lo = lanes < HD
    scale = HD ** (-0.5)
    half = length // 2
    for block in range(2):
        lo, hi = block * half, (block + 1) * half
        out = jnp.zeros((half, LANES), f32)
        stats = []
        for head in range(2):
            keep = lane_lo[:half] if head == 0 else ~lane_lo[:half]
            keep_v = lane_lo[:hi] if head == 0 else ~lane_lo[:hi]
            q_rows = jnp.where(keep, query[lo:hi].astype(f32), 0.0).astype(bf16)
            scores = dot_t(q_rows, keys2[:hi]) * scale + mask_ref[lo:hi, 0:hi]
            top = jnp.max(scores, axis=-1, keepdims=True)
            expo = jnp.exp(scores - top)
            total = jnp.sum(expo, axis=-1, keepdims=True)
            probs = (expo / total).astype(bf16)
            v_rows = jnp.where(keep_v, values2[:hi].astype(f32), 0.0).astype(bf16)
            out = out + dot(probs, v_rows)
            stats.append(top + jnp.log(total))
        att_ref[lo:hi, :] = out.astype(bf16)
        stat_ref[lo:hi, :] = jnp.where(lane_lo[:half], stats[0], stats[1])

    u = u_ref[...]
    acc = offs_ref[...] + taps_ref[0:1, :] * u
    spots = lax.broadcasted_iota(jnp.int32, (length, LANES), 0)
    for shift_by in range(1, taps_count):
        linked = (pltpu.roll(seg_col, shift_by, 0) == seg_col) & (spots >= shift_by)
        linked = jnp.where(linked, 1.0, 0.0)
        link_ref[shift_by - 1] = linked
        acc = acc + taps_ref[shift_by : shift_by + 1, :] * (
            linked[:, 0:1] * pltpu.roll(u, shift_by, 0)
        )
    acc_ref[...] = acc

    dt = jnp.maximum(raw, 0.0) + jnp.log1p(jnp.exp(-jnp.abs(raw)))
    tri = (row_pos >= col_pos).astype(f32).astype(bf16)
    run = exact_left(tri, dt * nega_ref[...])
    run_t = run.T
    dt_ref[...] = dt
    run_ref[...] = run
    run_t_ref[...] = run_t
    bc = acc_ref[:, wx:]
    bc = (bc * sigmoid(bc)).astype(bf16)
    g_ref[...] = dot_t(bc[:, state:], bc[:, :state])
    for pair in range(heads // 2):
        cols = slice(pair * LANES, (pair + 1) * LANES)
        xa = acc_ref[:, cols]
        xc = xa * sigmoid(xa)
        uu = xc * pair_columns(dt, pair, lanes)
        u_lo = jnp.where(lane_lo, uu, 0.0).astype(bf16)
        u_hi = jnp.where(lane_lo, 0.0, uu).astype(bf16)
        for block in range(2):
            lo, hi = block * half, (block + 1) * half
            total = jnp.zeros((half, LANES), f32)
            for side, masked in ((0, u_lo), (1, u_hi)):
                head = 2 * pair + side
                spread = run[lo:hi, head : head + 1] - run_t[head : head + 1, 0:hi]
                weight = jnp.exp(spread + mask_ref[lo:hi, 0:hi])
                mixing = (weight * g_ref[lo:hi, 0:hi]).astype(bf16)
                total = total + dot(mixing, masked[:hi])
            ysum_ref[lo:hi, cols] = total
        y = ysum_ref[:, cols] + skip_ref[0:1, cols] * xc
        z = z_ref[:, cols]
        gated_ref[:, cols] = (y * z * sigmoid(z)).astype(bf16)
    copies.wait(1)
    mixed = dot(att_ref[...], att_v[...]) + dot(gated_ref[...], mam_v[...])
    mixed_ref[...] = mixed.astype(bf16)
    for k in range(tensor):
        mixed_refs[k][...] = mixed_ref[pl.ds(pl.multiple_of((t ^ k) * rows, rows), rows), :]


def attention_bwd_body(widths, heads, tensor, *refs):
    t_ref = refs[0]
    dparts = refs[1 : 1 + tensor]
    (
        skip_ref,
        att_w_ref,
        mam_w_ref,
        mask_ref,
        qkv_ref,
        att_ref,
        stat_ref,
        z_ref,
        acc_ref,
        ysum_ref,
        gated_ref,
        n1_ref,
        d_ref,
        dssm_ref,
        keep_ref,
        send_ref,
        dmixed_ref,
    ) = refs[1 + tensor :]
    wq, wkv, _, wx, _, _ = widths
    t = t_ref[0]
    rows = dparts[0].shape[0]
    length = rows * tensor
    for k in range(tensor):
        dmixed_ref[pl.ds(pl.multiple_of((t ^ k) * rows, rows), rows), :] = dparts[k][...]
    dmixed = dmixed_ref[...]
    lane_lo = lane_ids(length, LANES) < HD
    half = length // 2
    scale = HD ** (-0.5)

    datt = dot_t(dmixed, att_w_ref[...]).astype(bf16)
    datt_f = datt.astype(f32)
    prod = datt_f * att_ref[...].astype(f32)
    query = qkv_ref[:, 0:wq]
    keys2 = qkv_ref[:, wq : wq + LANES]
    values2 = qkv_ref[:, wq + LANES :]
    stat = stat_ref[...]
    dq = [jnp.zeros((half, LANES), f32) for _ in range(2)]
    dk = [jnp.zeros((half, LANES), f32) for _ in range(2)]
    dv = [jnp.zeros((half, LANES), f32) for _ in range(2)]
    for head in range(2):
        keep = lane_lo if head == 0 else ~lane_lo
        q_m = jnp.where(keep, query.astype(f32), 0.0).astype(bf16)
        k_m = jnp.where(keep, keys2.astype(f32), 0.0).astype(bf16)
        d_m = jnp.where(keep, datt_f, 0.0).astype(bf16)
        delta = jnp.sum(jnp.where(keep, prod, 0.0), axis=-1, keepdims=True)
        logsum = stat[:, head * HD : head * HD + 1]
        for block in range(2):
            lo, hi = block * half, (block + 1) * half
            scores = dot_t(q_m[lo:hi], keys2[:hi]) * scale + mask_ref[lo:hi, 0:hi]
            probs = jnp.exp(scores - logsum[lo:hi])
            dprob = dot_t(d_m[lo:hi], values2[:hi])
            dscore = (probs * (dprob - delta[lo:hi]) * scale).astype(bf16)
            dq[block] = dq[block] + dot(dscore, k_m[:hi])
            dk_add = tdot(dscore, q_m[lo:hi])
            dv_add = tdot(probs.astype(bf16), d_m[lo:hi])
            for part in range(block + 1):
                dk[part] = dk[part] + dk_add[part * half : (part + 1) * half]
                dv[part] = dv[part] + dv_add[part * half : (part + 1) * half]
    for block in range(2):
        lo, hi = block * half, (block + 1) * half
        d_ref[lo:hi, 0:wq] = dq[block].astype(bf16)
        dk_sum = dk[block] + pltpu.roll(dk[block], HD, 1)
        dv_sum = dv[block] + pltpu.roll(dv[block], HD, 1)
        d_ref[lo:hi, wq : wq + wkv] = jnp.where(lane_lo[:half], dk_sum, dv_sum).astype(bf16)

    base = wq + wkv
    for pair in range(heads // 2):
        cols = slice(pair * LANES, (pair + 1) * LANES)
        xa = acc_ref[:, cols]
        xc = xa * sigmoid(xa)
        z = z_ref[:, cols]
        zs = sigmoid(z)
        dgated = dot_t(dmixed, mam_w_ref[cols, :])
        dssm_ref[:, cols] = dgated * z * zs
        y = ysum_ref[:, cols] + skip_ref[0:1, cols] * xc
        dz = dgated * y * zs * (1.0 + z * (1.0 - zs))
        d_ref[:, base + pair * LANES : base + (pair + 1) * LANES] = dz.astype(bf16)
    upper = t_ref[1] % 2
    n1 = n1_ref[...]
    gz = tdot(d_ref[:, base:], n1)
    split_store(upper, tdot(att_ref[...], dmixed), gz[wx - wq :], keep_ref, send_ref, 0)
    second = jnp.concatenate([gz[: wx - wq], tdot(d_ref[:, :wq], n1)], 0)
    split_store(upper, tdot(gated_ref[...], dmixed), second, keep_ref, send_ref, wq)


def state_bwd_body(widths, taps_count, heads, tensor, *refs):
    (
        t_ref,
        gain_ref,
        query_w_ref,
        kv_w_ref,
        gate_w_ref,
        input_w_ref,
        state_w_ref,
        step_w_ref,
        taps_ref,
        nega_ref,
        skip_ref,
        mask_ref,
        g_ref,
        run_ref,
        run_t_ref,
        dt_ref,
        link_ref,
        n1_ref,
        u_ref,
        acc_ref,
        ysum_ref,
        raw_ref,
        d1_ref,
        dssm_ref,
        gfeed_ref,
    ) = refs[:25]
    (
        keep_ref,
        send_ref,
        *dn1_refs,
        d2_ref,
        small_ref,
        dn1_ref,
        dg_ref,
        dact_ref,
        rows_ref,
    ) = refs[25:]
    wq, wkv, _, wx, wbc, _ = widths
    t = t_ref[0]
    length = n1_ref.shape[0]
    rows = length // tensor
    state = wbc // 2
    lanes = lane_ids(length, LANES)
    lane_lo = lanes < HD
    half = length // 2

    raw = raw_ref[...]
    dt = dt_ref[...]
    ld = dt * nega_ref[...]
    run = run_ref[...]
    run_t = run_t_ref[...]
    bc_acc = acc_ref[:, wx:]
    bc = (bc_acc * sigmoid(bc_acc)).astype(bf16)
    dg_ref[...] = jnp.zeros((length, length), f32)
    drun = jnp.zeros((length, LANES), f32)
    ddt = jnp.zeros((length, LANES), f32)
    skip_row = jnp.zeros((1, LANES), f32)
    small_ref[...] = jnp.zeros(small_ref.shape, f32)
    for pair in range(heads // 2):
        cols = slice(pair * LANES, (pair + 1) * LANES)
        xa = acc_ref[:, cols]
        xc = xa * sigmoid(xa)
        skip = skip_ref[0:1, cols]
        ysum = ysum_ref[:, cols]
        dssm = dssm_ref[:, cols]
        dskip = jnp.sum(dssm * xc, axis=0, keepdims=True)
        for side in range(2):
            keep = lane_lo[0:1] if side == 0 else ~lane_lo[0:1]
            head_sum = jnp.sum(jnp.where(keep, dskip, 0.0), axis=-1, keepdims=True)
            skip_row = jnp.where(lanes[0:1] == 2 * pair + side, head_sum, skip_row)
        dt_pair = pair_columns(dt, pair, lanes)
        u_b = (xc * dt_pair).astype(bf16)
        dy_b = dssm.astype(bf16)
        u_f = u_b.astype(f32)
        dy_f = dy_b.astype(f32)
        du = [jnp.zeros((half, LANES), f32) for _ in range(2)]
        for side in range(2):
            head = 2 * pair + side
            keep = lane_lo if side == 0 else ~lane_lo
            dy_m = jnp.where(keep, dy_f, 0.0).astype(bf16)
            for block in range(2):
                lo, hi = block * half, (block + 1) * half
                spread = run[lo:hi, head : head + 1] - run_t[head : head + 1, 0:hi]
                weight = jnp.exp(spread + mask_ref[lo:hi, 0:hi])
                mixing = (weight * g_ref[lo:hi, 0:hi]).astype(bf16)
                dmix = dot_t(dy_m[lo:hi], u_b[:hi])
                dg_ref[lo:hi, 0:hi] += weight * dmix
                du_add = tdot(mixing, dy_m[lo:hi])
                for part in range(block + 1):
                    du[part] = du[part] + du_add[part * half : (part + 1) * half]
        du = jnp.concatenate(du, 0)
        balance = dy_f * ysum - u_f * du
        weighted = du * xc
        for side in range(2):
            head = 2 * pair + side
            keep = lane_lo if side == 0 else ~lane_lo
            here = lanes == head
            drun = jnp.where(
                here, jnp.sum(jnp.where(keep, balance, 0.0), axis=-1, keepdims=True), drun
            )
            ddt = jnp.where(
                here, jnp.sum(jnp.where(keep, weighted, 0.0), axis=-1, keepdims=True), ddt
            )
        dact_ref[:, cols] = du * dt_pair + skip * dssm
    dg = dg_ref[...].astype(bf16)
    dact_ref[:, wx : wx + state] = tdot(dg, bc[:, state:])
    dact_ref[:, wx + state :] = dot(dg, bc[:, :state])
    linked = jnp.where(mask_ref[...] == 0.0, 1.0, 0.0).astype(bf16)
    high, mid, low = split3(drun)
    dld = tdot(linked, high) + (tdot(linked, mid) + tdot(linked, low))
    ddt = ddt + dld * nega_ref[...]
    dstep = ddt * sigmoid(raw)
    d2_ref[:, wx + wbc :] = dstep.astype(bf16)

    acc = acc_ref[...]
    sig = sigmoid(acc)
    dconv = dact_ref[...] * sig * (1.0 + acc * (1.0 - sig))
    u = u_ref[...]
    small_ref[0:1, :] = jnp.sum(dconv * u, axis=0, keepdims=True)
    small_ref[taps_count : taps_count + 1, :] = jnp.sum(dconv, axis=0, keepdims=True)
    du_in = dconv * taps_ref[0:1, :]
    for shift_by in range(1, taps_count):
        masked = dconv * link_ref[shift_by - 1, :, 0:1]
        small_ref[shift_by : shift_by + 1, :] = jnp.sum(
            masked * pltpu.roll(u, shift_by, 0), axis=0, keepdims=True
        )
        du_in = du_in + taps_ref[shift_by : shift_by + 1, :] * pltpu.roll(
            masked, length - shift_by, 0
        )
    d2_ref[:, 0 : wx + wbc] = du_in.astype(bf16)
    small_ref[taps_count + 1 : taps_count + 2, 0:LANES] = skip_row
    small_ref[taps_count + 2 : taps_count + 3, 0:LANES] = jnp.sum(dstep, axis=0, keepdims=True)
    small_ref[taps_count + 3 : taps_count + 4, 0:LANES] = jnp.sum(dld * ld, axis=0, keepdims=True)
    dn1 = dot_t(d1_ref[:, :wq], query_w_ref[...]) + dot_t(d1_ref[:, wq : wq + wkv], kv_w_ref[...])
    dn1 = dn1 + dot_t(d1_ref[:, wq + wkv :], gate_w_ref[...])
    dn1 = dn1 + dot_t(d2_ref[:, :wx], input_w_ref[...])
    dn1 = dn1 + dot_t(d2_ref[:, wx : wx + wbc], state_w_ref[...])
    dn1 = dn1 + dot(d2_ref[:, wx + wbc :], step_w_ref[...])
    dn1_ref[...] = dn1.astype(bf16)
    for k in range(tensor):
        dn1_refs[k][...] = dn1_ref[pl.ds(pl.multiple_of((t ^ k) * rows, rows), rows), :]
    gmix = jnp.sum(dn1 * n1_ref[...].astype(f32), axis=0, keepdims=True) / gain_ref[...]
    late_grads(
        widths, heads, t_ref[1] % 2, n1_ref, d1_ref, d2_ref, small_ref, gmix, gfeed_ref[...],
        keep_ref, send_ref, rows_ref,
    )


def feed_body(tensor, *refs):
    parts = refs[:tensor]
    dhidden_ref, gate_ref, up_ref, n2_ref, hidden_ref, dgu_ref = refs[tensor : tensor + 6]
    dn2_refs = refs[tensor + 6 :]
    rows = parts[0].shape[0]
    units = gate_ref.shape[1]
    for k in range(tensor):
        n2_ref[k * rows : (k + 1) * rows, :] = parts[k][...]
    n2 = n2_ref[...]
    gate_pre = dot(n2, gate_ref[...])
    up_pre = dot(n2, up_ref[...])
    gsig = sigmoid(gate_pre)
    gate_act = gate_pre * gsig
    dhidden = dhidden_ref[...]
    dgate = (dhidden * up_pre * gsig * (1.0 + gate_pre * (1.0 - gsig))).astype(bf16)
    dup = (dhidden * gate_act).astype(bf16)
    dn2 = (dot_t(dgate, gate_ref[...]) + dot_t(dup, up_ref[...])).astype(bf16)
    for k in range(tensor):
        dn2_refs[k][...] = dn2[k * rows : (k + 1) * rows]
    hidden_ref[...] = (gate_act * up_pre).astype(bf16)
    dgu_ref[:, :units] = dgate
    dgu_ref[:, units:] = dup


def split_store(upper, first, second, keep_ref, send_ref, at):
    size = first.shape[0]
    low = upper == 0
    keep_ref[at : at + size, :] = jnp.where(low, first, second).astype(bf16)
    send_ref[at : at + size, :] = jnp.where(low, second, first).astype(bf16)


def feed_grads_body(groups, u_ref, n2_ref, dgu_ref, hidden_ref, cot_ref, keep_ref, send_ref):
    upper = u_ref[1] % 2
    dgu = dgu_ref[...]
    cot = cot_ref[...]
    half_wide = n2_ref.shape[1] // 2
    half_tall = hidden_ref.shape[1] // 2
    wide, tall = half_wide // groups, half_tall // groups
    low = upper == 0
    for source, other, half, size, skip in (
        (n2_ref, dgu, half_wide, wide, 0),
        (hidden_ref, cot, half_tall, tall, wide),
    ):
        first = tdot(source[:, :half], other)
        second = tdot(source[:, half:], other)
        keep = jnp.where(low, first, second).astype(bf16)
        send = jnp.where(low, second, first).astype(bf16)
        for q in range(groups):
            at = q * (wide + tall) + skip
            keep_ref[at : at + size, :] = keep[q * size : (q + 1) * size]
            send_ref[at : at + size, :] = send[q * size : (q + 1) * size]


def late_grads(
    widths, heads, upper, n1_ref, d1_ref, d2_ref, small_ref, gmix, gfeed,
    keep_ref, send_ref, rows_ref,
):
    wq, wkv, _, wx, wbc, wst = widths
    count = small_ref.shape[0]
    width = n1_ref.shape[1]
    half = width // 2
    rows_ref[...] = jnp.zeros(rows_ref.shape, f32)
    at = heads
    rows_ref[at : at + count, 0:wx] = small_ref[:, :wx]
    at += count
    rows_ref[at : at + 1, :] = gmix
    rows_ref[at + 1 : at + 2, :] = gfeed
    at += 2
    rows_ref[at : at + count, 0:wbc] = small_ref[:, wx:]
    extra = rows_ref[...].T
    low = upper == 0
    for source, columns, where_to in (
        (d1_ref, (wq, wq + wkv), 0),
        (d2_ref, (wx, wx + wbc), wkv),
        (d2_ref, (wx + wbc, wx + wbc + wst), wkv + wbc),
        (d2_ref, (0, wx), wkv + wbc + wst),
    ):
        grads = tdot(n1_ref[...], source[:, columns[0] : columns[1]])
        if columns[0] == wx + wbc:
            grads = grads + extra
        first, second = grads[:half], grads[half:]
        span = slice(where_to, where_to + columns[1] - columns[0])
        keep_ref[:, span] = jnp.where(low, first, second).astype(bf16)
        send_ref[:, span] = jnp.where(low, second, first).astype(bf16)


def combine_body(widths, heads, counts, local_heads, t_ref, own_ref, sum_ref, other_ref, out_ref):
    _, wkv, _, _, wbc, wst = widths
    t = t_ref[0]
    group = QH // KVH
    picked = wkv + wbc + wst
    lanes = lane_ids(own_ref.shape[0], LANES)
    first = t * local_heads // group == 0
    own = own_ref[:, :picked].astype(f32)
    mine = sum_ref[...].astype(f32)
    other = other_ref[...].astype(f32)
    low = jnp.where(first, mine[:, :wkv], other[:, :wkv])
    high = jnp.where(first, other[:, :wkv], mine[:, :wkv])
    out_ref[:, :LANES] = jnp.where(lanes < HD, low, pltpu.roll(high, HD, 1)).astype(bf16)
    out_ref[:, LANES : 2 * LANES] = jnp.where(lanes < HD, pltpu.roll(low, HD, 1), high).astype(
        bf16
    )
    total = mine[:, wkv:] + other[:, wkv:]
    at = 2 * LANES
    out_ref[:, at : at + wbc] = total[:, :wbc].astype(bf16)
    at += wbc
    extra = jnp.where(lanes < heads + counts, own[:, wkv + wbc :], total[:, wbc:])
    out_ref[:, at : at + wst] = extra.astype(bf16)
    at += wst
    out_ref[:, at:] = own_ref[:, picked:]


def piece_places(d, groups):
    for side in range(2):
        half = d % 2 if side == 0 else 1 - d % 2
        for j in range(groups):
            yield side * groups + j, half, (d // 2) ^ j


def merge_rows(d, groups, pieces, full_ref):
    rows = pieces[0].shape[0]
    for at, half, group in piece_places(d, groups):
        where_to = pl.multiple_of((half * groups + group) * rows, rows)
        full_ref[pl.ds(where_to, rows), :] = pieces[at][...]


def feed_out_body(groups, d_ref, *refs):
    pieces = refs[: 2 * groups]
    gate_ref, up_ref, down_ref, gate_stage, up_stage, down_stage, sems = refs[2 * groups :]
    width, units = gate_ref.shape
    wide, tall = width // (2 * groups), units // (2 * groups)
    copies = Copies(sems)
    for at, half, group in piece_places(d_ref[1], groups):
        piece = pieces[at]
        place = half * groups + group
        rows = pl.ds(pl.multiple_of(place * wide, wide), wide)
        gate_stage[rows, :] = piece[:wide, :units].astype(f32)
        copies.start(gate_stage.at[rows, :], gate_ref.at[rows, :])
        up_stage[rows, :] = piece[:wide, units:].astype(f32)
        copies.start(up_stage.at[rows, :], up_ref.at[rows, :])
        rows = pl.ds(pl.multiple_of(place * tall, tall), tall)
        down_stage[rows, :] = piece[wide:, :].astype(f32)
        copies.start(down_stage.at[rows, :], down_ref.at[rows, :])
    copies.wait()


def mid_out_body(widths, groups, d_ref, *refs):
    wq, _, _, wx, _, _ = widths
    outs = refs[2 * groups : 2 * groups + 4]
    stages = refs[2 * groups + 4 : 2 * groups + 8]
    full_ref, sems = refs[2 * groups + 8 :]
    att_stage, mam_stage, gate_stage, query_stage = stages
    merge_rows(d_ref[1], groups, refs[: 2 * groups], full_ref)
    copies = Copies(sems)
    mam_stage[...] = full_ref[wq : wq + wx, :].astype(f32)
    copies.start(mam_stage, outs[1])
    att_stage[...] = full_ref[:wq, :].astype(f32)
    copies.start(att_stage, outs[0])
    at = wq + wx
    gate_stage[:, wx - wq :] = full_ref[at : at + wq, :].astype(f32).T
    gate_stage[:, : wx - wq] = full_ref[at + wq : at + wx, :].astype(f32).T
    copies.start(gate_stage, outs[2])
    query_stage[...] = full_ref[at + wx :, :].astype(f32).T
    copies.start(query_stage, outs[3])
    copies.wait()


def late_out_body(widths, heads, taps_count, groups, d_ref, *refs):
    _, _, _, wx, wbc, wst = widths
    big = refs[2 * groups : 2 * groups + 4]
    (
        step_ref, tap_in_ref, off_in_ref, skip_ref, bias_ref, decay_ref,
        mix_ref, feed_ref, tap_st_ref, off_st_ref,
    ) = refs[2 * groups + 4 : 2 * groups + 14]
    *stages, full_ref, rows_ref, sems = refs[2 * groups + 14 :]
    merge_rows(d_ref[1], groups, refs[: 2 * groups], full_ref)
    copies = Copies(sems)
    sizes = (KVH * HD, KVH * HD, wbc, wx)
    starts = (0, KVH * HD, 2 * KVH * HD, 2 * KVH * HD + wbc + wst)
    for out_ref, stage, size, at in zip(big, stages, sizes, starts):
        stage[...] = full_ref[:, at : at + size].astype(f32)
        copies.start(stage, out_ref)
    at = 2 * KVH * HD + wbc
    rows_ref[...] = full_ref[:, at : at + wst].astype(f32).T
    step_ref[...] = rows_ref[:heads, :]
    at = heads
    tap_in_ref[...] = rows_ref[at : at + taps_count, :wx]
    at += taps_count
    off_in_ref[...] = rows_ref[at : at + 1, :wx]
    skip_ref[...] = rows_ref[at + 1 : at + 2, :heads]
    bias_ref[...] = rows_ref[at + 2 : at + 3, :heads]
    decay_ref[...] = rows_ref[at + 3 : at + 4, :heads]
    at += taps_count
    mix_ref[...] = rows_ref[at : at + 1, :]
    feed_ref[...] = rows_ref[at + 1 : at + 2, :]
    at += 2
    tap_st_ref[...] = rows_ref[at : at + taps_count, :wbc]
    off_st_ref[...] = rows_ref[at + taps_count : at + taps_count + 1, :wbc]
    copies.wait()


def add_split_body(groups, d_ref, keep_ref, came_ref, *outs):
    group = d_ref[1] // 2
    rows = keep_ref.shape[0] // groups
    for j in range(groups):
        at = pl.ds(pl.multiple_of((group ^ j) * rows, rows), rows)
        outs[j][...] = (keep_ref[at, :].astype(f32) + came_ref[at, :].astype(f32)).astype(bf16)


def add_body(groups, picked, d_ref, *refs):
    total = refs[0][...].astype(f32)
    for j in range(1, groups):
        total = total + refs[j][...].astype(f32)
    total = total.astype(bf16)
    refs[groups][...] = total
    if picked:
        refs[groups + 1][...] = total[:, :picked]


def call_kernel(body, scalar, operands, out_shapes, scratch=(), leaves=False, far=(), far_outs=0):
    spec = pl.BlockSpec(memory_space=pltpu.VMEM)
    hbm = pl.BlockSpec(memory_space=pltpu.HBM)
    shape_of = jax.ShapeDtypeStruct if leaves else pltpu.VMEM
    placed = [
        pltpu.with_memory_space_constraint(value, pltpu.HBM if at in far else pltpu.VMEM)
        for at, value in enumerate(operands)
    ]
    return pl.pallas_call(
        body,
        in_specs=[pl.BlockSpec(memory_space=pltpu.SMEM)]
        + [hbm if at in far else spec for at in range(len(operands))],
        out_specs=[hbm if at < far_outs else spec for at in range(len(out_shapes))],
        out_shape=[shape_of(shape, kind) for shape, kind in out_shapes],
        scratch_shapes=[
            shape if kind is None else pltpu.VMEM(shape, kind) for shape, kind in scratch
        ],
        compiler_params=pltpu.CompilerParams(vmem_limit_bytes=24 * 1024 * 1024),
    )(scalar, *placed)


class Copies:
    def __init__(self, sems):
        self.sems = sems
        self.started = []

    def start(self, source, target):
        copy = pltpu.make_async_copy(source, target, self.sems.at[len(self.started)])
        copy.start()
        self.started.append(copy)

    def wait(self, first=0, last=None):
        for copy in self.started[first:last]:
            copy.wait()


def xor_pairs(size, bit):
    return [(at, at ^ bit) for at in range(size)]


def swap(value, axis, size, bit):
    return lax.ppermute(value, axis, xor_pairs(size, bit))


def lowest_bit(number):
    return number & -number


def gather_parts(value, size):
    got = {0: value}
    for k in range(size - 1, 0, -1):
        if lowest_bit(k) == k:
            got[k] = swap(value, "tensor", size, k)
    for k in range(1, size):
        low = lowest_bit(k)
        if k != low:
            got[k] = swap(got[k ^ low], "tensor", size, low)
    return [got[k] for k in range(size)]


def scatter_parts(blocks, size):
    held = list(blocks)
    for k in range(size - 1, 0, -1):
        low = lowest_bit(k)
        if k != low:
            came = swap(held[k], "tensor", size, low)
            held[k ^ low] = (held[k ^ low].astype(f32) + came.astype(f32)).astype(bf16)
    total = held[0].astype(f32)
    for k in range(size - 1, 0, -1):
        if lowest_bit(k) == k:
            total = total + swap(held[k], "tensor", size, k).astype(f32)
    return total


def sum_over_dp(keep, send, size, index, between=None, picked=0):
    groups = size // 2
    rows, width = keep.shape[0] // groups, keep.shape[1]
    came = swap(send, "dp", size, 1)
    pieces = call_kernel(
        functools.partial(add_split_body, groups),
        index,
        (keep, came),
        [((rows, width), bf16)] * groups,
    )
    came = [swap(pieces[j], "dp", size, 2 * j) for j in range(1, groups)]
    outs = [((rows, width), bf16)]
    if picked:
        outs = outs + [((rows, picked), bf16)]
    total, *rest = call_kernel(
        functools.partial(add_body, groups, picked), index, (pieces[0], *came), outs
    )
    if between is not None:
        total = between(total, *rest)
    mine = [total]
    mine = mine + [swap(total, "dp", size, 2 * j) for j in range(1, groups)]
    return mine + [swap(piece, "dp", size, 1) for piece in mine]


def block(
    inputs,
    segments,
    mixers_norm_gain,
    query_weight,
    key_weight,
    value_weight,
    attention_out,
    mamba_gate,
    mamba_input,
    state_weight,
    step_weight,
    kernel_input,
    kernel_state,
    offset_input,
    offset_state,
    step_bias,
    decay_log,
    skip_gain,
    mamba_out,
    feedforward_norm_gain,
    gate_weight,
    up_weight,
    down_weight,
    cotangent,
    *,
    dp,
    tensor,
):
    local_heads = query_weight.shape[1] // HD
    group = QH // KVH
    assert tensor == 4 and KVH * HD == LANES and 2 * local_heads == group
    rows, width = inputs.shape
    length = rows * tensor
    heads = step_weight.shape[1]
    wq = query_weight.shape[1]
    wkv = 2 * HD
    wx = mamba_input.shape[1]
    wbc = state_weight.shape[1]
    wst = LANES
    units = gate_weight.shape[1]
    kc = kernel_input.shape[0]
    widths = (wq, wkv, wx, wx, wbc, wst)
    t_index = lax.axis_index("tensor")
    t_array = jnp.where(
        lax.iota(jnp.int32, 2) == 0, t_index, lax.axis_index("dp")
    ).astype(jnp.int32)

    parts = gather_parts(inputs, tensor)
    cot_parts = gather_parts(cotangent, tensor)

    kv_index = t_index * local_heads // group
    key_slice = lax.dynamic_slice_in_dim(key_weight, kv_index * HD, HD, 1)
    value_slice = lax.dynamic_slice_in_dim(value_weight, kv_index * HD, HD, 1)
    step_pad = jnp.pad(step_weight.T, ((0, LANES - heads), (0, 0)))
    kv_weight = jnp.concatenate([key_slice, value_slice], 1)
    weights = (query_weight, kv_weight, mamba_gate, mamba_input, state_weight, step_pad)
    taps = jnp.concatenate([kernel_input, kernel_state], 1)
    offs = jnp.concatenate([offset_input, offset_state], 0)[None, :]
    bias = jnp.pad(step_bias, (0, LANES - heads))[None, :]
    nega = jnp.pad(-jnp.exp(decay_log), (0, LANES - heads))[None, :]
    skip = jnp.repeat(skip_gain, wx // heads)[None, :]
    seg_row = segments[None, :]
    gain1 = mixers_norm_gain[None, :]

    full = (length, width)
    blocks = [((rows, width), bf16)] * tensor
    square = ((length, length), f32)
    (n1, qkv, att, stat, z, u, acc, ysum, gated, raw, *held) = call_kernel(
        functools.partial(fwd_body, widths, kc, heads, tensor),
        t_array,
        (*parts, seg_row, gain1, *weights, taps, offs, bias, nega, skip, attention_out, mamba_out),
        [
            (full, bf16),
            ((length, wq + 2 * LANES), bf16),
            ((length, LANES), bf16),
            ((length, LANES), f32),
            ((length, wx), f32),
            ((length, wx + wbc), f32),
            ((length, wx + wbc), f32),
            ((length, wx), f32),
            ((length, wx), bf16),
            ((length, wst), f32),
            square,
            square,
            ((length, wst), f32),
            ((wst, length), f32),
            ((length, wst), f32),
            ((kc - 1, length, LANES), f32),
            *blocks,
        ],
        [
            (full, bf16),
            (query_weight.shape, bf16),
            (attention_out.shape, bf16),
            (mamba_out.shape, bf16),
            (pltpu.SemaphoreType.DMA((3,)), None),
        ],
        far=(tensor + 2, tensor + 13, tensor + 14),
    )
    mask, g, run, run_t, dt, link, *mixed_blocks = held

    inputs_float = inputs.astype(f32)
    reciprocal_first = rms_recip(inputs_float)
    unit_first = inputs_float * reciprocal_first
    hidden_first = inputs_float + scatter_parts(mixed_blocks, tensor)
    reciprocal_second = rms_recip(hidden_first)
    unit_second = hidden_first * reciprocal_second
    local_normed_second = (unit_second * feedforward_norm_gain[None, :]).astype(bf16)
    n2_parts = gather_parts(local_normed_second, tensor)

    cot_rows = jnp.concatenate(cot_parts, 0)
    dhidden = dot_t(cot_rows, down_weight)
    n2, hidden, dgu, *dn2_blocks = call_kernel(
        lambda scalar, *refs: feed_body(tensor, *refs),
        t_array,
        (*n2_parts, dhidden, gate_weight, up_weight),
        [(full, bf16), ((length, units), bf16), ((length, 2 * units), bf16), *blocks],
    )
    dn2 = scatter_parts(dn2_blocks, tensor)
    scaled_second = dn2 * feedforward_norm_gain[None, :]
    grad_hidden = cotangent.astype(f32) + reciprocal_second * (
        scaled_second - unit_second * jnp.mean(scaled_second * unit_second, axis=-1, keepdims=True)
    )
    feed_grad = jnp.sum(dn2 * unit_second, axis=0)
    dparts = gather_parts(grad_hidden.astype(bf16), tensor)

    span = width // 2 + units // 2
    feed_keep, feed_send = call_kernel(
        functools.partial(feed_grads_body, dp // 2),
        t_array,
        (n2, dgu, hidden, cot_rows),
        [((span, width), bf16)] * 2,
    )
    feed_sum = sum_over_dp(feed_keep, feed_send, dp, t_array)

    mid_rows = wq + wx
    d1, dssm, mid_keep, mid_send = call_kernel(
        functools.partial(attention_bwd_body, widths, heads, tensor),
        t_array,
        (
            *dparts, skip, attention_out, mamba_out, mask,
            qkv, att, stat, z, acc, ysum, gated, n1,
        ),
        [
            ((length, wq + wkv + wx), bf16),
            ((length, wx), f32),
            ((mid_rows, width), bf16),
            ((mid_rows, width), bf16),
        ],
        [(full, bf16)],
    )
    mid_sum = sum_over_dp(mid_keep, mid_send, dp, t_array)

    feed_part = dot(hidden, down_weight).astype(bf16)
    feed_blocks = [feed_part[k * rows : (k + 1) * rows] for k in range(tensor)]
    feed_total = scatter_parts(feed_blocks, tensor)
    hidden_held, feed_total = lax.optimization_barrier((hidden_first, feed_total))
    output = (hidden_held + feed_total).astype(bf16)

    wl = wkv + wbc + wst + wx
    late_keep, late_send, *dn1_blocks = call_kernel(
        functools.partial(state_bwd_body, widths, kc, heads, tensor),
        t_array,
        (
            gain1, *weights, taps, nega, skip, mask, g, run, run_t, dt, link,
            n1, u, acc, ysum, raw, d1, dssm, feed_grad[None, :],
        ),
        [((width // 2, wl), bf16), ((width // 2, wl), bf16), *blocks],
        [
            ((length, wx + wbc + wst), bf16),
            ((2 * kc, wx + wbc), f32),
            (full, bf16),
            square,
            ((length, wx + wbc), f32),
            ((LANES, width), f32),
        ],
    )
    dn1 = scatter_parts(dn1_blocks, tensor)
    scaled_first = dn1 * mixers_norm_gain[None, :]
    block_input_gradient = grad_hidden + reciprocal_first * (
        scaled_first - unit_first * jnp.mean(scaled_first * unit_first, axis=-1, keepdims=True)
    )

    picked = wkv + wbc + wst
    wide = 2 * KVH * HD + wbc + wst + wx

    def combine(own, shared):
        pair = shared + swap(shared, "tensor", tensor, 1)
        (out,) = call_kernel(
            functools.partial(combine_body, widths, heads, 2 * kc, local_heads),
            t_array,
            (own, pair, swap(pair, "tensor", tensor, 2)),
            [((own.shape[0], wide), bf16)],
        )
        return out

    late_sum = sum_over_dp(late_keep, late_send, dp, t_array, combine, picked)

    groups = dp // 2
    feed_shapes = [((width, units), f32), ((width, units), f32), ((units, width), f32)]
    grad_gate, grad_up, grad_down = call_kernel(
        functools.partial(feed_out_body, groups),
        t_array,
        feed_sum,
        feed_shapes,
        [*feed_shapes, (pltpu.SemaphoreType.DMA((6 * groups,)), None)],
        leaves=True,
        far_outs=3,
    )
    mid_shapes = [((wq, width), f32), ((wx, width), f32), ((width, wx), f32), ((width, wq), f32)]
    grad_attn_out, grad_mamba_out, grad_mgate, grad_query = call_kernel(
        functools.partial(mid_out_body, widths, groups),
        t_array,
        mid_sum,
        mid_shapes,
        [*mid_shapes, ((2 * (wq + wx), width), bf16), (pltpu.SemaphoreType.DMA((4,)), None)],
        leaves=True,
        far_outs=4,
    )
    late_shapes = [
        ((width, KVH * HD), f32),
        ((width, KVH * HD), f32),
        ((width, wbc), f32),
        ((width, wx), f32),
    ]
    (
        grad_key,
        grad_value,
        grad_state,
        grad_minput,
        grad_step,
        grad_kinput,
        grad_oinput,
        grad_skip,
        grad_sbias,
        grad_dlog,
        mixers_grad,
        feedforward_grad,
        grad_kstate,
        grad_ostate,
    ) = call_kernel(
        functools.partial(late_out_body, widths, heads, kc, groups),
        t_array,
        late_sum,
        [
            *late_shapes,
            ((heads, width), f32),
            ((kc, wx), f32),
            ((1, wx), f32),
            ((1, heads), f32),
            ((1, heads), f32),
            ((1, heads), f32),
            ((1, width), f32),
            ((1, width), f32),
            ((kc, wbc), f32),
            ((1, wbc), f32),
        ],
        [
            *late_shapes,
            ((width, wide), bf16),
            ((LANES, width), f32),
            (pltpu.SemaphoreType.DMA((4,)), None),
        ],
        leaves=True,
        far_outs=4,
    )
    grad_step = grad_step.T
    grad_oinput, grad_skip, grad_sbias, grad_dlog, mixers_grad, feedforward_grad, grad_ostate = (
        value[0]
        for value in (
            grad_oinput, grad_skip, grad_sbias, grad_dlog, mixers_grad, feedforward_grad, grad_ostate
        )
    )
    return (
        output,
        block_input_gradient,
        mixers_grad,
        grad_query,
        grad_key,
        grad_value,
        grad_attn_out,
        grad_mgate,
        grad_minput,
        grad_state,
        grad_step,
        grad_kinput,
        grad_kstate,
        grad_oinput,
        grad_ostate,
        grad_sbias,
        grad_dlog,
        grad_skip,
        grad_mamba_out,
        feedforward_grad,
        grad_gate,
        grad_up,
        grad_down,
    )


def solution(mesh):
    in_specs = (
        P(("dp", "tensor"), None),
        P("dp"),
        P(),
        P(None, "tensor"),
        P(),
        P(),
        P("tensor", None),
        P(None, "tensor"),
        P(None, "tensor"),
        P(),
        P(None, "tensor"),
        P(None, "tensor"),
        P(),
        P("tensor"),
        P(),
        P("tensor"),
        P("tensor"),
        P("tensor"),
        P("tensor", None),
        P(),
        P(None, "tensor"),
        P(None, "tensor"),
        P("tensor", None),
        P(("dp", "tensor"), None),
    )
    out_specs = (
        P(("dp", "tensor"), None),
        P(("dp", "tensor"), None),
        P(),
        P(None, "tensor"),
        P(),
        P(),
        P("tensor", None),
        P(None, "tensor"),
        P(None, "tensor"),
        P(),
        P(None, "tensor"),
        P(None, "tensor"),
        P(),
        P("tensor"),
        P(),
        P("tensor"),
        P("tensor"),
        P("tensor"),
        P("tensor", None),
        P(),
        P(None, "tensor"),
        P(None, "tensor"),
        P("tensor", None),
    )
    body = functools.partial(block, dp=mesh.shape["dp"], tensor=mesh.shape["tensor"])
    return jax.shard_map(body, mesh=mesh, in_specs=in_specs, out_specs=out_specs, check_vma=False)
```

profile of v0, /device:TPU:0, one launch (start us, length us, event | category | flops | bytes accessed | tf_op | source)
XLA Modules:
  0.0 263.8 jit_solution(558552568381657396)
XLA Ops:
  0.7 3.1 %collective-permute-start = (bf16[128,1024]{1,0:T(8,128)(2,1)}, bf16[128,1024]{1,0:T(8,128)(2,1)S(1)}, u32[]{:S(2)}, u32[]{:S(2)}) collective-permute-start(bf16[128,1024]{1,0:T(8,128)(2,1)} %refs_1_.1), channel_id=1, source_target_pairs={{0,1},{1,0},{2,3},{3,2},{4,5},{5,4},{6,7},{7,6},{8,9},{9,8},{10,11... | collective-permute-start | bytes 786440 | tf_op jit(solution)/shard_map/ppermute | solution.py:715
  9.8 8.6 %collective-permute-done.1.refs_3_ = bf16[128,1024]{1,0:T(8,128)(2,1)S(1)} collective-permute-done((bf16[128,1024]{1,0:T(8,128)(2,1)}, bf16[128,1024]{1,0:T(8,128)(2,1)S(1)}, u32[]{:S(2)}, u32[]{:S(2)}) %collective-permute-start.1) | collective-permute-done | bytes 262176 | tf_op jit(solution)/shard_map/ppermute | solution.py:715
  21.8 3.1 %collective-permute-done.2.refs_4_ = bf16[128,1024]{1,0:T(8,128)(2,1)} collective-permute-done((bf16[128,1024]{1,0:T(8,128)(2,1)S(1)}, bf16[128,1024]{1,0:T(8,128)(2,1)}, u32[]{:S(2)}, u32[]{:S(2)}) %collective-permute-start.2) | collective-permute-done | bytes 262176 | tf_op jit(solution)/shard_map/ppermute | solution.py:715
  26.0 10.2 %shard_map.407 = (bf16[512,1024]{1,0:T(8,128)(2,1)S(1)}, bf16[512,384]{1,0:T(8,128)(2,1)S(1)}, bf16[512,128]{1,0:T(8,128)(2,1)S(1)}, f32[512,128]{1,0:T(8,128)S(...) custom-call(s32[2]{0:T(128)S(1)} %compare_select_fusion.refs_0_.scal, ...), custom_call_target="tpu_custom_call" | custom-call | tf_op jit(solution)/shard_map/pallas_call | solution.py:682
  39.5 11.6 %collective-permute-done.3 = bf16[128,1024]{1,0:T(8,128)(2,1)S(1)} collective-permute-done((bf16[128,1024]{1,0:T(8,128)(2,1)S(1)}, bf16[128,1024]{1,0:T(8,128)(2,1)S(1)}, u32[]{:S(2)}, u32[]{:S(2)}) %collective-permute-start.3) | collective-permute-done | bytes 262176 | tf_op jit(solution)/shard_map/ppermute | solution.py:715
  53.6 11.0 %collective-permute-done.5 = bf16[128,1024]{1,0:T(8,128)(2,1)S(1)} collective-permute-done((bf16[128,1024]{1,0:T(8,128)(2,1)S(1)}, bf16[128,1024]{1,0:T(8,128)(2,1)S(1)}, u32[]{:S(2)}, u32[]{:S(2)}) %collective-permute-start.5) | collective-permute-done | bytes 262176 | tf_op jit(solution)/shard_map/ppermute | solution.py:715
  65.0 5.6 %collective-permute-done.9 = bf16[128,1024]{1,0:T(8,128)(2,1)S(1)} collective-permute-done((bf16[128,1024]{1,0:T(8,128)(2,1)S(1)}, bf16[128,1024]{1,0:T(8,128)(2,1)S(1)}, u32[]{:S(2)}, u32[]{:S(2)}) %collective-permute-start.9) | collective-permute-done | bytes 262176 | tf_op jit(solution)/shard_map/ppermute | solution.py:715
  70.7 6.9 %collective-permute-done.11 = bf16[128,1024]{1,0:T(8,128)(2,1)S(1)} collective-permute-done((bf16[128,1024]{1,0:T(8,128)(2,1)S(1)}, bf16[128,1024]{1,0:T(8,128)(2,1)S(1)}, u32[]{:S(2)}, u32[]{:S(2)}) %collective-permute-start.11) | collective-permute-done | bytes 262176 | tf_op jit(solution)/shard_map/ppermute | solution.py:715
  80.5 3.6 %collective-permute-done.6.refs_1_ = bf16[128,1024]{1,0:T(8,128)(2,1)S(1)} collective-permute-done((bf16[128,1024]{1,0:T(8,128)(2,1)S(1)}, bf16[128,1024]{1,0:T(8,128)(2,1)S(1)}, u32[]{:S(2)}, u32[]{:S(2)}) %collective-permute-start.6) | collective-permute-done | bytes 262176 | tf_op jit(solution)/shard_map/ppermute | solution.py:715
  84.1 2.8 %collective-permute-done.8.refs_3_ = bf16[128,1024]{1,0:T(8,128)(2,1)S(1)} collective-permute-done((bf16[128,1024]{1,0:T(8,128)(2,1)S(1)}, bf16[128,1024]{1,0:T(8,128)(2,1)S(1)}, u32[]{:S(2)}, u32[]{:S(2)}) %collective-permute-start.8) | collective-permute-done | bytes 262176 | tf_op jit(solution)/shard_map/ppermute | solution.py:715
  86.9 3.3 %shard_map.408 = (bf16[512,1024]{1,0:T(8,128)(2,1)S(1)}, bf16[512,512]{1,0:T(8,128)(2,1)S(1)}, bf16[512,1024]{1,0:T(8,128)(2,1)S(1)}, bf16[128,1024]{1,0:T(8,128...) custom-call(s32[2]{0:T(128)S(1)} %compare_select_fusion.refs_0_.scalar.d_ref, ...), custom_call_target="tpu_custom_call" | custom-call | tf_op jit(solution)/shard_map/pallas_call | solution.py:682
  92.3 8.0 %collective-permute-done.15 = bf16[128,1024]{1,0:T(8,128)(2,1)S(1)} collective-permute-done((bf16[128,1024]{1,0:T(8,128)(2,1)S(1)}, bf16[128,1024]{1,0:T(8,128)(2,1)S(1)}, u32[]{:S(2)}, u32[]{:S(2)}) %collective-permute-start.15) | collective-permute-done | bytes 262176 | tf_op jit(solution)/shard_map/ppermute | solution.py:715
  103.2 12.7 %collective-permute-done.16 = bf16[128,1024]{1,0:T(8,128)(2,1)S(1)} collective-permute-done((bf16[128,1024]{1,0:T(8,128)(2,1)S(1)}, bf16[128,1024]{1,0:T(8,128)(2,1)S(1)}, u32[]{:S(2)}, u32[]{:S(2)}) %collective-permute-start.16) | collective-permute-done | bytes 262176 | tf_op jit(solution)/shard_map/ppermute | solution.py:715
  116.7 7.7 %collective-permute-done.19.refs_3_ = bf16[128,1024]{1,0:T(8,128)(2,1)S(1)} collective-permute-done((bf16[128,1024]{1,0:T(8,128)(2,1)S(1)}, bf16[128,1024]{1,0:T(8,128)(2,1)S(1)}, u32[]{:S(2)}, u32[]{:S(2)}) %collective-permute-start.19) | collective-permute-done | bytes 262176 | tf_op jit(solution)/shard_map/ppermute | solution.py:715
  127.1 3.6 %collective-permute-done.20.refs_4_ = bf16[128,1024]{1,0:T(8,128)(2,1)S(1)} collective-permute-done((bf16[128,1024]{1,0:T(8,128)(2,1)S(1)}, bf16[128,1024]{1,0:T(8,128)(2,1)S(1)}, u32[]{:S(2)}, u32[]{:S(2)}) %collective-permute-start.20) | collective-permute-done | bytes 262176 | tf_op jit(solution)/shard_map/ppermute | solution.py:715
  130.8 5.6 %shard_map.409 = (bf16[512,640]{1,0:T(8,128)(2,1)S(1)}, f32[512,384]{1,0:T(8,128)S(1)}, bf16[512,1024]{1,0:T(8,128)(2,1)S(1)}, bf16[512,1024]{1,0:T(8,128)(2,1)S(1)}) custom-call(s32[2]{0:T(128)S(1)} %compare_select_fusion.refs_0_.scalar.d_ref.t_ref.u_ref, bf16[128,1024]{1,0:T(8,128)(2,1)S(1)} %get-tuple-element.177.refs_1_, ...), custom_call_target="tpu_custom_call" | custom-call | tf_op jit(solution)/shard_map/pallas_call | solution.py:682
  136.4 11.0 %shard_map.410 = (bf16[512,896]{1,0:T(8,128)(2,1)S(1)}, bf16[512,896]{1,0:T(8,128)(2,1)S(1)}, bf16[128,1024]{1,0:T(8,128)(2,1)S(1)}, bf16[128,1024]{1,0:T(8,128)...) custom-call(s32[2]{0:T(128)S(1)} %compare_select_fusion.refs_0_.scalar.d_ref.t_ref.u_ref, ...), custom_call_target="tpu_custom_call" | custom-call | tf_op jit(solution)/shard_map/pallas_call | solution.py:682
  149.6 7.1 %collective-permute-done.12 = bf16[128,1024]{1,0:T(8,128)(2,1)S(1)} collective-permute-done((bf16[128,1024]{1,0:T(8,128)(2,1)S(1)}, bf16[128,1024]{1,0:T(8,128)(2,1)S(1)}, u32[]{:S(2)}, u32[]{:S(2)}) %collective-permute-start.12) | collective-permute-done | bytes 262176 | tf_op jit(solution)/shard_map/ppermute | solution.py:715
  160.5 4.4 %collective-permute-done.14 = bf16[128,1024]{1,0:T(8,128)(2,1)S(1)} collective-permute-done((bf16[128,1024]{1,0:T(8,128)(2,1)S(1)}, bf16[128,1024]{1,0:T(8,128)(2,1)S(1)}, u32[]{:S(2)}, u32[]{:S(2)}) %collective-permute-start.14) | collective-permute-done | bytes 262176 | tf_op jit(solution)/shard_map/ppermute | solution.py:715
  166.4 4.4 %collective-permute-done.13 = bf16[128,1024]{1,0:T(8,128)(2,1)S(1)} collective-permute-done((bf16[128,1024]{1,0:T(8,128)(2,1)S(1)}, bf16[128,1024]{1,0:T(8,128)(2,1)S(1)}, u32[]{:S(2)}, u32[]{:S(2)}) %collective-permute-start.13) | collective-permute-done | bytes 262176 | tf_op jit(solution)/shard_map/ppermute | solution.py:715
  174.1 5.8 %collective-permute-done.21 = bf16[128,1024]{1,0:T(8,128)(2,1)S(1)} collective-permute-done((bf16[128,1024]{1,0:T(8,128)(2,1)S(1)}, bf16[128,1024]{1,0:T(8,128)(2,1)S(1)}, u32[]{:S(2)}, u32[]{:S(2)}) %collective-permute-start.21) | collective-permute-done | bytes 262176 | tf_op jit(solution)/shard_map/ppermute | solution.py:715
  180.4 3.6 %collective-permute-done.50.refs_2_ = bf16[192,1024]{1,0:T(8,128)(2,1)S(1)} collective-permute-done((bf16[192,1024]{1,0:T(8,128)(2,1)S(1)}, bf16[192,1024]{1,0:T(8,128)(2,1)S(1)}, u32[]{:S(2)}, u32[]{:S(2)}) %collective-permute-start.50) | collective-permute-done | bytes 393248 | tf_op jit(solution)/shard_map/ppermute | solution.py:715
  190.7 4.4 %collective-permute-done.26.refs_2_ = bf16[128,896]{1,0:T(8,128)(2,1)S(1)} collective-permute-done((bf16[128,896]{1,0:T(8,128)(2,1)S(1)}, bf16[128,896]{1,0:T(8,128)(2,1)S(1)}, u32[]{:S(2)}, u32[]{:S(2)}) %collective-permute-start.26) | collective-permute-done | bytes 229408 | tf_op jit(solution)/shard_map/ppermute | solution.py:715
  199.0 5.4 %collective-permute-done.28 = bf16[128,512]{1,0:T(8,128)(2,1)S(1)} collective-permute-done((bf16[128,512]{1,0:T(8,128)(2,1)S(1)}, bf16[128,512]{1,0:T(8,128)(2,1)S(1)}, u32[]{:S(2)}, u32[]{:S(2)}) %collective-permute-start.28) | collective-permute-done | bytes 131104 | tf_op jit(solution)/shard_map/ppermute | solution.py:715
  210.4 4.1 %collective-permute-done.40.refs_3_ = bf16[128,1024]{1,0:T(8,128)(2,1)S(1)} collective-permute-done((bf16[128,1024]{1,0:T(8,128)(2,1)S(1)}, bf16[128,1024]{1,0:T(8,128)(2,1)S(1)}, u32[]{:S(2)}, u32[]{:S(2)}) %collective-permute-start.40) | collective-permute-done | bytes 262176 | tf_op jit(solution)/shard_map/ppermute | solution.py:715
  217.2 4.6 %collective-permute-done.29.other_ref = bf16[128,512]{1,0:T(8,128)(2,1)S(1)} collective-permute-done((bf16[128,512]{1,0:T(8,128)(2,1)S(1)}, bf16[128,512]{1,0:T(8,128)(2,1)S(1)}, u32[]{:S(2)}, u32[]{:S(2)}) %collective-permute-start.29) | collective-permute-done | bytes 131104 | tf_op jit(solution)/shard_map/ppermute | solution.py:715
  223.0 5.5 %collective-permute-done.53.refs_2_ = bf16[192,1024]{1,0:T(8,128)(2,1)S(1)} collective-permute-done((bf16[192,1024]{1,0:T(8,128)(2,1)S(1)}, bf16[192,1024]{1,0:T(8,128)(2,1)S(1)}, u32[]{:S(2)}, u32[]{:S(2)}) %collective-permute-start.53) | collective-permute-done | bytes 393248 | tf_op jit(solution)/shard_map/ppermute | solution.py:715
  232.1 7.7 %collective-permute-done.42.refs_2_ = bf16[128,1024]{1,0:T(8,128)(2,1)S(1)} collective-permute-done((bf16[128,1024]{1,0:T(8,128)(2,1)S(1)}, bf16[128,1024]{1,0:T(8,128)(2,1)S(1)}, u32[]{:S(2)}, u32[]{:S(2)}) %collective-permute-start.42) | collective-permute-done | bytes 262176 | tf_op jit(solution)/shard_map/ppermute | solution.py:715
  242.3 7.7 %collective-permute-done.31.refs_2_ = bf16[128,1024]{1,0:T(8,128)(2,1)S(1)} collective-permute-done((bf16[128,1024]{1,0:T(8,128)(2,1)S(1)}, bf16[128,1024]{1,0:T(8,128)(2,1)S(1)}, u32[]{:S(2)}, u32[]{:S(2)}) %collective-permute-start.31) | collective-permute-done | bytes 262176 | tf_op jit(solution)/shard_map/ppermute | solution.py:715
  253.2 3.4 %shard_map.421 = (f32[1024,512]{1,0:T(8,128)}, f32[1024,512]{1,0:T(8,128)}, f32[512,1024]{1,0:T(8,128)}) custom-call(s32[2]{0:T(128)S(1)} %compare_select_fusion.refs_0_.scalar.d_ref.t_ref.u_ref, bf16[192,1024]{1,0:T(8,128)(2,1)S(1)} %shard_map.420.refs_0_, bf16[192,1024]{1,0:T(8,128)(2,1)S(1)} %collective-permute-done.52.refs_1_, ...), custom_call_target="tpu_custom_call" | custom-call | tf_op jit(solution)/shard_map/pallas_call | solution.py:682
  256.6 3.1 %shard_map.417 = (f32[128,1024]{1,0:T(8,128)}, f32[384,1024]{1,0:T(8,128)}, f32[1024,384]{1,0:T(8,128)}, f32[1024,128]{1,0:T(8,128)}) custom-call(s32[2]{0:T(128)S(1)} %compare_select_fusion.refs_0_.scalar.d_ref.t_ref.u_ref, bf16[128,1024]{1,0:T(8,128)(2,1)S(1)} %shard_map.416.refs_0_, bf16[128,1024]{1,0:T(8,128)(2,1)S(1)} %collective-permute-done.41.refs_1_, ...), custom_call_target="tpu_custom_call" | custom-call | tf_op jit(solution)/shard_map/pallas_call | solution.py:682
  259.8 3.3 %shard_map.414 = (f32[1024,128]{1,0:T(8,128)}, f32[1024,128]{1,0:T(8,128)}, f32[1024,256]{1,0:T(8,128)}, f32[1024,384]{1,0:T(8,128)}, f32[6,1024]{1,0:T(8,128)},...) custom-call(s32[2]{0:T(128)S(1)} %compare_select_fusion.refs_0_.scal, ...), custom_call_target="tpu_custom_call" | custom-call | tf_op jit(solution)/shard_map/pallas_call | solution.py:682
  (170 shorter events, 69.5 us)
Async XLA Ops:
  0.7 21.1 %collective-permute-start = (bf16[128,1024]{1,0:T(8,128)(2,1)}, bf16[128,1024]{1,0:T(8,128)(2,1)S(1)}, u32[]{:S(2)}, u32[]{:S(2)}) collective-permute-start(bf16[128,1024]{1,0:T(8,128)(2,1)} %refs_1_.1), channel_id=1, source_target_pairs={{0,1},{1,0},{2,3},{3,2},{4,5},{5,4},{6,7},{7,6},{8,9},{9,8},{10,11... | collective-permute-start | bytes 786440 | tf_op jit(solution)/shard_map/ppermute | solution.py:715
  3.8 14.6 %collective-permute-start.1 = (bf16[128,1024]{1,0:T(8,128)(2,1)}, bf16[128,1024]{1,0:T(8,128)(2,1)S(1)}, u32[]{:S(2)}, u32[]{:S(2)}) collective-permute-start(bf16[128,1024]{1,0:T(8,128)(2,1)} %refs_1_.1), channel_id=1, source_target_pairs={{0,2},{1,3},{2,0},{3,1},{4,6},{5,7},{6,4},{7,5},{8,10},{9,11},{10,... | collective-permute-start | bytes 786440 | tf_op jit(solution)/shard_map/ppermute | solution.py:715
  36.2 14.9 %collective-permute-start.3 = (bf16[128,1024]{1,0:T(8,128)(2,1)S(1)}, bf16[128,1024]{1,0:T(8,128)(2,1)S(1)}, u32[]{:S(2)}, u32[]{:S(2)}) collective-permute-start(bf16[128,1024]{1,0:T(8,128)(2,1)S(1)} %get-tuple-element.101), channel_id=1, source_target_pairs={{0,1},{1,0},{2,3},{3,2},{4,5},{5,4},{6,7},{7,6},{8,9},{9,8},{10,11... | collective-permute-start | bytes 786440 | tf_op jit(solution)/shard_map/ppermute | solution.py:715
  37.4 16.1 %collective-permute-start.10 = (bf16[128,1024]{1,0:T(8,128)(2,1)S(1)}, bf16[128,1024]{1,0:T(8,128)(2,1)S(1)}, u32[]{:S(2)}, u32[]{:S(2)}) collective-permute-start(bf16[128,1024]{1,0:T(8,128)(2,1)S(1)} %copy-done.14), channel_id=1, source_target_pairs={{0,2},{1,3},{2,0},{3,1},{4,6},{5,7},{6,4},{7,5},{8,10},{9,11},{10,... | collective-permute-start | bytes 786440 | tf_op jit(solution)/shard_map/ppermute | solution.py:715
  39.4 25.2 %collective-permute-start.5 = (bf16[128,1024]{1,0:T(8,128)(2,1)S(1)}, bf16[128,1024]{1,0:T(8,128)(2,1)S(1)}, u32[]{:S(2)}, u32[]{:S(2)}) collective-permute-start(bf16[128,1024]{1,0:T(8,128)(2,1)S(1)} %get-tuple-element.102), channel_id=1, source_target_pairs={{0,1},{1,0},{2,3},{3,2},{4,5},{5,4},{6,7},{7,6},{8,9},{9,8},{10,11... | collective-permute-start | bytes 786440 | tf_op jit(solution)/shard_map/ppermute | solution.py:715
  51.1 13.4 %collective-permute-start.4 = (bf16[128,1024]{1,0:T(8,128)(2,1)S(1)}, bf16[128,1024]{1,0:T(8,128)(2,1)S(1)}, u32[]{:S(2)}, u32[]{:S(2)}) collective-permute-start(bf16[128,1024]{1,0:T(8,128)(2,1)S(1)} %add_convert_fusion.4), channel_id=1, source_target_pairs={{0,2},{1,3},{2,0},{3,1},{4,6},{5,7},{6,4},{7,5},{8,10},{9,11},{10,... | collective-permute-start | bytes 786440 | tf_op jit(solution)/shard_map/ppermute | solution.py:715
  51.2 19.5 %collective-permute-start.9 = (bf16[128,1024]{1,0:T(8,128)(2,1)S(1)}, bf16[128,1024]{1,0:T(8,128)(2,1)S(1)}, u32[]{:S(2)}, u32[]{:S(2)}) collective-permute-start(bf16[128,1024]{1,0:T(8,128)(2,1)S(1)} %copy-done.14), channel_id=1, source_target_pairs={{0,1},{1,0},{2,3},{3,2},{4,5},{5,4},{6,7},{7,6},{8,9},{9,8},{10,11... | collective-permute-start | bytes 786440 | tf_op jit(solution)/shard_map/ppermute | solution.py:715
  53.5 24.1 %collective-permute-start.11 = (bf16[128,1024]{1,0:T(8,128)(2,1)S(1)}, bf16[128,1024]{1,0:T(8,128)(2,1)S(1)}, u32[]{:S(2)}, u32[]{:S(2)}) collective-permute-start(bf16[128,1024]{1,0:T(8,128)(2,1)S(1)} %collective-permute-done.10), channel_id=1, source_target_pairs={{0,1},{1,0},{2,3},{3,2},{4,5},{5,4},{6,7},{7,6},{8,9},{9,8},{10,11... | collective-permute-start | bytes 786440 | tf_op jit(solution)/shard_map/ppermute | solution.py:715
  65.0 12.9 %collective-permute-start.7 = (bf16[128,1024]{1,0:T(8,128)(2,1)S(1)}, bf16[128,1024]{1,0:T(8,128)(2,1)S(1)}, u32[]{:S(2)}, u32[]{:S(2)}) collective-permute-start(bf16[128,1024]{1,0:T(8,128)(2,1)S(1)} %multiply_convert_fusion.refs_0_), channel_id=1, source_target_pairs={{0,2},{1,3},{2,0},{3,1},{4,6},{5,7},{6,4},{7,5},{8,10},{9,11},{10,... | collective-permute-start | bytes 786440 | tf_op jit(solution)/shard_map/ppermute | solution.py:715
  100.4 15.5 %collective-permute-start.16 = (bf16[128,1024]{1,0:T(8,128)(2,1)S(1)}, bf16[128,1024]{1,0:T(8,128)(2,1)S(1)}, u32[]{:S(2)}, u32[]{:S(2)}) collective-permute-start(bf16[128,1024]{1,0:T(8,128)(2,1)S(1)} %add_convert_fusion.1), channel_id=1, source_target_pairs={{0,2},{1,3},{2,0},{3,1},{4,6},{5,7},{6,4},{7,5},{8,10},{9,11},{10,... | collective-permute-start | bytes 786440 | tf_op jit(solution)/shard_map/ppermute | solution.py:715
  103.1 54.9 %collective-permute-start.48 = (bf16[768,1024]{1,0:T(8,128)(2,1)S(1)}, bf16[768,1024]{1,0:T(8,128)(2,1)S(1)}, u32[]{:S(2)}, u32[]{:S(2)}) collective-permute-start(bf16[768,1024]{1,0:T(8,128)(2,1)S(1)} %get-tuple-element.167), channel_id=1, source_target_pairs={{0,4},{4,0},{8,12},{12,8},{16,20},{20,16},{24,28},{28,24},{1,5},{5... | collective-permute-start | bytes 4718600 | tf_op jit(solution)/shard_map/ppermute | solution.py:715
  147.4 25.9 %collective-permute-start.24 = (bf16[512,896]{1,0:T(8,128)(2,1)S(1)}, bf16[512,896]{1,0:T(8,128)(2,1)S(1)}, u32[]{:S(2)}, u32[]{:S(2)}) collective-permute-start(bf16[512,896]{1,0:T(8,128)(2,1)S(1)} %get-tuple-element.133), channel_id=1, source_target_pairs={{0,4},{4,0},{8,12},{12,8},{16,20},{20,16},{24,28},{28,24},{1,5},{5... | collective-permute-start | bytes 2752520 | tf_op jit(solution)/shard_map/ppermute | solution.py:715
  147.6 17.3 %collective-permute-start.14 = (bf16[128,1024]{1,0:T(8,128)(2,1)S(1)}, bf16[128,1024]{1,0:T(8,128)(2,1)S(1)}, u32[]{:S(2)}, u32[]{:S(2)}) collective-permute-start(bf16[128,1024]{1,0:T(8,128)(2,1)S(1)} %get-tuple-element.182), channel_id=1, source_target_pairs={{0,1},{1,0},{2,3},{3,2},{4,5},{5,4},{6,7},{7,6},{8,9},{9,8},{10,11... | collective-permute-start | bytes 786440 | tf_op jit(solution)/shard_map/ppermute | solution.py:715
  149.6 37.4 %collective-permute-start.37 = (bf16[512,1024]{1,0:T(8,128)(2,1)S(1)}, bf16[512,1024]{1,0:T(8,128)(2,1)S(1)}, u32[]{:S(2)}, u32[]{:S(2)}) collective-permute-start(bf16[512,1024]{1,0:T(8,128)(2,1)S(1)} %get-tuple-element.142), channel_id=1, source_target_pairs={{0,4},{4,0},{8,12},{12,8},{16,20},{20,16},{24,28},{28,24},{1,5},{5... | collective-permute-start | bytes 3145736 | tf_op jit(solution)/shard_map/ppermute | solution.py:715
  156.8 14.0 %collective-permute-start.13 = (bf16[128,1024]{1,0:T(8,128)(2,1)S(1)}, bf16[128,1024]{1,0:T(8,128)(2,1)S(1)}, u32[]{:S(2)}, u32[]{:S(2)}) collective-permute-start(bf16[128,1024]{1,0:T(8,128)(2,1)S(1)} %add_convert_fusion.3), channel_id=1, source_target_pairs={{0,2},{1,3},{2,0},{3,1},{4,6},{5,7},{6,4},{7,5},{8,10},{9,11},{10,... | collective-permute-start | bytes 786440 | tf_op jit(solution)/shard_map/ppermute | solution.py:715
  159.0 20.9 %collective-permute-start.49 = (bf16[192,1024]{1,0:T(8,128)(2,1)S(1)}, bf16[192,1024]{1,0:T(8,128)(2,1)S(1)}, u32[]{:S(2)}, u32[]{:S(2)}) collective-permute-start(bf16[192,1024]{1,0:T(8,128)(2,1)S(1)} %get-tuple-element.169), channel_id=1, source_target_pairs={{0,8},{4,12},{8,0},{12,4},{16,24},{20,28},{24,16},{28,20},{1,9},{5... | collective-permute-start | bytes 1179656 | tf_op jit(solution)/shard_map/ppermute | solution.py:715
  164.9 19.1 %collective-permute-start.50 = (bf16[192,1024]{1,0:T(8,128)(2,1)S(1)}, bf16[192,1024]{1,0:T(8,128)(2,1)S(1)}, u32[]{:S(2)}, u32[]{:S(2)}) collective-permute-start(bf16[192,1024]{1,0:T(8,128)(2,1)S(1)} %get-tuple-element.170), channel_id=1, source_target_pairs={{0,16},{4,20},{8,24},{12,28},{16,0},{20,4},{24,8},{28,12},{1,17},{... | collective-permute-start | bytes 1179656 | tf_op jit(solution)/shard_map/ppermute | solution.py:715
  170.8 14.6 %collective-permute-start.51 = (bf16[192,1024]{1,0:T(8,128)(2,1)S(1)}, bf16[192,1024]{1,0:T(8,128)(2,1)S(1)}, u32[]{:S(2)}, u32[]{:S(2)}) collective-permute-start(bf16[192,1024]{1,0:T(8,128)(2,1)S(1)} %get-tuple-element.171), channel_id=1, source_target_pairs={{0,24},{4,28},{8,16},{12,20},{16,8},{20,12},{24,0},{28,4},{1,25},{... | collective-permute-start | bytes 1179656 | tf_op jit(solution)/shard_map/ppermute | solution.py:715
  187.0 12.0 %collective-permute-start.22 = (bf16[128,1024]{1,0:T(8,128)(2,1)S(1)}, bf16[128,1024]{1,0:T(8,128)(2,1)S(1)}, u32[]{:S(2)}, u32[]{:S(2)}) collective-permute-start(bf16[128,1024]{1,0:T(8,128)(2,1)S(1)} %add_convert_fusion), channel_id=1, source_target_pairs={{0,2},{1,3},{2,0},{3,1},{4,6},{5,7},{6,4},{7,5},{8,10},{9,11},{10,... | collective-permute-start | bytes 786440 | tf_op jit(solution)/shard_map/ppermute | solution.py:715
  188.6 27.7 %collective-permute-start.52 = (bf16[192,1024]{1,0:T(8,128)(2,1)S(1)}, bf16[192,1024]{1,0:T(8,128)(2,1)S(1)}, u32[]{:S(2)}, u32[]{:S(2)}) collective-permute-start(bf16[192,1024]{1,0:T(8,128)(2,1)S(1)} %shard_map.420.refs_0_), channel_id=1, source_target_pairs={{0,8},{4,12},{8,0},{12,4},{16,24},{20,28},{24,16},{28,20},{1,9},{5... | collective-permute-start | bytes 1179656 | tf_op jit(solution)/shard_map/ppermute | solution.py:715
  189.2 18.6 %collective-permute-start.38 = (bf16[128,1024]{1,0:T(8,128)(2,1)S(1)}, bf16[128,1024]{1,0:T(8,128)(2,1)S(1)}, u32[]{:S(2)}, u32[]{:S(2)}) collective-permute-start(bf16[128,1024]{1,0:T(8,128)(2,1)S(1)} %get-tuple-element.144), channel_id=1, source_target_pairs={{0,8},{4,12},{8,0},{12,4},{16,24},{20,28},{24,16},{28,20},{1,9},{5... | collective-permute-start | bytes 786440 | tf_op jit(solution)/shard_map/ppermute | solution.py:715
  195.1 15.3 %collective-permute-start.39 = (bf16[128,1024]{1,0:T(8,128)(2,1)S(1)}, bf16[128,1024]{1,0:T(8,128)(2,1)S(1)}, u32[]{:S(2)}, u32[]{:S(2)}) collective-permute-start(bf16[128,1024]{1,0:T(8,128)(2,1)S(1)} %get-tuple-element.145), channel_id=1, source_target_pairs={{0,16},{4,20},{8,24},{12,28},{16,0},{20,4},{24,8},{28,12},{1,17},{... | collective-permute-start | bytes 786440 | tf_op jit(solution)/shard_map/ppermute | solution.py:715
  196.6 17.8 %collective-permute-start.40 = (bf16[128,1024]{1,0:T(8,128)(2,1)S(1)}, bf16[128,1024]{1,0:T(8,128)(2,1)S(1)}, u32[]{:S(2)}, u32[]{:S(2)}) collective-permute-start(bf16[128,1024]{1,0:T(8,128)(2,1)S(1)} %get-tuple-element.146), channel_id=1, source_target_pairs={{0,24},{4,28},{8,16},{12,20},{16,8},{20,12},{24,0},{28,4},{1,25},{... | collective-permute-start | bytes 786440 | tf_op jit(solution)/shard_map/ppermute | solution.py:715
  204.4 24.1 %collective-permute-start.53 = (bf16[192,1024]{1,0:T(8,128)(2,1)S(1)}, bf16[192,1024]{1,0:T(8,128)(2,1)S(1)}, u32[]{:S(2)}, u32[]{:S(2)}) collective-permute-start(bf16[192,1024]{1,0:T(8,128)(2,1)S(1)} %shard_map.420.refs_0_), channel_id=1, source_target_pairs={{0,16},{4,20},{8,24},{12,28},{16,0},{20,4},{24,8},{28,12},{1,17},{... | collective-permute-start | bytes 1179656 | tf_op jit(solution)/shard_map/ppermute | solution.py:715
  207.9 21.8 %collective-permute-start.54 = (bf16[192,1024]{1,0:T(8,128)(2,1)S(1)}, bf16[192,1024]{1,0:T(8,128)(2,1)S(1)}, u32[]{:S(2)}, u32[]{:S(2)}) collective-permute-start(bf16[192,1024]{1,0:T(8,128)(2,1)S(1)} %shard_map.420.refs_0_), channel_id=1, source_target_pairs={{0,24},{4,28},{8,16},{12,20},{16,8},{20,12},{24,0},{28,4},{1,25},{... | collective-permute-start | bytes 1179656 | tf_op jit(solution)/shard_map/ppermute | solution.py:715
  210.4 19.3 %collective-permute-start.55 = (bf16[192,1024]{1,0:T(8,128)(2,1)S(1)}, bf16[192,1024]{1,0:T(8,128)(2,1)S(1)}, u32[]{:S(2)}, u32[]{:S(2)}) collective-permute-start(bf16[192,1024]{1,0:T(8,128)(2,1)S(1)} %shard_map.420.refs_0_), channel_id=1, source_target_pairs={{0,4},{4,0},{8,12},{12,8},{16,20},{20,16},{24,28},{28,24},{1,5},{5... | collective-permute-start | bytes 1179656 | tf_op jit(solution)/shard_map/ppermute | solution.py:715
  216.3 14.6 %collective-permute-start.41 = (bf16[128,1024]{1,0:T(8,128)(2,1)S(1)}, bf16[128,1024]{1,0:T(8,128)(2,1)S(1)}, u32[]{:S(2)}, u32[]{:S(2)}) collective-permute-start(bf16[128,1024]{1,0:T(8,128)(2,1)S(1)} %shard_map.416.refs_0_), channel_id=1, source_target_pairs={{0,8},{4,12},{8,0},{12,4},{16,24},{20,28},{24,16},{28,20},{1,9},{5... | collective-permute-start | bytes 786440 | tf_op jit(solution)/shard_map/ppermute | solution.py:715
  221.8 18.0 %collective-permute-start.42 = (bf16[128,1024]{1,0:T(8,128)(2,1)S(1)}, bf16[128,1024]{1,0:T(8,128)(2,1)S(1)}, u32[]{:S(2)}, u32[]{:S(2)}) collective-permute-start(bf16[128,1024]{1,0:T(8,128)(2,1)S(1)} %shard_map.416.refs_0_), channel_id=1, source_target_pairs={{0,16},{4,20},{8,24},{12,28},{16,0},{20,4},{24,8},{28,12},{1,17},{... | collective-permute-start | bytes 786440 | tf_op jit(solution)/shard_map/ppermute | solution.py:715
  228.5 13.3 %collective-permute-start.43 = (bf16[128,1024]{1,0:T(8,128)(2,1)S(1)}, bf16[128,1024]{1,0:T(8,128)(2,1)S(1)}, u32[]{:S(2)}, u32[]{:S(2)}) collective-permute-start(bf16[128,1024]{1,0:T(8,128)(2,1)S(1)} %shard_map.416.refs_0_), channel_id=1, source_target_pairs={{0,24},{4,28},{8,16},{12,20},{16,8},{20,12},{24,0},{28,4},{1,25},{... | collective-permute-start | bytes 786440 | tf_op jit(solution)/shard_map/ppermute | solution.py:715
  229.6 12.1 %collective-permute-start.44 = (bf16[128,1024]{1,0:T(8,128)(2,1)S(1)}, bf16[128,1024]{1,0:T(8,128)(2,1)S(1)}, u32[]{:S(2)}, u32[]{:S(2)}) collective-permute-start(bf16[128,1024]{1,0:T(8,128)(2,1)S(1)} %shard_map.416.refs_0_), channel_id=1, source_target_pairs={{0,4},{4,0},{8,12},{12,8},{16,20},{20,16},{24,28},{28,24},{1,5},{5... | collective-permute-start | bytes 786440 | tf_op jit(solution)/shard_map/ppermute | solution.py:715
  229.6 12.6 %collective-permute-start.30 = (bf16[128,1024]{1,0:T(8,128)(2,1)S(1)}, bf16[128,1024]{1,0:T(8,128)(2,1)S(1)}, u32[]{:S(2)}, u32[]{:S(2)}) collective-permute-start(bf16[128,1024]{1,0:T(8,128)(2,1)S(1)} %shard_map.413.refs_0_), channel_id=1, source_target_pairs={{0,8},{4,12},{8,0},{12,4},{16,24},{20,28},{24,16},{28,20},{1,9},{5... | collective-permute-start | bytes 786440 | tf_op jit(solution)/shard_map/ppermute | solution.py:715
  231.0 19.1 %collective-permute-start.31 = (bf16[128,1024]{1,0:T(8,128)(2,1)S(1)}, bf16[128,1024]{1,0:T(8,128)(2,1)S(1)}, u32[]{:S(2)}, u32[]{:S(2)}) collective-permute-start(bf16[128,1024]{1,0:T(8,128)(2,1)S(1)} %shard_map.413.refs_0_), channel_id=1, source_target_pairs={{0,16},{4,20},{8,24},{12,28},{16,0},{20,4},{24,8},{28,12},{1,17},{... | collective-permute-start | bytes 786440 | tf_op jit(solution)/shard_map/ppermute | solution.py:715
  (43 other events, 523.9 us)
where the time goes:
time: 264 us
  waiting for transfers between devices  156 us (59%)
  Pallas kernels  47.8 us (18%)
  starting transfers between devices  46.1 us (17%)
  local copies, waits for them, and re-layouts  6.06 us (2%)
  other arithmetic  5.58 us (2%)
    ppermute x59, waiting for transfers between devices, swap(): return lax.ppermute(value, axis, xor_pairs(size, bit))  156 us
    pallas_call x15, Pallas kernels, call_kernel(): pl.pallas_call(body, in_specs=[pl.BlockSpec(memory_space=pltpu.SMEM)] + [...  47.8 us
    ppermute x59, starting transfers between devices, swap(): return lax.ppermute(value, axis, xor_pairs(size, bit))  46.1 us
  transfers between devices with their start and end apart: 59, of which 29 were waited for; matrix products, arithmetic and copies ran while one was open for 4% of the time, Pallas kernels for 12%

commit v1 on v0

--- a/solution.py
+++ b/solution.py
@@ -17,6 +17,9 @@
 big_negative = -1e30
 f32 = jnp.float32
 bf16 = jnp.bfloat16
+
+DP = "dp"
+TP = "tensor"
 
 
 def dot(left, right):
@@ -564,6 +567,16 @@
     out_ref[:, at:] = own_ref[:, picked:]
 
 
+def input_grad_body(t_ref, *refs):
+    *hops, inputs_ref, dhidden_ref, gain_ref, out_ref = refs
+    xf = inputs_ref[...].astype(f32)
+    recip = rms_recip(xf)
+    unit = xf * recip
+    scaled = sum_of([hop[...] for hop in hops]) * gain_ref[...]
+    mean = jnp.mean(scaled * unit, axis=-1, keepdims=True)
+    out_ref[...] = dhidden_ref[...] + recip * (scaled - unit * mean)
+
+
 def piece_places(d, groups):
     for side in range(2):
         half = d % 2 if side == 0 else 1 - d % 2
@@ -723,39 +736,46 @@
     got = {0: value}
     for k in range(size - 1, 0, -1):
         if lowest_bit(k) == k:
-            got[k] = swap(value, "tensor", size, k)
+            got[k] = swap(value, TP, size, k)
     for k in range(1, size):
         low = lowest_bit(k)
         if k != low:
-            got[k] = swap(got[k ^ low], "tensor", size, low)
+            got[k] = swap(got[k ^ low], TP, size, low)
     return [got[k] for k in range(size)]
 
 
-def scatter_parts(blocks, size):
+def scatter_parts(blocks, size, total=True):
     held = list(blocks)
     for k in range(size - 1, 0, -1):
         low = lowest_bit(k)
         if k != low:
-            came = swap(held[k], "tensor", size, low)
+            came = swap(held[k], TP, size, low)
             held[k ^ low] = (held[k ^ low].astype(f32) + came.astype(f32)).astype(bf16)
-    total = held[0].astype(f32)
+    hops = [held[0]]
     for k in range(size - 1, 0, -1):
         if lowest_bit(k) == k:
-            total = total + swap(held[k], "tensor", size, k).astype(f32)
+            hops.append(swap(held[k], TP, size, k))
+    return sum_of(hops) if total else hops
+
+
+def sum_of(arrays):
+    total = arrays[0].astype(f32)
+    for value in arrays[1:]:
+        total = total + value.astype(f32)
     return total
 
 
 def sum_over_dp(keep, send, size, index, between=None, picked=0):
     groups = size // 2
     rows, width = keep.shape[0] // groups, keep.shape[1]
-    came = swap(send, "dp", size, 1)
+    came = swap(send, DP, size, 1)
     pieces = call_kernel(
         functools.partial(add_split_body, groups),
         index,
         (keep, came),
         [((rows, width), bf16)] * groups,
     )
-    came = [swap(pieces[j], "dp", size, 2 * j) for j in range(1, groups)]
+    came = [swap(pieces[j], DP, size, 2 * j) for j in range(1, groups)]
     outs = [((rows, width), bf16)]
     if picked:
         outs = outs + [((rows, picked), bf16)]
@@ -765,8 +785,8 @@
     if between is not None:
         total = between(total, *rest)
     mine = [total]
-    mine = mine + [swap(total, "dp", size, 2 * j) for j in range(1, groups)]
-    return mine + [swap(piece, "dp", size, 1) for piece in mine]
+    mine = mine + [swap(total, DP, size, 2 * j) for j in range(1, groups)]
+    return mine + [swap(piece, DP, size, 1) for piece in mine]
 
 
 def block(
@@ -812,9 +832,9 @@
     units = gate_weight.shape[1]
     kc = kernel_input.shape[0]
     widths = (wq, wkv, wx, wx, wbc, wst)
-    t_index = lax.axis_index("tensor")
+    t_index = lax.axis_index(TP)
     t_array = jnp.where(
-        lax.iota(jnp.int32, 2) == 0, t_index, lax.axis_index("dp")
+        lax.iota(jnp.int32, 2) == 0, t_index, lax.axis_index(DP)
     ).astype(jnp.int32)
 
     parts = gather_parts(inputs, tensor)
@@ -872,8 +892,6 @@
     mask, g, run, run_t, dt, link, *mixed_blocks = held
 
     inputs_float = inputs.astype(f32)
-    reciprocal_first = rms_recip(inputs_float)
-    unit_first = inputs_float * reciprocal_first
     hidden_first = inputs_float + scatter_parts(mixed_blocks, tensor)
     reciprocal_second = rms_recip(hidden_first)
     unit_second = hidden_first * reciprocal_second
@@ -947,27 +965,30 @@
             ((LANES, width), f32),
         ],
     )
-    dn1 = scatter_parts(dn1_blocks, tensor)
-    scaled_first = dn1 * mixers_norm_gain[None, :]
-    block_input_gradient = grad_hidden + reciprocal_first * (
-        scaled_first - unit_first * jnp.mean(scaled_first * unit_first, axis=-1, keepdims=True)
-    )
-
+    dn1_hops = scatter_parts(dn1_blocks, tensor, total=False)
     picked = wkv + wbc + wst
     wide = 2 * KVH * HD + wbc + wst + wx
 
     def combine(own, shared):
-        pair = shared + swap(shared, "tensor", tensor, 1)
+        pair = shared + swap(shared, TP, tensor, 1)
         (out,) = call_kernel(
             functools.partial(combine_body, widths, heads, 2 * kc, local_heads),
             t_array,
-            (own, pair, swap(pair, "tensor", tensor, 2)),
+            (own, pair, swap(pair, TP, tensor, 2)),
             [((own.shape[0], wide), bf16)],
         )
         return out
 
     late_sum = sum_over_dp(late_keep, late_send, dp, t_array, combine, picked)
 
+    (dn1_hops, _) = lax.optimization_barrier((dn1_hops, late_sum[len(late_sum) // 2 :]))
+    (block_input_gradient,) = call_kernel(
+        input_grad_body,
+        t_array,
+        (*dn1_hops, inputs, grad_hidden, gain1),
+        [((rows, width), f32)],
+        leaves=True,
+    )
     groups = dp // 2
     feed_shapes = [((width, units), f32), ((width, units), f32), ((units, width), f32)]
     grad_gate, grad_up, grad_down = call_kernel(
@@ -1072,55 +1093,55 @@
 
 def solution(mesh):
     in_specs = (
-        P(("dp", "tensor"), None),
-        P("dp"),
-        P(),
-        P(None, "tensor"),
-        P(),
-        P(),
-        P("tensor", None),
-        P(None, "tensor"),
-        P(None, "tensor"),
-        P(),
-        P(None, "tensor"),
-        P(None, "tensor"),
-        P(),
-        P("tensor"),
-        P(),
-        P("tensor"),
-        P("tensor"),
-        P("tensor"),
-        P("tensor", None),
-        P(),
-        P(None, "tensor"),
-        P(None, "tensor"),
-        P("tensor", None),
-        P(("dp", "tensor"), None),
+        P((DP, TP), None),
+        P(DP),
+        P(),
+        P(None, TP),
+        P(),
+        P(),
+        P(TP, None),
+        P(None, TP),
+        P(None, TP),
+        P(),
+        P(None, TP),
+        P(None, TP),
+        P(),
+        P(TP),
+        P(),
+        P(TP),
+        P(TP),
+        P(TP),
+        P(TP, None),
+        P(),
+        P(None, TP),
+        P(None, TP),
+        P(TP, None),
+        P((DP, TP), None),
     )
     out_specs = (
-        P(("dp", "tensor"), None),
-        P(("dp", "tensor"), None),
-        P(),
-        P(None, "tensor"),
-        P(),
-        P(),
-        P("tensor", None),
-        P(None, "tensor"),
-        P(None, "tensor"),
-        P(),
-        P(None, "tensor"),
-        P(None, "tensor"),
-        P(),
-        P("tensor"),
-        P(),
-        P("tensor"),
-        P("tensor"),
-        P("tensor"),
-        P("tensor", None),
-        P(),
-        P(None, "tensor"),
-        P(None, "tensor"),
-        P("tensor", None),
-    )
-    body = functools.partial(block, dp=mesh.shape["dp"], tensor=mesh.shape["tensor"])
+        P((DP, TP), None),
+        P((DP, TP), None),
+        P(),
+        P(None, TP),
+        P(),
+        P(),
+        P(TP, None),
+        P(None, TP),
+        P(None, TP),
+        P(),
+        P(None, TP),
+        P(None, TP),
+        P(),
+        P(TP),
+        P(),
+        P(TP),
+        P(TP),
+        P(TP),
+        P(TP, None),
+        P(),
+        P(None, TP),
+        P(None, TP),
+        P(TP, None),
+    )
+    body = functools.partial(block, dp=mesh.shape[DP], tensor=mesh.shape[TP])
     return jax.shard_map(body, mesh=mesh, in_specs=in_specs, out_specs=out_specs, check_vma=False)

time: 264 us -> 275 us (1.042)
  waiting for transfers between devices: 156 us -> 165 us
    ppermute x59, waiting for transfers between devices: 156 us -> 165 us  [swap(): return lax.ppermute(value, axis, xor_pairs(size, bit))]
    pallas_call x15 -> x16, Pallas kernels: 47.8 us -> 48.4 us  [call_kernel(): pl.pallas_call(body, in_specs=[pl.BlockSpec(memory_space=pltpu.SMEM)] + [...]
  transfers between devices with their start and end apart: 59 -> 59, of which waited for: 29 -> 31; matrix products, arithmetic and copies ran while one was open for 4% -> 3% of each run, Pallas kernels for 12% -> 11%
where the time goes in v1:
time: 275 us
  waiting for transfers between devices  165 us (60%)
  Pallas kernels  48.4 us (18%)
  starting transfers between devices  46.4 us (17%)
  local copies, waits for them, and re-layouts  7.71 us (3%)
  other arithmetic  4.37 us (2%)
    ppermute x59, waiting for transfers between devices, swap(): return lax.ppermute(value, axis, xor_pairs(size, bit))  165 us
    pallas_call x16, Pallas kernels, call_kernel(): pl.pallas_call(body, in_specs=[pl.BlockSpec(memory_space=pltpu.SMEM)] + [...  48.4 us
    ppermute x59, starting transfers between devices, swap(): return lax.ppermute(value, axis, xor_pairs(size, bit))  46.4 us
  transfers between devices with their start and end apart: 59, of which 31 were waited for; matrix products, arithmetic and copies ran while one was open for 3% of the time, Pallas kernels for 11%

profile of v1, /device:TPU:0, one launch (start us, length us, event | category | flops | bytes accessed | tf_op | source)
XLA Modules:
  0.0 274.6 jit_solution(4920633922662075642)
XLA Ops:
  0.7 3.1 %collective-permute-start = (bf16[128,1024]{1,0:T(8,128)(2,1)}, bf16[128,1024]{1,0:T(8,128)(2,1)S(1)}, u32[]{:S(2)}, u32[]{:S(2)}) collective-permute-start(bf16[128,1024]{1,0:T(8,128)(2,1)} %refs_3_.1), channel_id=1, source_target_pairs={{0,1},{1,0},{2,3},{3,2},{4,5},{5,4},{6,7},{7,6},{8,9},{9,8},{10,11... | collective-permute-start | bytes 786440 | tf_op jit(solution)/shard_map/ppermute | solution.py:728
  9.8 8.6 %collective-permute-done.1.refs_3_ = bf16[128,1024]{1,0:T(8,128)(2,1)S(1)} collective-permute-done((bf16[128,1024]{1,0:T(8,128)(2,1)}, bf16[128,1024]{1,0:T(8,128)(2,1)S(1)}, u32[]{:S(2)}, u32[]{:S(2)}) %collective-permute-start.1) | collective-permute-done | bytes 262176 | tf_op jit(solution)/shard_map/ppermute | solution.py:728
  21.8 3.1 %collective-permute-done.2.refs_4_ = bf16[128,1024]{1,0:T(8,128)(2,1)} collective-permute-done((bf16[128,1024]{1,0:T(8,128)(2,1)S(1)}, bf16[128,1024]{1,0:T(8,128)(2,1)}, u32[]{:S(2)}, u32[]{:S(2)}) %collective-permute-start.2) | collective-permute-done | bytes 262176 | tf_op jit(solution)/shard_map/ppermute | solution.py:728
  26.0 9.9 %shard_map.407 = (bf16[512,1024]{1,0:T(8,128)(2,1)S(1)}, bf16[512,384]{1,0:T(8,128)(2,1)S(1)}, bf16[512,128]{1,0:T(8,128)(2,1)S(1)}, f32[512,128]{1,0:T(8,128)S(...) custom-call(s32[2]{0:T(128)S(1)} %compare_select_fusion.refs_0_.scal, ...), custom_call_target="tpu_custom_call" | custom-call | tf_op jit(solution)/shard_map/pallas_call | solution.py:695
  39.1 11.6 %collective-permute-done.3 = bf16[128,1024]{1,0:T(8,128)(2,1)S(1)} collective-permute-done((bf16[128,1024]{1,0:T(8,128)(2,1)S(1)}, bf16[128,1024]{1,0:T(8,128)(2,1)S(1)}, u32[]{:S(2)}, u32[]{:S(2)}) %collective-permute-start.3) | collective-permute-done | bytes 262176 | tf_op jit(solution)/shard_map/ppermute | solution.py:728
  53.3 10.9 %collective-permute-done.5 = bf16[128,1024]{1,0:T(8,128)(2,1)S(1)} collective-permute-done((bf16[128,1024]{1,0:T(8,128)(2,1)S(1)}, bf16[128,1024]{1,0:T(8,128)(2,1)S(1)}, u32[]{:S(2)}, u32[]{:S(2)}) %collective-permute-start.5) | collective-permute-done | bytes 262176 | tf_op jit(solution)/shard_map/ppermute | solution.py:728
  64.7 5.7 %collective-permute-done.9 = bf16[128,1024]{1,0:T(8,128)(2,1)S(1)} collective-permute-done((bf16[128,1024]{1,0:T(8,128)(2,1)S(1)}, bf16[128,1024]{1,0:T(8,128)(2,1)S(1)}, u32[]{:S(2)}, u32[]{:S(2)}) %collective-permute-start.9) | collective-permute-done | bytes 262176 | tf_op jit(solution)/shard_map/ppermute | solution.py:728
  70.4 6.9 %collective-permute-done.11 = bf16[128,1024]{1,0:T(8,128)(2,1)S(1)} collective-permute-done((bf16[128,1024]{1,0:T(8,128)(2,1)S(1)}, bf16[128,1024]{1,0:T(8,128)(2,1)S(1)}, u32[]{:S(2)}, u32[]{:S(2)}) %collective-permute-start.11) | collective-permute-done | bytes 262176 | tf_op jit(solution)/shard_map/ppermute | solution.py:728
  80.2 3.6 %collective-permute-done.6.refs_1_ = bf16[128,1024]{1,0:T(8,128)(2,1)S(1)} collective-permute-done((bf16[128,1024]{1,0:T(8,128)(2,1)S(1)}, bf16[128,1024]{1,0:T(8,128)(2,1)S(1)}, u32[]{:S(2)}, u32[]{:S(2)}) %collective-permute-start.6) | collective-permute-done | bytes 262176 | tf_op jit(solution)/shard_map/ppermute | solution.py:728
  83.8 2.8 %collective-permute-done.8.refs_3_ = bf16[128,1024]{1,0:T(8,128)(2,1)S(1)} collective-permute-done((bf16[128,1024]{1,0:T(8,128)(2,1)S(1)}, bf16[128,1024]{1,0:T(8,128)(2,1)S(1)}, u32[]{:S(2)}, u32[]{:S(2)}) %collective-permute-start.8) | collective-permute-done | bytes 262176 | tf_op jit(solution)/shard_map/ppermute | solution.py:728
  86.6 3.3 %shard_map.408 = (bf16[512,1024]{1,0:T(8,128)(2,1)S(1)}, bf16[512,512]{1,0:T(8,128)(2,1)S(1)}, bf16[512,1024]{1,0:T(8,128)(2,1)S(1)}, bf16[128,1024]{1,0:T(8,128...) custom-call(s32[2]{0:T(128)S(1)} %compare_select_fusion.refs_0_.scalar.d_ref, ...), custom_call_target="tpu_custom_call" | custom-call | tf_op jit(solution)/shard_map/pallas_call | solution.py:695
  92.0 8.1 %collective-permute-done.15 = bf16[128,1024]{1,0:T(8,128)(2,1)S(1)} collective-permute-done((bf16[128,1024]{1,0:T(8,128)(2,1)S(1)}, bf16[128,1024]{1,0:T(8,128)(2,1)S(1)}, u32[]{:S(2)}, u32[]{:S(2)}) %collective-permute-start.15) | collective-permute-done | bytes 262176 | tf_op jit(solution)/shard_map/ppermute | solution.py:728
  102.9 12.7 %collective-permute-done.16 = bf16[128,1024]{1,0:T(8,128)(2,1)S(1)} collective-permute-done((bf16[128,1024]{1,0:T(8,128)(2,1)S(1)}, bf16[128,1024]{1,0:T(8,128)(2,1)S(1)}, u32[]{:S(2)}, u32[]{:S(2)}) %collective-permute-start.16) | collective-permute-done | bytes 262176 | tf_op jit(solution)/shard_map/ppermute | solution.py:728
  120.0 4.1 %collective-permute-done.19.refs_3_ = bf16[128,1024]{1,0:T(8,128)(2,1)S(1)} collective-permute-done((bf16[128,1024]{1,0:T(8,128)(2,1)S(1)}, bf16[128,1024]{1,0:T(8,128)(2,1)S(1)}, u32[]{:S(2)}, u32[]{:S(2)}) %collective-permute-start.19) | collective-permute-done | bytes 262176 | tf_op jit(solution)/shard_map/ppermute | solution.py:728
  124.2 5.5 %collective-permute-done.18.refs_2_ = bf16[128,1024]{1,0:T(8,128)(2,1)S(1)} collective-permute-done((bf16[128,1024]{1,0:T(8,128)(2,1)S(1)}, bf16[128,1024]{1,0:T(8,128)(2,1)S(1)}, u32[]{:S(2)}, u32[]{:S(2)}) %collective-permute-start.18) | collective-permute-done | bytes 262176 | tf_op jit(solution)/shard_map/ppermute | solution.py:728
  129.7 5.6 %collective-permute-done.20.refs_4_ = bf16[128,1024]{1,0:T(8,128)(2,1)S(1)} collective-permute-done((bf16[128,1024]{1,0:T(8,128)(2,1)S(1)}, bf16[128,1024]{1,0:T(8,128)(2,1)S(1)}, u32[]{:S(2)}, u32[]{:S(2)}) %collective-permute-start.20) | collective-permute-done | bytes 262176 | tf_op jit(solution)/shard_map/ppermute | solution.py:728
  135.3 5.6 %shard_map.409 = (bf16[512,640]{1,0:T(8,128)(2,1)S(1)}, f32[512,384]{1,0:T(8,128)S(1)}, bf16[512,1024]{1,0:T(8,128)(2,1)S(1)}, bf16[512,1024]{1,0:T(8,128)(2,1)S(1)}) custom-call(s32[2]{0:T(128)S(1)} %compare_select_fusion.refs_0_.scalar.d_ref.t_ref.u_ref, bf16[128,1024]{1,0:T(8,128)(2,1)S(1)} %get-tuple-element.183.refs_1_, ...), custom_call_target="tpu_custom_call" | custom-call | tf_op jit(solution)/shard_map/pallas_call | solution.py:695
  140.8 10.4 %shard_map.410 = (bf16[512,896]{1,0:T(8,128)(2,1)S(1)}, bf16[512,896]{1,0:T(8,128)(2,1)S(1)}, bf16[128,1024]{1,0:T(8,128)(2,1)S(1)}, bf16[128,1024]{1,0:T(8,128)...) custom-call(s32[2]{0:T(128)S(1)} %compare_select_fusion.refs_0_.scalar.d_ref.t_ref.u_ref, ...), custom_call_target="tpu_custom_call" | custom-call | tf_op jit(solution)/shard_map/pallas_call | solution.py:695
  154.7 7.2 %collective-permute-done.12 = bf16[128,1024]{1,0:T(8,128)(2,1)S(1)} collective-permute-done((bf16[128,1024]{1,0:T(8,128)(2,1)S(1)}, bf16[128,1024]{1,0:T(8,128)(2,1)S(1)}, u32[]{:S(2)}, u32[]{:S(2)}) %collective-permute-start.12) | collective-permute-done | bytes 262176 | tf_op jit(solution)/shard_map/ppermute | solution.py:728
  172.1 3.1 %collective-permute-done.13 = bf16[128,1024]{1,0:T(8,128)(2,1)S(1)} collective-permute-done((bf16[128,1024]{1,0:T(8,128)(2,1)S(1)}, bf16[128,1024]{1,0:T(8,128)(2,1)S(1)}, u32[]{:S(2)}, u32[]{:S(2)}) %collective-permute-start.13) | collective-permute-done | bytes 262176 | tf_op jit(solution)/shard_map/ppermute | solution.py:728
  179.7 15.6 %collective-permute-done.27.refs_3_ = bf16[128,896]{1,0:T(8,128)(2,1)S(1)} collective-permute-done((bf16[128,896]{1,0:T(8,128)(2,1)S(1)}, bf16[128,896]{1,0:T(8,128)(2,1)S(1)}, u32[]{:S(2)}, u32[]{:S(2)}) %collective-permute-start.27) | collective-permute-done | bytes 229408 | tf_op jit(solution)/shard_map/ppermute | solution.py:728
  207.5 2.8 %collective-permute-done.39.refs_2_ = bf16[128,1024]{1,0:T(8,128)(2,1)S(1)} collective-permute-done((bf16[128,1024]{1,0:T(8,128)(2,1)S(1)}, bf16[128,1024]{1,0:T(8,128)(2,1)S(1)}, u32[]{:S(2)}, u32[]{:S(2)}) %collective-permute-start.39) | collective-permute-done | bytes 262176 | tf_op jit(solution)/shard_map/ppermute | solution.py:728
  210.3 10.0 %collective-permute-done.40.refs_3_ = bf16[128,1024]{1,0:T(8,128)(2,1)S(1)} collective-permute-done((bf16[128,1024]{1,0:T(8,128)(2,1)S(1)}, bf16[128,1024]{1,0:T(8,128)(2,1)S(1)}, u32[]{:S(2)}, u32[]{:S(2)}) %collective-permute-start.40) | collective-permute-done | bytes 262176 | tf_op jit(solution)/shard_map/ppermute | solution.py:728
  223.3 10.5 %collective-permute-done.53.refs_2_ = bf16[192,1024]{1,0:T(8,128)(2,1)S(1)} collective-permute-done((bf16[192,1024]{1,0:T(8,128)(2,1)S(1)}, bf16[192,1024]{1,0:T(8,128)(2,1)S(1)}, u32[]{:S(2)}, u32[]{:S(2)}) %collective-permute-start.53) | collective-permute-done | bytes 393248 | tf_op jit(solution)/shard_map/ppermute | solution.py:728
  234.6 3.5 %collective-permute-start.31 = (bf16[128,1024]{1,0:T(8,128)(2,1)S(1)}, bf16[128,1024]{1,0:T(8,128)(2,1)S(1)}, u32[]{:S(2)}, u32[]{:S(2)}) collective-permute-start(bf16[128,1024]{1,0:T(8,128)(2,1)S(1)} %shard_map.413.refs_0_), channel_id=1, source_target_pairs={{0,8},{4,12},{8,0},{12,4},{16,24},{20,28},{24,16},{28,20},{1,9},{5... | collective-permute-start | bytes 786440 | tf_op jit(solution)/shard_map/ppermute | solution.py:728
  238.3 5.6 %collective-permute-done.42.refs_2_ = bf16[128,1024]{1,0:T(8,128)(2,1)S(1)} collective-permute-done((bf16[128,1024]{1,0:T(8,128)(2,1)S(1)}, bf16[128,1024]{1,0:T(8,128)(2,1)S(1)}, u32[]{:S(2)}, u32[]{:S(2)}) %collective-permute-start.42) | collective-permute-done | bytes 262176 | tf_op jit(solution)/shard_map/ppermute | solution.py:728
  243.9 5.6 %collective-permute-done.31.refs_1_ = bf16[128,1024]{1,0:T(8,128)(2,1)S(1)} collective-permute-done((bf16[128,1024]{1,0:T(8,128)(2,1)S(1)}, bf16[128,1024]{1,0:T(8,128)(2,1)S(1)}, u32[]{:S(2)}, u32[]{:S(2)}) %collective-permute-start.31) | collective-permute-done | bytes 262176 | tf_op jit(solution)/shard_map/ppermute | solution.py:728
  249.5 5.0 %collective-permute-done.33.refs_2_ = bf16[128,1024]{1,0:T(8,128)(2,1)S(1)} collective-permute-done((bf16[128,1024]{1,0:T(8,128)(2,1)S(1)}, bf16[128,1024]{1,0:T(8,128)(2,1)S(1)}, u32[]{:S(2)}, u32[]{:S(2)}) %collective-permute-start.33) | collective-permute-done | bytes 262176 | tf_op jit(solution)/shard_map/ppermute | solution.py:728
  257.8 3.4 %shard_map.422 = (f32[1024,512]{1,0:T(8,128)}, f32[1024,512]{1,0:T(8,128)}, f32[512,1024]{1,0:T(8,128)}) custom-call(s32[2]{0:T(128)S(1)} %compare_select_fusion.refs_0_.scalar.d_ref.t_ref.u_ref, bf16[192,1024]{1,0:T(8,128)(2,1)S(1)} %shard_map.421.refs_0_, bf16[192,1024]{1,0:T(8,128)(2,1)S(1)} %collective-permute-done.52.refs_1_, ...), custom_call_target="tpu_custom_call" | custom-call | tf_op jit(solution)/shard_map/pallas_call | solution.py:695
  261.2 3.1 %shard_map.418 = (f32[128,1024]{1,0:T(8,128)}, f32[384,1024]{1,0:T(8,128)}, f32[1024,384]{1,0:T(8,128)}, f32[1024,128]{1,0:T(8,128)}) custom-call(s32[2]{0:T(128)S(1)} %compare_select_fusion.refs_0_.scalar.d_ref.t_ref.u_ref, bf16[128,1024]{1,0:T(8,128)(2,1)S(1)} %shard_map.417.refs_0_, bf16[128,1024]{1,0:T(8,128)(2,1)S(1)} %collective-permute-done.41.refs_1_, ...), custom_call_target="tpu_custom_call" | custom-call | tf_op jit(solution)/shard_map/pallas_call | solution.py:695
  264.4 3.6 %collective-permute-done.22.refs_1_ = bf16[128,1024]{1,0:T(8,128)(2,1)S(1)} collective-permute-done((bf16[128,1024]{1,0:T(8,128)(2,1)S(1)}, bf16[128,1024]{1,0:T(8,128)(2,1)S(1)}, u32[]{:S(2)}, u32[]{:S(2)}) %collective-permute-start.22) | collective-permute-done | bytes 262176 | tf_op jit(solution)/shard_map/ppermute | solution.py:728
  268.0 3.3 %shard_map.415 = (f32[1024,128]{1,0:T(8,128)}, f32[1024,128]{1,0:T(8,128)}, f32[1024,256]{1,0:T(8,128)}, f32[1024,384]{1,0:T(8,128)}, f32[6,1024]{1,0:T(8,128)},...) custom-call(s32[2]{0:T(128)S(1)} %compare_select_fusion.refs_0_.scal, ...), custom_call_target="tpu_custom_call" | custom-call | tf_op jit(solution)/shard_map/pallas_call | solution.py:695
  (177 shorter events, 69.7 us)
Async XLA Ops:
  0.7 21.1 %collective-permute-start = (bf16[128,1024]{1,0:T(8,128)(2,1)}, bf16[128,1024]{1,0:T(8,128)(2,1)S(1)}, u32[]{:S(2)}, u32[]{:S(2)}) collective-permute-start(bf16[128,1024]{1,0:T(8,128)(2,1)} %refs_3_.1), channel_id=1, source_target_pairs={{0,1},{1,0},{2,3},{3,2},{4,5},{5,4},{6,7},{7,6},{8,9},{9,8},{10,11... | collective-permute-start | bytes 786440 | tf_op jit(solution)/shard_map/ppermute | solution.py:728
  3.8 14.6 %collective-permute-start.1 = (bf16[128,1024]{1,0:T(8,128)(2,1)}, bf16[128,1024]{1,0:T(8,128)(2,1)S(1)}, u32[]{:S(2)}, u32[]{:S(2)}) collective-permute-start(bf16[128,1024]{1,0:T(8,128)(2,1)} %refs_3_.1), channel_id=1, source_target_pairs={{0,2},{1,3},{2,0},{3,1},{4,6},{5,7},{6,4},{7,5},{8,10},{9,11},{10,... | collective-permute-start | bytes 786440 | tf_op jit(solution)/shard_map/ppermute | solution.py:728
  35.9 14.9 %collective-permute-start.3 = (bf16[128,1024]{1,0:T(8,128)(2,1)S(1)}, bf16[128,1024]{1,0:T(8,128)(2,1)S(1)}, u32[]{:S(2)}, u32[]{:S(2)}) collective-permute-start(bf16[128,1024]{1,0:T(8,128)(2,1)S(1)} %get-tuple-element.104), channel_id=1, source_target_pairs={{0,1},{1,0},{2,3},{3,2},{4,5},{5,4},{6,7},{7,6},{8,9},{9,8},{10,11... | collective-permute-start | bytes 786440 | tf_op jit(solution)/shard_map/ppermute | solution.py:728
  37.1 16.1 %collective-permute-start.10 = (bf16[128,1024]{1,0:T(8,128)(2,1)S(1)}, bf16[128,1024]{1,0:T(8,128)(2,1)S(1)}, u32[]{:S(2)}, u32[]{:S(2)}) collective-permute-start(bf16[128,1024]{1,0:T(8,128)(2,1)S(1)} %copy-done.19), channel_id=1, source_target_pairs={{0,2},{1,3},{2,0},{3,1},{4,6},{5,7},{6,4},{7,5},{8,10},{9,11},{10,... | collective-permute-start | bytes 786440 | tf_op jit(solution)/shard_map/ppermute | solution.py:728
  39.0 25.2 %collective-permute-start.5 = (bf16[128,1024]{1,0:T(8,128)(2,1)S(1)}, bf16[128,1024]{1,0:T(8,128)(2,1)S(1)}, u32[]{:S(2)}, u32[]{:S(2)}) collective-permute-start(bf16[128,1024]{1,0:T(8,128)(2,1)S(1)} %get-tuple-element.105), channel_id=1, source_target_pairs={{0,1},{1,0},{2,3},{3,2},{4,5},{5,4},{6,7},{7,6},{8,9},{9,8},{10,11... | collective-permute-start | bytes 786440 | tf_op jit(solution)/shard_map/ppermute | solution.py:728
  50.8 13.4 %collective-permute-start.4 = (bf16[128,1024]{1,0:T(8,128)(2,1)S(1)}, bf16[128,1024]{1,0:T(8,128)(2,1)S(1)}, u32[]{:S(2)}, u32[]{:S(2)}) collective-permute-start(bf16[128,1024]{1,0:T(8,128)(2,1)S(1)} %add_convert_fusion.4), channel_id=1, source_target_pairs={{0,2},{1,3},{2,0},{3,1},{4,6},{5,7},{6,4},{7,5},{8,10},{9,11},{10,... | collective-permute-start | bytes 786440 | tf_op jit(solution)/shard_map/ppermute | solution.py:728
  50.9 19.5 %collective-permute-start.9 = (bf16[128,1024]{1,0:T(8,128)(2,1)S(1)}, bf16[128,1024]{1,0:T(8,128)(2,1)S(1)}, u32[]{:S(2)}, u32[]{:S(2)}) collective-permute-start(bf16[128,1024]{1,0:T(8,128)(2,1)S(1)} %copy-done.19), channel_id=1, source_target_pairs={{0,1},{1,0},{2,3},{3,2},{4,5},{5,4},{6,7},{7,6},{8,9},{9,8},{10,11... | collective-permute-start | bytes 786440 | tf_op jit(solution)/shard_map/ppermute | solution.py:728
  53.2 24.1 %collective-permute-start.11 = (bf16[128,1024]{1,0:T(8,128)(2,1)S(1)}, bf16[128,1024]{1,0:T(8,128)(2,1)S(1)}, u32[]{:S(2)}, u32[]{:S(2)}) collective-permute-start(bf16[128,1024]{1,0:T(8,128)(2,1)S(1)} %collective-permute-done.10), channel_id=1, source_target_pairs={{0,1},{1,0},{2,3},{3,2},{4,5},{5,4},{6,7},{7,6},{8,9},{9,8},{10,11... | collective-permute-start | bytes 786440 | tf_op jit(solution)/shard_map/ppermute | solution.py:728
  64.6 12.9 %collective-permute-start.7 = (bf16[128,1024]{1,0:T(8,128)(2,1)S(1)}, bf16[128,1024]{1,0:T(8,128)(2,1)S(1)}, u32[]{:S(2)}, u32[]{:S(2)}) collective-permute-start(bf16[128,1024]{1,0:T(8,128)(2,1)S(1)} %multiply_convert_fusion.refs_0_), channel_id=1, source_target_pairs={{0,2},{1,3},{2,0},{3,1},{4,6},{5,7},{6,4},{7,5},{8,10},{9,11},{10,... | collective-permute-start | bytes 786440 | tf_op jit(solution)/shard_map/ppermute | solution.py:728
  100.2 15.4 %collective-permute-start.16 = (bf16[128,1024]{1,0:T(8,128)(2,1)S(1)}, bf16[128,1024]{1,0:T(8,128)(2,1)S(1)}, u32[]{:S(2)}, u32[]{:S(2)}) collective-permute-start(bf16[128,1024]{1,0:T(8,128)(2,1)S(1)} %add_convert_fusion.1), channel_id=1, source_target_pairs={{0,2},{1,3},{2,0},{3,1},{4,6},{5,7},{6,4},{7,5},{8,10},{9,11},{10,... | collective-permute-start | bytes 786440 | tf_op jit(solution)/shard_map/ppermute | solution.py:728
  118.8 47.0 %collective-permute-start.48 = (bf16[768,1024]{1,0:T(8,128)(2,1)S(1)}, bf16[768,1024]{1,0:T(8,128)(2,1)S(1)}, u32[]{:S(2)}, u32[]{:S(2)}) collective-permute-start(bf16[768,1024]{1,0:T(8,128)(2,1)S(1)} %get-tuple-element.173), channel_id=1, source_target_pairs={{0,4},{4,0},{8,12},{12,8},{16,20},{20,16},{24,28},{28,24},{1,5},{5... | collective-permute-start | bytes 4718600 | tf_op jit(solution)/shard_map/ppermute | solution.py:728
  151.4 25.2 %collective-permute-start.37 = (bf16[512,1024]{1,0:T(8,128)(2,1)S(1)}, bf16[512,1024]{1,0:T(8,128)(2,1)S(1)}, u32[]{:S(2)}, u32[]{:S(2)}) collective-permute-start(bf16[512,1024]{1,0:T(8,128)(2,1)S(1)} %get-tuple-element.148), channel_id=1, source_target_pairs={{0,4},{4,0},{8,12},{12,8},{16,20},{20,16},{24,28},{28,24},{1,5},{5... | collective-permute-start | bytes 3145736 | tf_op jit(solution)/shard_map/ppermute | solution.py:728
  152.7 17.9 %collective-permute-start.14 = (bf16[128,1024]{1,0:T(8,128)(2,1)S(1)}, bf16[128,1024]{1,0:T(8,128)(2,1)S(1)}, u32[]{:S(2)}, u32[]{:S(2)}) collective-permute-start(bf16[128,1024]{1,0:T(8,128)(2,1)S(1)} %get-tuple-element.188), channel_id=1, source_target_pairs={{0,1},{1,0},{2,3},{3,2},{4,5},{5,4},{6,7},{7,6},{8,9},{9,8},{10,11... | collective-permute-start | bytes 786440 | tf_op jit(solution)/shard_map/ppermute | solution.py:728
  162.0 13.2 %collective-permute-start.13 = (bf16[128,1024]{1,0:T(8,128)(2,1)S(1)}, bf16[128,1024]{1,0:T(8,128)(2,1)S(1)}, u32[]{:S(2)}, u32[]{:S(2)}) collective-permute-start(bf16[128,1024]{1,0:T(8,128)(2,1)S(1)} %add_convert_fusion.3), channel_id=1, source_target_pairs={{0,2},{1,3},{2,0},{3,1},{4,6},{5,7},{6,4},{7,5},{8,10},{9,11},{10,... | collective-permute-start | bytes 786440 | tf_op jit(solution)/shard_map/ppermute | solution.py:728
  164.3 13.8 %collective-permute-start.25 = (bf16[128,896]{1,0:T(8,128)(2,1)S(1)}, bf16[128,896]{1,0:T(8,128)(2,1)S(1)}, u32[]{:S(2)}, u32[]{:S(2)}) collective-permute-start(bf16[128,896]{1,0:T(8,128)(2,1)S(1)} %get-tuple-element.138), channel_id=1, source_target_pairs={{0,8},{4,12},{8,0},{12,4},{16,24},{20,28},{24,16},{28,20},{1,9},{5... | collective-permute-start | bytes 688136 | tf_op jit(solution)/shard_map/ppermute | solution.py:728
  165.8 13.8 %collective-permute-start.26 = (bf16[128,896]{1,0:T(8,128)(2,1)S(1)}, bf16[128,896]{1,0:T(8,128)(2,1)S(1)}, u32[]{:S(2)}, u32[]{:S(2)}) collective-permute-start(bf16[128,896]{1,0:T(8,128)(2,1)S(1)} %get-tuple-element.139), channel_id=1, source_target_pairs={{0,16},{4,20},{8,24},{12,28},{16,0},{20,4},{24,8},{28,12},{1,17},{... | collective-permute-start | bytes 688136 | tf_op jit(solution)/shard_map/ppermute | solution.py:728
  170.6 26.1 %collective-permute-start.49 = (bf16[192,1024]{1,0:T(8,128)(2,1)S(1)}, bf16[192,1024]{1,0:T(8,128)(2,1)S(1)}, u32[]{:S(2)}, u32[]{:S(2)}) collective-permute-start(bf16[192,1024]{1,0:T(8,128)(2,1)S(1)} %get-tuple-element.175), channel_id=1, source_target_pairs={{0,8},{4,12},{8,0},{12,4},{16,24},{20,28},{24,16},{28,20},{1,9},{5... | collective-permute-start | bytes 1179656 | tf_op jit(solution)/shard_map/ppermute | solution.py:728
  175.1 23.2 %collective-permute-start.50 = (bf16[192,1024]{1,0:T(8,128)(2,1)S(1)}, bf16[192,1024]{1,0:T(8,128)(2,1)S(1)}, u32[]{:S(2)}, u32[]{:S(2)}) collective-permute-start(bf16[192,1024]{1,0:T(8,128)(2,1)S(1)} %get-tuple-element.176), channel_id=1, source_target_pairs={{0,16},{4,20},{8,24},{12,28},{16,0},{20,4},{24,8},{28,12},{1,17},{... | collective-permute-start | bytes 1179656 | tf_op jit(solution)/shard_map/ppermute | solution.py:728
  176.7 23.6 %collective-permute-start.51 = (bf16[192,1024]{1,0:T(8,128)(2,1)S(1)}, bf16[192,1024]{1,0:T(8,128)(2,1)S(1)}, u32[]{:S(2)}, u32[]{:S(2)}) collective-permute-start(bf16[192,1024]{1,0:T(8,128)(2,1)S(1)} %get-tuple-element.177), channel_id=1, source_target_pairs={{0,24},{4,28},{8,16},{12,20},{16,8},{20,12},{24,0},{28,4},{1,25},{... | collective-permute-start | bytes 1179656 | tf_op jit(solution)/shard_map/ppermute | solution.py:728
  178.1 17.1 %collective-permute-start.27 = (bf16[128,896]{1,0:T(8,128)(2,1)S(1)}, bf16[128,896]{1,0:T(8,128)(2,1)S(1)}, u32[]{:S(2)}, u32[]{:S(2)}) collective-permute-start(bf16[128,896]{1,0:T(8,128)(2,1)S(1)} %get-tuple-element.140), channel_id=1, source_target_pairs={{0,24},{4,28},{8,16},{12,20},{16,8},{20,12},{24,0},{28,4},{1,25},{... | collective-permute-start | bytes 688136 | tf_op jit(solution)/shard_map/ppermute | solution.py:728
  179.6 21.9 %collective-permute-start.21 = (bf16[128,1024]{1,0:T(8,128)(2,1)S(1)}, bf16[128,1024]{1,0:T(8,128)(2,1)S(1)}, u32[]{:S(2)}, u32[]{:S(2)}) collective-permute-start(bf16[128,1024]{1,0:T(8,128)(2,1)S(1)} %get-tuple-element.133), channel_id=1, source_target_pairs={{0,1},{1,0},{2,3},{3,2},{4,5},{5,4},{6,7},{7,6},{8,9},{9,8},{10,11... | collective-permute-start | bytes 786440 | tf_op jit(solution)/shard_map/ppermute | solution.py:728
  201.5 20.2 %collective-permute-start.52 = (bf16[192,1024]{1,0:T(8,128)(2,1)S(1)}, bf16[192,1024]{1,0:T(8,128)(2,1)S(1)}, u32[]{:S(2)}, u32[]{:S(2)}) collective-permute-start(bf16[192,1024]{1,0:T(8,128)(2,1)S(1)} %shard_map.421.refs_0_), channel_id=1, source_target_pairs={{0,8},{4,12},{8,0},{12,4},{16,24},{20,28},{24,16},{28,20},{1,9},{5... | collective-permute-start | bytes 1179656 | tf_op jit(solution)/shard_map/ppermute | solution.py:728
  203.9 30.0 %collective-permute-start.53 = (bf16[192,1024]{1,0:T(8,128)(2,1)S(1)}, bf16[192,1024]{1,0:T(8,128)(2,1)S(1)}, u32[]{:S(2)}, u32[]{:S(2)}) collective-permute-start(bf16[192,1024]{1,0:T(8,128)(2,1)S(1)} %shard_map.421.refs_0_), channel_id=1, source_target_pairs={{0,16},{4,20},{8,24},{12,28},{16,0},{20,4},{24,8},{28,12},{1,17},{... | collective-permute-start | bytes 1179656 | tf_op jit(solution)/shard_map/ppermute | solution.py:728
  204.6 15.7 %collective-permute-start.40 = (bf16[128,1024]{1,0:T(8,128)(2,1)S(1)}, bf16[128,1024]{1,0:T(8,128)(2,1)S(1)}, u32[]{:S(2)}, u32[]{:S(2)}) collective-permute-start(bf16[128,1024]{1,0:T(8,128)(2,1)S(1)} %get-tuple-element.152), channel_id=1, source_target_pairs={{0,24},{4,28},{8,16},{12,20},{16,8},{20,12},{24,0},{28,4},{1,25},{... | collective-permute-start | bytes 786440 | tf_op jit(solution)/shard_map/ppermute | solution.py:728
  206.8 27.7 %collective-permute-start.54 = (bf16[192,1024]{1,0:T(8,128)(2,1)S(1)}, bf16[192,1024]{1,0:T(8,128)(2,1)S(1)}, u32[]{:S(2)}, u32[]{:S(2)}) collective-permute-start(bf16[192,1024]{1,0:T(8,128)(2,1)S(1)} %shard_map.421.refs_0_), channel_id=1, source_target_pairs={{0,24},{4,28},{8,16},{12,20},{16,8},{20,12},{24,0},{28,4},{1,25},{... | collective-permute-start | bytes 1179656 | tf_op jit(solution)/shard_map/ppermute | solution.py:728
  210.3 24.3 %collective-permute-start.55 = (bf16[192,1024]{1,0:T(8,128)(2,1)S(1)}, bf16[192,1024]{1,0:T(8,128)(2,1)S(1)}, u32[]{:S(2)}, u32[]{:S(2)}) collective-permute-start(bf16[192,1024]{1,0:T(8,128)(2,1)S(1)} %shard_map.421.refs_0_), channel_id=1, source_target_pairs={{0,4},{4,0},{8,12},{12,8},{16,20},{20,16},{24,28},{28,24},{1,5},{5... | collective-permute-start | bytes 1179656 | tf_op jit(solution)/shard_map/ppermute | solution.py:728
  220.3 13.5 %collective-permute-start.29 = (bf16[128,512]{1,0:T(8,128)(2,1)S(1)}, bf16[128,512]{1,0:T(8,128)(2,1)S(1)}, u32[]{:S(2)}, u32[]{:S(2)}) collective-permute-start(bf16[128,512]{1,0:T(8,128)(2,1)S(1)} %add.80.sum_ref), channel_id=1, source_target_pairs={{0,2},{1,3},{2,0},{3,1},{4,6},{5,7},{6,4},{7,5},{8,10},{9,11},{10,... | collective-permute-start | bytes 393224 | tf_op jit(solution)/shard_map/ppermute | solution.py:728
  221.8 16.4 %collective-permute-start.41 = (bf16[128,1024]{1,0:T(8,128)(2,1)S(1)}, bf16[128,1024]{1,0:T(8,128)(2,1)S(1)}, u32[]{:S(2)}, u32[]{:S(2)}) collective-permute-start(bf16[128,1024]{1,0:T(8,128)(2,1)S(1)} %shard_map.417.refs_0_), channel_id=1, source_target_pairs={{0,8},{4,12},{8,0},{12,4},{16,24},{20,28},{24,16},{28,20},{1,9},{5... | collective-permute-start | bytes 786440 | tf_op jit(solution)/shard_map/ppermute | solution.py:728
  234.6 14.9 %collective-permute-start.31 = (bf16[128,1024]{1,0:T(8,128)(2,1)S(1)}, bf16[128,1024]{1,0:T(8,128)(2,1)S(1)}, u32[]{:S(2)}, u32[]{:S(2)}) collective-permute-start(bf16[128,1024]{1,0:T(8,128)(2,1)S(1)} %shard_map.413.refs_0_), channel_id=1, source_target_pairs={{0,8},{4,12},{8,0},{12,4},{16,24},{20,28},{24,16},{28,20},{1,9},{5... | collective-permute-start | bytes 786440 | tf_op jit(solution)/shard_map/ppermute | solution.py:728
  238.1 16.9 %collective-permute-start.56 = (bf16[192,1024]{1,0:T(8,128)(2,1)S(1)}, bf16[192,1024]{1,0:T(8,128)(2,1)S(1)}, u32[]{:S(2)}, u32[]{:S(2)}) collective-permute-start(bf16[192,1024]{1,0:T(8,128)(2,1)S(1)} %collective-permute-done.52.refs_1_), channel_id=1, source_target_pairs={{0,4},{4,0},{8,12},{12,8},{16,20},{20,16},{24,28},{28,24},{1,5},{5... | collective-permute-start | bytes 1179656 | tf_op jit(solution)/shard_map/ppermute | solution.py:728
  255.2 12.8 %collective-permute-start.22 = (bf16[128,1024]{1,0:T(8,128)(2,1)S(1)}, bf16[128,1024]{1,0:T(8,128)(2,1)S(1)}, u32[]{:S(2)}, u32[]{:S(2)}) collective-permute-start(bf16[128,1024]{1,0:T(8,128)(2,1)S(1)} %add_convert_fusion), channel_id=1, source_target_pairs={{0,2},{1,3},{2,0},{3,1},{4,6},{5,7},{6,4},{7,5},{8,10},{9,11},{10,... | collective-permute-start | bytes 786440 | tf_op jit(solution)/shard_map/ppermute | solution.py:728
  255.3 12.7 %collective-permute-start.30 = (bf16[128,1024]{1,0:T(8,128)(2,1)S(1)}, bf16[128,1024]{1,0:T(8,128)(2,1)S(1)}, u32[]{:S(2)}, u32[]{:S(2)}) collective-permute-start(bf16[128,1024]{1,0:T(8,128)(2,1)S(1)} %shard_map.413.refs_0_), channel_id=1, source_target_pairs={{0,4},{4,0},{8,12},{12,8},{16,20},{20,16},{24,28},{28,24},{1,5},{5... | collective-permute-start | bytes 786440 | tf_op jit(solution)/shard_map/ppermute | solution.py:728
  (48 other events, 565.9 us)

commit v2 on v1

--- a/solution.py
+++ b/solution.py
@@ -12,6 +12,7 @@
 KVH = 2
 HD = 64
 LANES = 128
+BLOCKS = 4
 
 eps = 1e-05
 big_negative = -1e30
@@ -64,11 +65,71 @@
     return jnp.where(lanes < HD, first, second)
 
 
+def masks_body(taps_count, t_ref, seg_ref, mask_ref, tri_ref, link_ref):
+    length = mask_ref.shape[0]
+    seg_row = seg_ref[0:1, :].astype(f32)
+    seg_col = jnp.broadcast_to(seg_row, (LANES, length)).T
+    row_pos = lax.broadcasted_iota(jnp.int32, (length, length), 0)
+    col_pos = lax.broadcasted_iota(jnp.int32, (length, length), 1)
+    allowed = (row_pos >= col_pos) & (seg_col[:, 0:1] == seg_row)
+    mask_ref[...] = jnp.where(allowed, 0.0, big_negative)
+    tri_ref[...] = (row_pos >= col_pos).astype(f32).astype(bf16)
+    spots = lax.broadcasted_iota(jnp.int32, (length, LANES), 0)
+    for shift_by in range(1, taps_count):
+        linked = (pltpu.roll(seg_col, shift_by, 0) == seg_col) & (spots >= shift_by)
+        link_ref[shift_by - 1] = jnp.where(linked, 1.0, 0.0)
+
+
+def ahead_body(
+    widths, taps_count, heads, t_ref, mask_ref, link_ref, qkv_ref, stat_ref, u_ref, acc_ref,
+    g_ref, run_ref, run_t_ref, dt_ref,
+    probs_ref, weight_ref, mixing_ref, slope_ref, xc_ref, ub_ref, moved_ref, linked_ref,
+):
+    wq, _, _, _, _, _ = widths
+    length = acc_ref.shape[0]
+    lanes = lane_ids(length, LANES)
+    lane_lo = lanes < HD
+    half = length // BLOCKS
+    scale = HD ** (-0.5)
+    keys2 = qkv_ref[:, wq : wq + LANES]
+    for head in range(2):
+        keep = lane_lo if head == 0 else ~lane_lo
+        q_m = jnp.where(keep, qkv_ref[:, 0:wq].astype(f32), 0.0).astype(bf16)
+        logsum = stat_ref[:, head * HD : head * HD + 1]
+        for block in range(BLOCKS):
+            lo, hi = block * half, (block + 1) * half
+            scores = dot_t(q_m[lo:hi], keys2[:hi]) * scale + mask_ref[lo:hi, 0:hi]
+            probs_ref[head, lo:hi, 0:hi] = jnp.exp(scores - logsum[lo:hi])
+    run = run_ref[...]
+    run_t = run_t_ref[...]
+    for head in range(heads):
+        for block in range(BLOCKS):
+            lo, hi = block * half, (block + 1) * half
+            spread = run[lo:hi, head : head + 1] - run_t[head : head + 1, 0:hi]
+            weight = jnp.exp(spread + mask_ref[lo:hi, 0:hi])
+            weight_ref[head, lo:hi, 0:hi] = weight
+            mixing_ref[head, lo:hi, 0:hi] = (weight * g_ref[lo:hi, 0:hi]).astype(bf16)
+    acc = acc_ref[...]
+    sig = sigmoid(acc)
+    slope_ref[...] = sig * (1.0 + acc * (1.0 - sig))
+    for pair in range(heads // 2):
+        cols = slice(pair * LANES, (pair + 1) * LANES)
+        xc = acc[:, cols] * sig[:, cols]
+        xc_ref[:, cols] = xc
+        ub_ref[:, cols] = (xc * pair_columns(dt_ref[...], pair, lanes)).astype(bf16)
+    u = u_ref[...]
+    for shift_by in range(1, taps_count):
+        moved_ref[shift_by - 1] = link_ref[shift_by - 1, :, 0:1] * pltpu.roll(u, shift_by, 0)
+    linked_ref[...] = jnp.where(mask_ref[...] == 0.0, 1.0, 0.0).astype(bf16)
+
+
 def fwd_body(widths, taps_count, heads, tensor, *refs):
     (t_ref,) = refs[:1]
     parts = refs[1 : 1 + tensor]
     (
-        seg_ref,
+        mask_ref,
+        tri_ref,
+        link_ref,
         gain_ref,
         query_w_ref,
         kv_w_ref,
@@ -93,15 +154,14 @@
         ysum_ref,
         gated_ref,
         raw_ref,
-        mask_ref,
         g_ref,
         run_ref,
         run_t_ref,
         dt_ref,
-        link_ref,
         *mixed_refs,
         mixed_ref,
         query_v,
+        state_v,
         att_v,
         mam_v,
         sems,
@@ -110,6 +170,7 @@
     copies = Copies(sems)
     for source, target in (
         (query_w_ref, query_v),
+        (state_w_ref, state_v),
         (att_w_ref, att_v),
         (mam_w_ref, mam_v),
     ):
@@ -123,12 +184,6 @@
         normed = (xf * rms_recip(xf) * gain_ref[...]).astype(bf16)
         n1_ref[pl.ds(pl.multiple_of((t ^ k) * rows, rows), rows), :] = normed
     n1 = n1_ref[...]
-    seg_row = seg_ref[0:1, :].astype(f32)
-    seg_col = jnp.broadcast_to(seg_row, (LANES, length)).T
-    row_pos = lax.broadcasted_iota(jnp.int32, (length, length), 0)
-    col_pos = lax.broadcasted_iota(jnp.int32, (length, length), 1)
-    allowed = (row_pos >= col_pos) & (seg_col[:, 0:1] == seg_row)
-    mask_ref[...] = jnp.where(allowed, 0.0, big_negative)
     copies.wait(0, 1)
     query = dot(n1, query_v[...]).astype(bf16)
     kv = dot(n1, kv_w_ref[...])
@@ -141,14 +196,15 @@
     qkv_ref[:, wq + LANES :] = values2
     z_ref[...] = dot(n1, gate_w_ref[...])
     u_ref[:, :wx] = dot(n1, input_w_ref[...])
-    u_ref[:, wx:] = dot(n1, state_w_ref[...])
+    copies.wait(1, 2)
+    u_ref[:, wx:] = dot(n1, state_v[...])
     raw = dot_t(n1, step_w_ref[...]) + bias_ref[...]
     raw_ref[...] = raw
 
     lane_lo = lanes < HD
     scale = HD ** (-0.5)
-    half = length // 2
-    for block in range(2):
+    half = length // BLOCKS
+    for block in range(BLOCKS):
         lo, hi = block * half, (block + 1) * half
         out = jnp.zeros((half, LANES), f32)
         stats = []
@@ -169,19 +225,14 @@
 
     u = u_ref[...]
     acc = offs_ref[...] + taps_ref[0:1, :] * u
-    spots = lax.broadcasted_iota(jnp.int32, (length, LANES), 0)
     for shift_by in range(1, taps_count):
-        linked = (pltpu.roll(seg_col, shift_by, 0) == seg_col) & (spots >= shift_by)
-        linked = jnp.where(linked, 1.0, 0.0)
-        link_ref[shift_by - 1] = linked
         acc = acc + taps_ref[shift_by : shift_by + 1, :] * (
-            linked[:, 0:1] * pltpu.roll(u, shift_by, 0)
+            link_ref[shift_by - 1, :, 0:1] * pltpu.roll(u, shift_by, 0)
         )
     acc_ref[...] = acc
 
     dt = jnp.maximum(raw, 0.0) + jnp.log1p(jnp.exp(-jnp.abs(raw)))
-    tri = (row_pos >= col_pos).astype(f32).astype(bf16)
-    run = exact_left(tri, dt * nega_ref[...])
+    run = exact_left(tri_ref[...], dt * nega_ref[...])
     run_t = run.T
     dt_ref[...] = dt
     run_ref[...] = run
@@ -196,7 +247,7 @@
         uu = xc * pair_columns(dt, pair, lanes)
         u_lo = jnp.where(lane_lo, uu, 0.0).astype(bf16)
         u_hi = jnp.where(lane_lo, 0.0, uu).astype(bf16)
-        for block in range(2):
+        for block in range(BLOCKS):
             lo, hi = block * half, (block + 1) * half
             total = jnp.zeros((half, LANES), f32)
             for side, masked in ((0, u_lo), (1, u_hi)):
@@ -209,7 +260,7 @@
         y = ysum_ref[:, cols] + skip_ref[0:1, cols] * xc
         z = z_ref[:, cols]
         gated_ref[:, cols] = (y * z * sigmoid(z)).astype(bf16)
-    copies.wait(1)
+    copies.wait(2)
     mixed = dot(att_ref[...], att_v[...]) + dot(gated_ref[...], mam_v[...])
     mixed_ref[...] = mixed.astype(bf16)
     for k in range(tensor):
@@ -223,12 +274,11 @@
         skip_ref,
         att_w_ref,
         mam_w_ref,
-        mask_ref,
+        probs_ref,
+        xc_ref,
         qkv_ref,
         att_ref,
-        stat_ref,
         z_ref,
-        acc_ref,
         ysum_ref,
         gated_ref,
         n1_ref,
@@ -246,7 +296,7 @@
         dmixed_ref[pl.ds(pl.multiple_of((t ^ k) * rows, rows), rows), :] = dparts[k][...]
     dmixed = dmixed_ref[...]
     lane_lo = lane_ids(length, LANES) < HD
-    half = length // 2
+    half = length // BLOCKS
     scale = HD ** (-0.5)
 
     datt = dot_t(dmixed, att_w_ref[...]).astype(bf16)
@@ -255,21 +305,18 @@
     query = qkv_ref[:, 0:wq]
     keys2 = qkv_ref[:, wq : wq + LANES]
     values2 = qkv_ref[:, wq + LANES :]
-    stat = stat_ref[...]
-    dq = [jnp.zeros((half, LANES), f32) for _ in range(2)]
-    dk = [jnp.zeros((half, LANES), f32) for _ in range(2)]
-    dv = [jnp.zeros((half, LANES), f32) for _ in range(2)]
+    dq = [jnp.zeros((half, LANES), f32) for _ in range(BLOCKS)]
+    dk = [jnp.zeros((half, LANES), f32) for _ in range(BLOCKS)]
+    dv = [jnp.zeros((half, LANES), f32) for _ in range(BLOCKS)]
     for head in range(2):
         keep = lane_lo if head == 0 else ~lane_lo
         q_m = jnp.where(keep, query.astype(f32), 0.0).astype(bf16)
         k_m = jnp.where(keep, keys2.astype(f32), 0.0).astype(bf16)
         d_m = jnp.where(keep, datt_f, 0.0).astype(bf16)
         delta = jnp.sum(jnp.where(keep, prod, 0.0), axis=-1, keepdims=True)
-        logsum = stat[:, head * HD : head * HD + 1]
-        for block in range(2):
+        for block in range(BLOCKS):
             lo, hi = block * half, (block + 1) * half
-            scores = dot_t(q_m[lo:hi], keys2[:hi]) * scale + mask_ref[lo:hi, 0:hi]
-            probs = jnp.exp(scores - logsum[lo:hi])
+            probs = probs_ref[head, lo:hi, 0:hi]
             dprob = dot_t(d_m[lo:hi], values2[:hi])
             dscore = (probs * (dprob - delta[lo:hi]) * scale).astype(bf16)
             dq[block] = dq[block] + dot(dscore, k_m[:hi])
@@ -278,7 +325,7 @@
             for part in range(block + 1):
                 dk[part] = dk[part] + dk_add[part * half : (part + 1) * half]
                 dv[part] = dv[part] + dv_add[part * half : (part + 1) * half]
-    for block in range(2):
+    for block in range(BLOCKS):
         lo, hi = block * half, (block + 1) * half
         d_ref[lo:hi, 0:wq] = dq[block].astype(bf16)
         dk_sum = dk[block] + pltpu.roll(dk[block], HD, 1)
@@ -288,8 +335,7 @@
     base = wq + wkv
     for pair in range(heads // 2):
         cols = slice(pair * LANES, (pair + 1) * LANES)
-        xa = acc_ref[:, cols]
-        xc = xa * sigmoid(xa)
+        xc = xc_ref[:, cols]
         z = z_ref[:, cols]
         zs = sigmoid(z)
         dgated = dot_t(dmixed, mam_w_ref[cols, :])
@@ -318,10 +364,13 @@
         taps_ref,
         nega_ref,
         skip_ref,
-        mask_ref,
-        g_ref,
-        run_ref,
-        run_t_ref,
+        weight_ref,
+        mixing_ref,
+        slope_ref,
+        xc_ref,
+        ub_ref,
+        moved_ref,
+        linked_ref,
         dt_ref,
         link_ref,
         n1_ref,
@@ -332,7 +381,7 @@
         d1_ref,
         dssm_ref,
         gfeed_ref,
-    ) = refs[:25]
+    ) = refs[:28]
     (
         keep_ref,
         send_ref,
@@ -343,7 +392,7 @@
         dg_ref,
         dact_ref,
         rows_ref,
-    ) = refs[25:]
+    ) = refs[28:]
     wq, wkv, _, wx, wbc, _ = widths
     t = t_ref[0]
     length = n1_ref.shape[0]
@@ -351,13 +400,11 @@
     state = wbc // 2
     lanes = lane_ids(length, LANES)
     lane_lo = lanes < HD
-    half = length // 2
+    half = length // BLOCKS
 
     raw = raw_ref[...]
     dt = dt_ref[...]
     ld = dt * nega_ref[...]
-    run = run_ref[...]
-    run_t = run_t_ref[...]
     bc_acc = acc_ref[:, wx:]
     bc = (bc_acc * sigmoid(bc_acc)).astype(bf16)
     dg_ref[...] = jnp.zeros((length, length), f32)
@@ -367,8 +414,7 @@
     small_ref[...] = jnp.zeros(small_ref.shape, f32)
     for pair in range(heads // 2):
         cols = slice(pair * LANES, (pair + 1) * LANES)
-        xa = acc_ref[:, cols]
-        xc = xa * sigmoid(xa)
+        xc = xc_ref[:, cols]
         skip = skip_ref[0:1, cols]
         ysum = ysum_ref[:, cols]
         dssm = dssm_ref[:, cols]
@@ -378,20 +424,19 @@
             head_sum = jnp.sum(jnp.where(keep, dskip, 0.0), axis=-1, keepdims=True)
             skip_row = jnp.where(lanes[0:1] == 2 * pair + side, head_sum, skip_row)
         dt_pair = pair_columns(dt, pair, lanes)
-        u_b = (xc * dt_pair).astype(bf16)
+        u_b = ub_ref[:, cols]
         dy_b = dssm.astype(bf16)
         u_f = u_b.astype(f32)
         dy_f = dy_b.astype(f32)
-        du = [jnp.zeros((half, LANES), f32) for _ in range(2)]
+        du = [jnp.zeros((half, LANES), f32) for _ in range(BLOCKS)]
         for side in range(2):
             head = 2 * pair + side
             keep = lane_lo if side == 0 else ~lane_lo
             dy_m = jnp.where(keep, dy_f, 0.0).astype(bf16)
-            for block in range(2):
+            for block in range(BLOCKS):
                 lo, hi = block * half, (block + 1) * half
-                spread = run[lo:hi, head : head + 1] - run_t[head : head + 1, 0:hi]
-                weight = jnp.exp(spread + mask_ref[lo:hi, 0:hi])
-                mixing = (weight * g_ref[lo:hi, 0:hi]).astype(bf16)
+                weight = weight_ref[head, lo:hi, 0:hi]
+                mixing = mixing_ref[head, lo:hi, 0:hi]
                 dmix = dot_t(dy_m[lo:hi], u_b[:hi])
                 dg_ref[lo:hi, 0:hi] += weight * dmix
                 du_add = tdot(mixing, dy_m[lo:hi])
@@ -414,16 +459,14 @@
     dg = dg_ref[...].astype(bf16)
     dact_ref[:, wx : wx + state] = tdot(dg, bc[:, state:])
     dact_ref[:, wx + state :] = dot(dg, bc[:, :state])
-    linked = jnp.where(mask_ref[...] == 0.0, 1.0, 0.0).astype(bf16)
+    linked = linked_ref[...]
     high, mid, low = split3(drun)
     dld = tdot(linked, high) + (tdot(linked, mid) + tdot(linked, low))
     ddt = ddt + dld * nega_ref[...]
     dstep = ddt * sigmoid(raw)
     d2_ref[:, wx + wbc :] = dstep.astype(bf16)
 
-    acc = acc_ref[...]
-    sig = sigmoid(acc)
-    dconv = dact_ref[...] * sig * (1.0 + acc * (1.0 - sig))
+    dconv = dact_ref[...] * slope_ref[...]
     u = u_ref[...]
     small_ref[0:1, :] = jnp.sum(dconv * u, axis=0, keepdims=True)
     small_ref[taps_count : taps_count + 1, :] = jnp.sum(dconv, axis=0, keepdims=True)
@@ -431,7 +474,7 @@
     for shift_by in range(1, taps_count):
         masked = dconv * link_ref[shift_by - 1, :, 0:1]
         small_ref[shift_by : shift_by + 1, :] = jnp.sum(
-            masked * pltpu.roll(u, shift_by, 0), axis=0, keepdims=True
+            dconv * moved_ref[shift_by - 1], axis=0, keepdims=True
         )
         du_in = du_in + taps_ref[shift_by : shift_by + 1, :] * pltpu.roll(
             masked, length - shift_by, 0
@@ -455,13 +498,13 @@
     )
 
 
-def feed_body(tensor, *refs):
-    parts = refs[:tensor]
-    dhidden_ref, gate_ref, up_ref, n2_ref, hidden_ref, dgu_ref = refs[tensor : tensor + 6]
-    dn2_refs = refs[tensor + 6 :]
+def feed_body(count, *refs):
+    parts = refs[:count]
+    dhidden_ref, gate_ref, up_ref, n2_ref, hidden_ref, dgu_ref = refs[count : count + 6]
+    dn2_refs = refs[count + 6 :]
     rows = parts[0].shape[0]
     units = gate_ref.shape[1]
-    for k in range(tensor):
+    for k in range(count):
         n2_ref[k * rows : (k + 1) * rows, :] = parts[k][...]
     n2 = n2_ref[...]
     gate_pre = dot(n2, gate_ref[...])
@@ -472,7 +515,7 @@
     dgate = (dhidden * up_pre * gsig * (1.0 + gate_pre * (1.0 - gsig))).astype(bf16)
     dup = (dhidden * gate_act).astype(bf16)
     dn2 = (dot_t(dgate, gate_ref[...]) + dot_t(dup, up_ref[...])).astype(bf16)
-    for k in range(tensor):
+    for k in range(count):
         dn2_refs[k][...] = dn2[k * rows : (k + 1) * rows]
     hidden_ref[...] = (gate_act * up_pre).astype(bf16)
     dgu_ref[:, :units] = dgate
@@ -486,20 +529,24 @@
     send_ref[at : at + size, :] = jnp.where(low, second, first).astype(bf16)
 
 
-def feed_grads_body(groups, u_ref, n2_ref, dgu_ref, hidden_ref, cot_ref, keep_ref, send_ref):
-    upper = u_ref[1] % 2
-    dgu = dgu_ref[...]
-    cot = cot_ref[...]
-    half_wide = n2_ref.shape[1] // 2
-    half_tall = hidden_ref.shape[1] // 2
+def feed_grads_body(groups, u_ref, *refs):
+    n2_refs, dgu_refs, hidden_refs, cot_refs = refs[0:2], refs[2:4], refs[4:6], refs[6:8]
+    keep_ref, send_ref = refs[8:]
+    half_wide = n2_refs[0].shape[1] // 2
+    half_tall = hidden_refs[0].shape[1] // 2
     wide, tall = half_wide // groups, half_tall // groups
-    low = upper == 0
-    for source, other, half, size, skip in (
-        (n2_ref, dgu, half_wide, wide, 0),
-        (hidden_ref, cot, half_tall, tall, wide),
+    low = u_ref[1] % 2 == 0
+    for sources, others, half, size, skip in (
+        (n2_refs, dgu_refs, half_wide, wide, 0),
+        (hidden_refs, cot_refs, half_tall, tall, wide),
     ):
-        first = tdot(source[:, :half], other)
-        second = tdot(source[:, half:], other)
+        first, second = (
+            sum(
+                tdot(source[:, side * half : (side + 1) * half], other[...])
+                for source, other in zip(sources, others)
+            )
+            for side in range(2)
+        )
         keep = jnp.where(low, first, second).astype(bf16)
         send = jnp.where(low, second, first).astype(bf16)
         for q in range(groups):
@@ -701,7 +748,7 @@
         scratch_shapes=[
             shape if kind is None else pltpu.VMEM(shape, kind) for shape, kind in scratch
         ],
-        compiler_params=pltpu.CompilerParams(vmem_limit_bytes=24 * 1024 * 1024),
+        compiler_params=pltpu.CompilerParams(vmem_limit_bytes=16 * 1024 * 1024),
     )(scalar, *placed)
 
 
@@ -851,16 +898,22 @@
     bias = jnp.pad(step_bias, (0, LANES - heads))[None, :]
     nega = jnp.pad(-jnp.exp(decay_log), (0, LANES - heads))[None, :]
     skip = jnp.repeat(skip_gain, wx // heads)[None, :]
-    seg_row = segments[None, :]
+    square = ((length, length), f32)
+    wide_bits = ((length, length), bf16)
+    mask, tri, link = call_kernel(
+        functools.partial(masks_body, kc),
+        t_array,
+        (segments[None, :],),
+        [square, wide_bits, ((kc - 1, length, LANES), f32)],
+    )
     gain1 = mixers_norm_gain[None, :]
 
     full = (length, width)
     blocks = [((rows, width), bf16)] * tensor
-    square = ((length, length), f32)
     (n1, qkv, att, stat, z, u, acc, ysum, gated, raw, *held) = call_kernel(
         functools.partial(fwd_body, widths, kc, heads, tensor),
         t_array,
-        (*parts, seg_row, gain1, *weights, taps, offs, bias, nega, skip, attention_out, mamba_out),
+        (*parts, mask, tri, link, gain1, *weights, taps, offs, bias, nega, skip, attention_out, mamba_out),
         [
             (full, bf16),
             ((length, wq + 2 * LANES), bf16),
@@ -873,23 +926,37 @@
             ((length, wx), bf16),
             ((length, wst), f32),
             square,
-            square,
             ((length, wst), f32),
             ((wst, length), f32),
             ((length, wst), f32),
-            ((kc - 1, length, LANES), f32),
             *blocks,
         ],
         [
             (full, bf16),
             (query_weight.shape, bf16),
+            (state_weight.shape, bf16),
             (attention_out.shape, bf16),
             (mamba_out.shape, bf16),
-            (pltpu.SemaphoreType.DMA((3,)), None),
+            (pltpu.SemaphoreType.DMA((4,)), None),
         ],
-        far=(tensor + 2, tensor + 13, tensor + 14),
-    )
-    mask, g, run, run_t, dt, link, *mixed_blocks = held
+        far=(tensor + 4, tensor + 8, tensor + 15, tensor + 16),
+    )
+    g, run, run_t, dt, *mixed_blocks = held
+    probs, weight, mixing, slope, xc, ub, moved, linked = call_kernel(
+        functools.partial(ahead_body, widths, kc, heads),
+        t_array,
+        (mask, link, qkv, stat, u, acc, g, run, run_t, dt),
+        [
+            ((2, length, length), f32),
+            ((heads, length, length), f32),
+            ((heads, length, length), bf16),
+            ((length, wx + wbc), f32),
+            ((length, wx), f32),
+            ((length, wx), bf16),
+            ((kc - 1, length, wx + wbc), f32),
+            wide_bits,
+        ],
+    )
 
     inputs_float = inputs.astype(f32)
     hidden_first = inputs_float + scatter_parts(mixed_blocks, tensor)
@@ -898,14 +965,27 @@
     local_normed_second = (unit_second * feedforward_norm_gain[None, :]).astype(bf16)
     n2_parts = gather_parts(local_normed_second, tensor)
 
-    cot_rows = jnp.concatenate(cot_parts, 0)
-    dhidden = dot_t(cot_rows, down_weight)
-    n2, hidden, dgu, *dn2_blocks = call_kernel(
-        lambda scalar, *refs: feed_body(tensor, *refs),
-        t_array,
-        (*n2_parts, dhidden, gate_weight, up_weight),
-        [(full, bf16), ((length, units), bf16), ((length, 2 * units), bf16), *blocks],
-    )
+    stages = (range(tensor - 1), range(tensor - 1, tensor))
+    cots = [jnp.concatenate([cot_parts[k] for k in stage], 0) for stage in stages]
+    n2s, hiddens, dgus, dn2_blocks = [], [], [], []
+    for at, stage in enumerate(stages):
+        dhidden = dot_t(cots[at], down_weight)
+        span = rows * len(stage)
+        n2, hidden, dgu, *dn2_stage = call_kernel(
+            lambda scalar, *refs, count=len(stage): feed_body(count, *refs),
+            t_array,
+            (*[n2_parts[k] for k in stage], dhidden, gate_weight, up_weight),
+            [
+                ((span, width), bf16),
+                ((span, units), bf16),
+                ((span, 2 * units), bf16),
+                *blocks[: len(stage)],
+            ],
+        )
+        n2s.append(n2)
+        hiddens.append(hidden)
+        dgus.append(dgu)
+        dn2_blocks.extend(dn2_stage)
     dn2 = scatter_parts(dn2_blocks, tensor)
     scaled_second = dn2 * feedforward_norm_gain[None, :]
     grad_hidden = cotangent.astype(f32) + reciprocal_second * (
@@ -918,7 +998,7 @@
     feed_keep, feed_send = call_kernel(
         functools.partial(feed_grads_body, dp // 2),
         t_array,
-        (n2, dgu, hidden, cot_rows),
+        (*n2s, *dgus, *hiddens, *cots),
         [((span, width), bf16)] * 2,
     )
     feed_sum = sum_over_dp(feed_keep, feed_send, dp, t_array)
@@ -928,8 +1008,8 @@
         functools.partial(attention_bwd_body, widths, heads, tensor),
         t_array,
         (
-            *dparts, skip, attention_out, mamba_out, mask,
-            qkv, att, stat, z, acc, ysum, gated, n1,
+            *dparts, skip, attention_out, mamba_out, probs, xc,
+            qkv, att, z, ysum, gated, n1,
         ),
         [
             ((length, wq + wkv + wx), bf16),
@@ -941,8 +1021,10 @@
     )
     mid_sum = sum_over_dp(mid_keep, mid_send, dp, t_array)
 
-    feed_part = dot(hidden, down_weight).astype(bf16)
-    feed_blocks = [feed_part[k * rows : (k + 1) * rows] for k in range(tensor)]
+    feed_blocks = []
+    for hidden, stage in zip(hiddens, stages):
+        feed_part = dot(hidden, down_weight).astype(bf16)
+        feed_blocks += [feed_part[k * rows : (k + 1) * rows] for k in range(len(stage))]
     feed_total = scatter_parts(feed_blocks, tensor)
     hidden_held, feed_total = lax.optimization_barrier((hidden_first, feed_total))
     output = (hidden_held + feed_total).astype(bf16)
@@ -952,7 +1034,7 @@
         functools.partial(state_bwd_body, widths, kc, heads, tensor),
         t_array,
         (
-            gain1, *weights, taps, nega, skip, mask, g, run, run_t, dt, link,
+            gain1, *weights, taps, nega, skip, weight, mixing, slope, xc, ub, moved, linked, dt, link,
             n1, u, acc, ysum, raw, d1, dssm, feed_grad[None, :],
         ),
         [((width // 2, wl), bf16), ((width // 2, wl), bf16), *blocks],

time: 275 us -> 267 us (0.971)
  waiting for transfers between devices: 165 us -> 135 us
  starting transfers between devices: 46.4 us -> 62.5 us
  Pallas kernels: 48.4 us -> 51.7 us
    ppermute x59, waiting for transfers between devices: 165 us -> 135 us  [swap(): return lax.ppermute(value, axis, xor_pairs(size, bit))]
    ppermute x59, starting transfers between devices: 46.4 us -> 62.5 us  [swap(): return lax.ppermute(value, axis, xor_pairs(size, bit))]
    pallas_call x16 -> x19, Pallas kernels: 48.4 us -> 51.7 us  [call_kernel(): pl.pallas_call(body, in_specs=[pl.BlockSpec(memory_space=pltpu.SMEM)] + [...]
  transfers between devices with their start and end apart: 59 -> 59, of which waited for: 31 -> 29; matrix products, arithmetic and copies ran while one was open for 3% -> 4% of each run, Pallas kernels for 11% -> 14%
where the time goes in v2:
time: 267 us
  waiting for transfers between devices  135 us (51%)
  starting transfers between devices  62.5 us (23%)
  Pallas kernels  51.7 us (19%)
  local copies, waits for them, and re-layouts  9.25 us (3%)
  other arithmetic  5.19 us (2%)
    ppermute x59, waiting for transfers between devices, swap(): return lax.ppermute(value, axis, xor_pairs(size, bit))  135 us
    ppermute x59, starting transfers between devices, swap(): return lax.ppermute(value, axis, xor_pairs(size, bit))  62.5 us
    pallas_call x19, Pallas kernels, call_kernel(): pl.pallas_call(body, in_specs=[pl.BlockSpec(memory_space=pltpu.SMEM)] + [...  51.7 us
  transfers between devices with their start and end apart: 59, of which 29 were waited for; matrix products, arithmetic and copies ran while one was open for 4% of the time, Pallas kernels for 14%

profile of v2, /device:TPU:0, one launch (start us, length us, event | category | flops | bytes accessed | tf_op | source)
XLA Modules:
  0.0 266.8 jit_solution(12821786609473818271)
XLA Ops:
  0.7 3.1 %collective-permute-start = (bf16[128,1024]{1,0:T(8,128)(2,1)}, bf16[128,1024]{1,0:T(8,128)(2,1)S(1)}, u32[]{:S(2)}, u32[]{:S(2)}) collective-permute-start(bf16[128,1024]{1,0:T(8,128)(2,1)} %refs_3_.3), channel_id=1, source_target_pairs={{0,1},{1,0},{2,3},{3,2},{4,5},{5,4},{6,7},{7,6},{8,9},{9,8},{10,11... | collective-permute-start | bytes 786440 | tf_op jit(solution)/shard_map/ppermute | solution.py:775
  3.8 2.6 collective-permute-start.1
  9.8 8.7 %collective-permute-done.1.refs_3_ = bf16[128,1024]{1,0:T(8,128)(2,1)} collective-permute-done((bf16[128,1024]{1,0:T(8,128)(2,1)}, bf16[128,1024]{1,0:T(8,128)(2,1)}, u32[]{:S(2)}, u32[]{:S(2)}) %collective-permute-start.1) | collective-permute-done | bytes 262176 | tf_op jit(solution)/shard_map/ppermute | solution.py:775
  26.2 10.5 %shard_map.408 = (bf16[512,1024]{1,0:T(8,128)(2,1)S(1)}, bf16[512,384]{1,0:T(8,128)(2,1)S(1)}, bf16[512,128]{1,0:T(8,128)(2,1)S(1)}, f32[512,128]{1,0:T(8,128)S(...) custom-call(s32[2]{0:T(128)S(1)} %compare_select_fusion.t_ref.refs_0, ...), custom_call_target="tpu_custom_call" | custom-call | tf_op jit(solution)/shard_map/pallas_call | solution.py:742
  40.7 10.9 %collective-permute-done.3 = bf16[128,1024]{1,0:T(8,128)(2,1)S(1)} collective-permute-done((bf16[128,1024]{1,0:T(8,128)(2,1)S(1)}, bf16[128,1024]{1,0:T(8,128)(2,1)S(1)}, u32[]{:S(2)}, u32[]{:S(2)}) %collective-permute-start.3) | collective-permute-done | bytes 262176 | tf_op jit(solution)/shard_map/ppermute | solution.py:775
  53.9 9.8 %collective-permute-done.5 = bf16[128,1024]{1,0:T(8,128)(2,1)S(1)} collective-permute-done((bf16[128,1024]{1,0:T(8,128)(2,1)S(1)}, bf16[128,1024]{1,0:T(8,128)(2,1)S(1)}, u32[]{:S(2)}, u32[]{:S(2)}) %collective-permute-start.5) | collective-permute-done | bytes 262176 | tf_op jit(solution)/shard_map/ppermute | solution.py:775
  65.4 6.8 %collective-permute-done.8 = bf16[128,1024]{1,0:T(8,128)(2,1)S(1)} collective-permute-done((bf16[128,1024]{1,0:T(8,128)(2,1)S(1)}, bf16[128,1024]{1,0:T(8,128)(2,1)S(1)}, u32[]{:S(2)}, u32[]{:S(2)}) %collective-permute-start.8) | collective-permute-done | bytes 262176 | tf_op jit(solution)/shard_map/ppermute | solution.py:775
  72.3 5.7 %collective-permute-done.7.refs_2_ = bf16[128,1024]{1,0:T(8,128)(2,1)S(1)} collective-permute-done((bf16[128,1024]{1,0:T(8,128)(2,1)S(1)}, bf16[128,1024]{1,0:T(8,128)(2,1)S(1)}, u32[]{:S(2)}, u32[]{:S(2)}) %collective-permute-start.7) | collective-permute-done | bytes 262176 | tf_op jit(solution)/shard_map/ppermute | solution.py:775
  80.5 5.9 %collective-permute-done.10.refs_0_ = bf16[128,1024]{1,0:T(8,128)(2,1)S(1)} collective-permute-done((bf16[128,1024]{1,0:T(8,128)(2,1)S(1)}, bf16[128,1024]{1,0:T(8,128)(2,1)S(1)}, u32[]{:S(2)}, u32[]{:S(2)}) %collective-permute-start.10) | collective-permute-done | bytes 262176 | tf_op jit(solution)/shard_map/ppermute | solution.py:775
  89.5 2.4 collective-permute-done.6.refs_1_
  91.9 2.5 shard_map.409
  95.3 3.8 %collective-permute-done.15 = bf16[128,1024]{1,0:T(8,128)(2,1)S(1)} collective-permute-done((bf16[128,1024]{1,0:T(8,128)(2,1)S(1)}, bf16[128,1024]{1,0:T(8,128)(2,1)S(1)}, u32[]{:S(2)}, u32[]{:S(2)}) %collective-permute-start.15) | collective-permute-done | bytes 262176 | tf_op jit(solution)/shard_map/ppermute | solution.py:775
  101.1 3.2 %shard_map.422 = (bf16[768,1024]{1,0:T(8,128)(2,1)S(1)}, bf16[768,1024]{1,0:T(8,128)(2,1)S(1)}) custom-call(s32[2]{0:T(128)S(1)} %compare_select_fusion.t_ref.refs_0_.scalar.d_ref.u_ref, bf16[384,1024]{1,0:T(8,128)(2,1)S(1)} %get-tuple-element.192.refs_0_, bf16[128,1024]{1,0:T(8,128)(2,1)S(1)} %get-tuple-element.193.refs_1_, ...), custom_call_target="tpu_custom_call" | custom-call | tf_op jit(solution)/shard_map/pallas_call | solution.py:742
  104.4 5.0 %collective-permute-done.16 = bf16[128,1024]{1,0:T(8,128)(2,1)S(1)} collective-permute-done((bf16[128,1024]{1,0:T(8,128)(2,1)S(1)}, bf16[128,1024]{1,0:T(8,128)(2,1)S(1)}, u32[]{:S(2)}, u32[]{:S(2)}) %collective-permute-start.16) | collective-permute-done | bytes 262176 | tf_op jit(solution)/shard_map/ppermute | solution.py:775
  110.8 6.6 %collective-permute-start.18 = (bf16[128,1024]{1,0:T(8,128)(2,1)S(1)}, bf16[128,1024]{1,0:T(8,128)(2,1)S(1)}, u32[]{:S(2)}, u32[]{:S(2)}) collective-permute-start(bf16[128,1024]{1,0:T(8,128)(2,1)S(1)} %get-tuple-element.207.refs_1_), channel_id=1, source_target_pairs={{0,1},{1,0},{2,3},{3,2},{4,5},{5,4},{6,7},{7,6},{8,9},{9,8},{10,11... | collective-permute-start | bytes 786440 | tf_op jit(solution)/shard_map/ppermute | solution.py:775
  118.2 6.0 %collective-permute-start.20 = (bf16[128,1024]{1,0:T(8,128)(2,1)S(1)}, bf16[128,1024]{1,0:T(8,128)(2,1)S(1)}, u32[]{:S(2)}, u32[]{:S(2)}) collective-permute-start(bf16[128,1024]{1,0:T(8,128)(2,1)S(1)} %collective-permute-done.19.refs_3_), channel_id=1, source_target_pairs={{0,1},{1,0},{2,3},{3,2},{4,5},{5,4},{6,7},{7,6},{8,9},{9,8},{10,11... | collective-permute-start | bytes 786440 | tf_op jit(solution)/shard_map/ppermute | solution.py:775
  124.2 3.1 %shard_map.411 = (f32[2,512,512]{2,1,0:T(8,128)S(1)}, f32[6,512,512]{2,1,0:T(8,128)S(1)}, bf16[6,512,512]{2,1,0:T(8,128)(2,1)S(1)}, f32[512,640]{1,0:T(8,128)S(1...) custom-call(s32[2]{0:T(128)S(1)} %compare_select_fusion.t_ref.refs_0, ...), custom_call_target="tpu_custom_call" | custom-call | tf_op jit(solution)/shard_map/pallas_call | solution.py:742
  128.6 4.9 %shard_map.412 = (bf16[512,640]{1,0:T(8,128)(2,1)S(1)}, f32[512,384]{1,0:T(8,128)S(1)}, bf16[512,1024]{1,0:T(8,128)(2,1)S(1)}, bf16[512,1024]{1,0:T(8,128)(2,1)S(1)}) custom-call(s32[2]{0:T(128)S(1)} %compare_select_fusion.t_ref.refs_0_.scalar.d_ref.u_ref, bf16[128,1024]{1,0:T(8,128)(2,1)S(1)} %get-tuple-element.207.refs_1_, ...), custom_call_target="tpu_custom_call" | custom-call | tf_op jit(solution)/shard_map/pallas_call | solution.py:742
  133.6 8.1 %shard_map.413 = (bf16[512,896]{1,0:T(8,128)(2,1)S(1)}, bf16[512,896]{1,0:T(8,128)(2,1)S(1)}, bf16[128,1024]{1,0:T(8,128)(2,1)S(1)}, bf16[128,1024]{1,0:T(8,128)...) custom-call(s32[2]{0:T(128)S(1)} %compare_select_fusion.t_ref.refs_0_.scalar.d_ref.u_ref, ...), custom_call_target="tpu_custom_call" | custom-call | tf_op jit(solution)/shard_map/pallas_call | solution.py:742
  145.4 6.5 %collective-permute-done.12 = bf16[128,1024]{1,0:T(8,128)(2,1)S(1)} collective-permute-done((bf16[128,1024]{1,0:T(8,128)(2,1)S(1)}, bf16[128,1024]{1,0:T(8,128)(2,1)S(1)}, u32[]{:S(2)}, u32[]{:S(2)}) %collective-permute-start.12) | collective-permute-done | bytes 262176 | tf_op jit(solution)/shard_map/ppermute | solution.py:775
  162.0 3.7 %collective-permute-done.13 = bf16[128,1024]{1,0:T(8,128)(2,1)S(1)} collective-permute-done((bf16[128,1024]{1,0:T(8,128)(2,1)S(1)}, bf16[128,1024]{1,0:T(8,128)(2,1)S(1)}, u32[]{:S(2)}, u32[]{:S(2)}) %collective-permute-start.13) | collective-permute-done | bytes 262176 | tf_op jit(solution)/shard_map/ppermute | solution.py:775
  170.1 15.3 %collective-permute-done.27.refs_3_ = bf16[128,896]{1,0:T(8,128)(2,1)S(1)} collective-permute-done((bf16[128,896]{1,0:T(8,128)(2,1)S(1)}, bf16[128,896]{1,0:T(8,128)(2,1)S(1)}, u32[]{:S(2)}, u32[]{:S(2)}) %collective-permute-start.27) | collective-permute-done | bytes 229408 | tf_op jit(solution)/shard_map/ppermute | solution.py:775
  199.8 10.6 %collective-permute-done.40.refs_3_ = bf16[128,1024]{1,0:T(8,128)(2,1)S(1)} collective-permute-done((bf16[128,1024]{1,0:T(8,128)(2,1)S(1)}, bf16[128,1024]{1,0:T(8,128)(2,1)S(1)}, u32[]{:S(2)}, u32[]{:S(2)}) %collective-permute-start.40) | collective-permute-done | bytes 262176 | tf_op jit(solution)/shard_map/ppermute | solution.py:775
  215.5 8.4 %collective-permute-done.53.refs_2_ = bf16[192,1024]{1,0:T(8,128)(2,1)S(1)} collective-permute-done((bf16[192,1024]{1,0:T(8,128)(2,1)S(1)}, bf16[192,1024]{1,0:T(8,128)(2,1)S(1)}, u32[]{:S(2)}, u32[]{:S(2)}) %collective-permute-start.53) | collective-permute-done | bytes 393248 | tf_op jit(solution)/shard_map/ppermute | solution.py:775
  224.6 3.5 %collective-permute-start.31 = (bf16[128,1024]{1,0:T(8,128)(2,1)S(1)}, bf16[128,1024]{1,0:T(8,128)(2,1)S(1)}, u32[]{:S(2)}, u32[]{:S(2)}) collective-permute-start(bf16[128,1024]{1,0:T(8,128)(2,1)S(1)} %shard_map.416.refs_0_), channel_id=1, source_target_pairs={{0,8},{4,12},{8,0},{12,4},{16,24},{20,28},{24,16},{28,20},{1,9},{5... | collective-permute-start | bytes 786440 | tf_op jit(solution)/shard_map/ppermute | solution.py:775
  228.3 5.5 %collective-permute-done.42.refs_2_ = bf16[128,1024]{1,0:T(8,128)(2,1)S(1)} collective-permute-done((bf16[128,1024]{1,0:T(8,128)(2,1)S(1)}, bf16[128,1024]{1,0:T(8,128)(2,1)S(1)}, u32[]{:S(2)}, u32[]{:S(2)}) %collective-permute-start.42) | collective-permute-done | bytes 262176 | tf_op jit(solution)/shard_map/ppermute | solution.py:775
  234.0 5.6 %collective-permute-done.31.refs_1_ = bf16[128,1024]{1,0:T(8,128)(2,1)S(1)} collective-permute-done((bf16[128,1024]{1,0:T(8,128)(2,1)S(1)}, bf16[128,1024]{1,0:T(8,128)(2,1)S(1)}, u32[]{:S(2)}, u32[]{:S(2)}) %collective-permute-start.31) | collective-permute-done | bytes 262176 | tf_op jit(solution)/shard_map/ppermute | solution.py:775
  239.6 5.0 %collective-permute-done.33.refs_2_ = bf16[128,1024]{1,0:T(8,128)(2,1)S(1)} collective-permute-done((bf16[128,1024]{1,0:T(8,128)(2,1)S(1)}, bf16[128,1024]{1,0:T(8,128)(2,1)S(1)}, u32[]{:S(2)}, u32[]{:S(2)}) %collective-permute-start.33) | collective-permute-done | bytes 262176 | tf_op jit(solution)/shard_map/ppermute | solution.py:775
  247.9 3.4 %shard_map.425 = (f32[1024,512]{1,0:T(8,128)}, f32[1024,512]{1,0:T(8,128)}, f32[512,1024]{1,0:T(8,128)}) custom-call(s32[2]{0:T(128)S(1)} %compare_select_fusion.t_ref.refs_0_.scalar.d_ref.u_ref, bf16[192,1024]{1,0:T(8,128)(2,1)S(1)} %shard_map.424.refs_0_, bf16[192,1024]{1,0:T(8,128)(2,1)S(1)} %collective-permute-done.52.refs_1_, ...), custom_call_target="tpu_custom_call" | custom-call | tf_op jit(solution)/shard_map/pallas_call | solution.py:742
  251.3 3.1 %shard_map.421 = (f32[128,1024]{1,0:T(8,128)}, f32[384,1024]{1,0:T(8,128)}, f32[1024,384]{1,0:T(8,128)}, f32[1024,128]{1,0:T(8,128)}) custom-call(s32[2]{0:T(128)S(1)} %compare_select_fusion.t_ref.refs_0_.scalar.d_ref.u_ref, bf16[128,1024]{1,0:T(8,128)(2,1)S(1)} %shard_map.420.refs_0_, bf16[128,1024]{1,0:T(8,128)(2,1)S(1)} %collective-permute-done.41.refs_1_, ...), custom_call_target="tpu_custom_call" | custom-call | tf_op jit(solution)/shard_map/pallas_call | solution.py:742
  254.4 5.8 %collective-permute-done.22.refs_1_ = bf16[128,1024]{1,0:T(8,128)(2,1)S(1)} collective-permute-done((bf16[128,1024]{1,0:T(8,128)(2,1)S(1)}, bf16[128,1024]{1,0:T(8,128)(2,1)S(1)}, u32[]{:S(2)}, u32[]{:S(2)}) %collective-permute-start.22) | collective-permute-done | bytes 262176 | tf_op jit(solution)/shard_map/ppermute | solution.py:775
  260.2 3.3 %shard_map.418 = (f32[1024,128]{1,0:T(8,128)}, f32[1024,128]{1,0:T(8,128)}, f32[1024,256]{1,0:T(8,128)}, f32[1024,384]{1,0:T(8,128)}, f32[6,1024]{1,0:T(8,128)},...) custom-call(s32[2]{0:T(128)S(1)} %compare_select_fusion.t_ref.refs_0, ...), custom_call_target="tpu_custom_call" | custom-call | tf_op jit(solution)/shard_map/pallas_call | solution.py:742
  (181 shorter events, 76.0 us)
Async XLA Ops:
  0.7 23.6 %collective-permute-start = (bf16[128,1024]{1,0:T(8,128)(2,1)}, bf16[128,1024]{1,0:T(8,128)(2,1)S(1)}, u32[]{:S(2)}, u32[]{:S(2)}) collective-permute-start(bf16[128,1024]{1,0:T(8,128)(2,1)} %refs_3_.3), channel_id=1, source_target_pairs={{0,1},{1,0},{2,3},{3,2},{4,5},{5,4},{6,7},{7,6},{8,9},{9,8},{10,11... | collective-permute-start | bytes 786440 | tf_op jit(solution)/shard_map/ppermute | solution.py:775
  3.8 14.7 %collective-permute-start.1 = (bf16[128,1024]{1,0:T(8,128)(2,1)}, bf16[128,1024]{1,0:T(8,128)(2,1)}, u32[]{:S(2)}, u32[]{:S(2)}) collective-permute-start(bf16[128,1024]{1,0:T(8,128)(2,1)} %refs_3_.3), channel_id=1, source_target_pairs={{0,2},{1,3},{2,0},{3,1},{4,6},{5,7},{6,4},{7,5},{8,10},{9,11},{10,... | collective-permute-start | bytes 786440 | tf_op jit(solution)/shard_map/ppermute | solution.py:775
  36.8 14.9 %collective-permute-start.3 = (bf16[128,1024]{1,0:T(8,128)(2,1)S(1)}, bf16[128,1024]{1,0:T(8,128)(2,1)S(1)}, u32[]{:S(2)}, u32[]{:S(2)}) collective-permute-start(bf16[128,1024]{1,0:T(8,128)(2,1)S(1)} %get-tuple-element.119), channel_id=1, source_target_pairs={{0,1},{1,0},{2,3},{3,2},{4,5},{5,4},{6,7},{7,6},{8,9},{9,8},{10,11... | collective-permute-start | bytes 786440 | tf_op jit(solution)/shard_map/ppermute | solution.py:775
  38.0 15.7 %collective-permute-start.9 = (bf16[128,1024]{1,0:T(8,128)(2,1)S(1)}, bf16[128,1024]{1,0:T(8,128)(2,1)S(1)}, u32[]{:S(2)}, u32[]{:S(2)}) collective-permute-start(bf16[128,1024]{1,0:T(8,128)(2,1)S(1)} %copy-done.19), channel_id=1, source_target_pairs={{0,2},{1,3},{2,0},{3,1},{4,6},{5,7},{6,4},{7,5},{8,10},{9,11},{10,... | collective-permute-start | bytes 786440 | tf_op jit(solution)/shard_map/ppermute | solution.py:775
  39.9 23.8 %collective-permute-start.5 = (bf16[128,1024]{1,0:T(8,128)(2,1)S(1)}, bf16[128,1024]{1,0:T(8,128)(2,1)S(1)}, u32[]{:S(2)}, u32[]{:S(2)}) collective-permute-start(bf16[128,1024]{1,0:T(8,128)(2,1)S(1)} %get-tuple-element.120), channel_id=1, source_target_pairs={{0,1},{1,0},{2,3},{3,2},{4,5},{5,4},{6,7},{7,6},{8,9},{9,8},{10,11... | collective-permute-start | bytes 786440 | tf_op jit(solution)/shard_map/ppermute | solution.py:775
  51.8 20.4 %collective-permute-start.8 = (bf16[128,1024]{1,0:T(8,128)(2,1)S(1)}, bf16[128,1024]{1,0:T(8,128)(2,1)S(1)}, u32[]{:S(2)}, u32[]{:S(2)}) collective-permute-start(bf16[128,1024]{1,0:T(8,128)(2,1)S(1)} %copy-done.19), channel_id=1, source_target_pairs={{0,1},{1,0},{2,3},{3,2},{4,5},{5,4},{6,7},{7,6},{8,9},{9,8},{10,11... | collective-permute-start | bytes 786440 | tf_op jit(solution)/shard_map/ppermute | solution.py:775
  53.8 24.2 %collective-permute-start.11 = (bf16[128,1024]{1,0:T(8,128)(2,1)S(1)}, bf16[128,1024]{1,0:T(8,128)(2,1)S(1)}, u32[]{:S(2)}, u32[]{:S(2)}) collective-permute-start(bf16[128,1024]{1,0:T(8,128)(2,1)S(1)} %collective-permute-done.9), channel_id=1, source_target_pairs={{0,1},{1,0},{2,3},{3,2},{4,5},{5,4},{6,7},{7,6},{8,9},{9,8},{10,11... | collective-permute-start | bytes 786440 | tf_op jit(solution)/shard_map/ppermute | solution.py:775
  64.1 13.8 %collective-permute-start.7 = (bf16[128,1024]{1,0:T(8,128)(2,1)S(1)}, bf16[128,1024]{1,0:T(8,128)(2,1)S(1)}, u32[]{:S(2)}, u32[]{:S(2)}) collective-permute-start(bf16[128,1024]{1,0:T(8,128)(2,1)S(1)} %multiply_convert_fusion.refs_0_), channel_id=1, source_target_pairs={{0,2},{1,3},{2,0},{3,1},{4,6},{5,7},{6,4},{7,5},{8,10},{9,11},{10,... | collective-permute-start | bytes 786440 | tf_op jit(solution)/shard_map/ppermute | solution.py:775
  104.3 51.7 %collective-permute-start.48 = (bf16[768,1024]{1,0:T(8,128)(2,1)S(1)}, bf16[768,1024]{1,0:T(8,128)(2,1)S(1)}, u32[]{:S(2)}, u32[]{:S(2)}) collective-permute-start(bf16[768,1024]{1,0:T(8,128)(2,1)S(1)} %get-tuple-element.197), channel_id=1, source_target_pairs={{0,4},{4,0},{8,12},{12,8},{16,20},{20,16},{24,28},{28,24},{1,5},{5... | collective-permute-start | bytes 4718600 | tf_op jit(solution)/shard_map/ppermute | solution.py:775
  110.8 16.6 %collective-permute-start.18 = (bf16[128,1024]{1,0:T(8,128)(2,1)S(1)}, bf16[128,1024]{1,0:T(8,128)(2,1)S(1)}, u32[]{:S(2)}, u32[]{:S(2)}) collective-permute-start(bf16[128,1024]{1,0:T(8,128)(2,1)S(1)} %get-tuple-element.207.refs_1_), channel_id=1, source_target_pairs={{0,1},{1,0},{2,3},{3,2},{4,5},{5,4},{6,7},{7,6},{8,9},{9,8},{10,11... | collective-permute-start | bytes 786440 | tf_op jit(solution)/shard_map/ppermute | solution.py:775
  141.8 25.4 %collective-permute-start.37 = (bf16[512,1024]{1,0:T(8,128)(2,1)S(1)}, bf16[512,1024]{1,0:T(8,128)(2,1)S(1)}, u32[]{:S(2)}, u32[]{:S(2)}) collective-permute-start(bf16[512,1024]{1,0:T(8,128)(2,1)S(1)} %get-tuple-element.170), channel_id=1, source_target_pairs={{0,4},{4,0},{8,12},{12,8},{16,20},{20,16},{24,28},{28,24},{1,5},{5... | collective-permute-start | bytes 3145736 | tf_op jit(solution)/shard_map/ppermute | solution.py:775
  145.3 15.2 %collective-permute-start.14 = (bf16[128,1024]{1,0:T(8,128)(2,1)S(1)}, bf16[128,1024]{1,0:T(8,128)(2,1)S(1)}, u32[]{:S(2)}, u32[]{:S(2)}) collective-permute-start(bf16[128,1024]{1,0:T(8,128)(2,1)S(1)} %slice.14), channel_id=1, source_target_pairs={{0,1},{1,0},{2,3},{3,2},{4,5},{5,4},{6,7},{7,6},{8,9},{9,8},{10,11... | collective-permute-start | bytes 786440 | tf_op jit(solution)/shard_map/ppermute | solution.py:775
  151.9 13.7 %collective-permute-start.13 = (bf16[128,1024]{1,0:T(8,128)(2,1)S(1)}, bf16[128,1024]{1,0:T(8,128)(2,1)S(1)}, u32[]{:S(2)}, u32[]{:S(2)}) collective-permute-start(bf16[128,1024]{1,0:T(8,128)(2,1)S(1)} %add_convert_fusion.3), channel_id=1, source_target_pairs={{0,2},{1,3},{2,0},{3,1},{4,6},{5,7},{6,4},{7,5},{8,10},{9,11},{10,... | collective-permute-start | bytes 786440 | tf_op jit(solution)/shard_map/ppermute | solution.py:775
  154.4 14.2 %collective-permute-start.25 = (bf16[128,896]{1,0:T(8,128)(2,1)S(1)}, bf16[128,896]{1,0:T(8,128)(2,1)S(1)}, u32[]{:S(2)}, u32[]{:S(2)}) collective-permute-start(bf16[128,896]{1,0:T(8,128)(2,1)S(1)} %get-tuple-element.160), channel_id=1, source_target_pairs={{0,8},{4,12},{8,0},{12,4},{16,24},{20,28},{24,16},{28,20},{1,9},{5... | collective-permute-start | bytes 688136 | tf_op jit(solution)/shard_map/ppermute | solution.py:775
  156.0 14.1 %collective-permute-start.26 = (bf16[128,896]{1,0:T(8,128)(2,1)S(1)}, bf16[128,896]{1,0:T(8,128)(2,1)S(1)}, u32[]{:S(2)}, u32[]{:S(2)}) collective-permute-start(bf16[128,896]{1,0:T(8,128)(2,1)S(1)} %get-tuple-element.161), channel_id=1, source_target_pairs={{0,16},{4,20},{8,24},{12,28},{16,0},{20,4},{24,8},{28,12},{1,17},{... | collective-permute-start | bytes 688136 | tf_op jit(solution)/shard_map/ppermute | solution.py:775
  160.5 26.4 %collective-permute-start.49 = (bf16[192,1024]{1,0:T(8,128)(2,1)S(1)}, bf16[192,1024]{1,0:T(8,128)(2,1)S(1)}, u32[]{:S(2)}, u32[]{:S(2)}) collective-permute-start(bf16[192,1024]{1,0:T(8,128)(2,1)S(1)} %get-tuple-element.199), channel_id=1, source_target_pairs={{0,8},{4,12},{8,0},{12,4},{16,24},{20,28},{24,16},{28,20},{1,9},{5... | collective-permute-start | bytes 1179656 | tf_op jit(solution)/shard_map/ppermute | solution.py:775
  165.6 22.8 %collective-permute-start.50 = (bf16[192,1024]{1,0:T(8,128)(2,1)S(1)}, bf16[192,1024]{1,0:T(8,128)(2,1)S(1)}, u32[]{:S(2)}, u32[]{:S(2)}) collective-permute-start(bf16[192,1024]{1,0:T(8,128)(2,1)S(1)} %get-tuple-element.200), channel_id=1, source_target_pairs={{0,16},{4,20},{8,24},{12,28},{16,0},{20,4},{24,8},{28,12},{1,17},{... | collective-permute-start | bytes 1179656 | tf_op jit(solution)/shard_map/ppermute | solution.py:775
  167.2 23.3 %collective-permute-start.51 = (bf16[192,1024]{1,0:T(8,128)(2,1)S(1)}, bf16[192,1024]{1,0:T(8,128)(2,1)S(1)}, u32[]{:S(2)}, u32[]{:S(2)}) collective-permute-start(bf16[192,1024]{1,0:T(8,128)(2,1)S(1)} %get-tuple-element.201), channel_id=1, source_target_pairs={{0,24},{4,28},{8,16},{12,20},{16,8},{20,12},{24,0},{28,4},{1,25},{... | collective-permute-start | bytes 1179656 | tf_op jit(solution)/shard_map/ppermute | solution.py:775
  168.6 16.8 %collective-permute-start.27 = (bf16[128,896]{1,0:T(8,128)(2,1)S(1)}, bf16[128,896]{1,0:T(8,128)(2,1)S(1)}, u32[]{:S(2)}, u32[]{:S(2)}) collective-permute-start(bf16[128,896]{1,0:T(8,128)(2,1)S(1)} %get-tuple-element.162), channel_id=1, source_target_pairs={{0,24},{4,28},{8,16},{12,20},{16,8},{20,12},{24,0},{28,4},{1,25},{... | collective-permute-start | bytes 688136 | tf_op jit(solution)/shard_map/ppermute | solution.py:775
  170.1 21.6 %collective-permute-start.21 = (bf16[128,1024]{1,0:T(8,128)(2,1)S(1)}, bf16[128,1024]{1,0:T(8,128)(2,1)S(1)}, u32[]{:S(2)}, u32[]{:S(2)}) collective-permute-start(bf16[128,1024]{1,0:T(8,128)(2,1)S(1)} %get-tuple-element.155), channel_id=1, source_target_pairs={{0,1},{1,0},{2,3},{3,2},{4,5},{5,4},{6,7},{7,6},{8,9},{9,8},{10,11... | collective-permute-start | bytes 786440 | tf_op jit(solution)/shard_map/ppermute | solution.py:775
  191.7 21.8 %collective-permute-start.52 = (bf16[192,1024]{1,0:T(8,128)(2,1)S(1)}, bf16[192,1024]{1,0:T(8,128)(2,1)S(1)}, u32[]{:S(2)}, u32[]{:S(2)}) collective-permute-start(bf16[192,1024]{1,0:T(8,128)(2,1)S(1)} %shard_map.424.refs_0_), channel_id=1, source_target_pairs={{0,8},{4,12},{8,0},{12,4},{16,24},{20,28},{24,16},{28,20},{1,9},{5... | collective-permute-start | bytes 1179656 | tf_op jit(solution)/shard_map/ppermute | solution.py:775
  194.3 29.6 %collective-permute-start.53 = (bf16[192,1024]{1,0:T(8,128)(2,1)S(1)}, bf16[192,1024]{1,0:T(8,128)(2,1)S(1)}, u32[]{:S(2)}, u32[]{:S(2)}) collective-permute-start(bf16[192,1024]{1,0:T(8,128)(2,1)S(1)} %shard_map.424.refs_0_), channel_id=1, source_target_pairs={{0,16},{4,20},{8,24},{12,28},{16,0},{20,4},{24,8},{28,12},{1,17},{... | collective-permute-start | bytes 1179656 | tf_op jit(solution)/shard_map/ppermute | solution.py:775
  195.0 15.4 %collective-permute-start.40 = (bf16[128,1024]{1,0:T(8,128)(2,1)S(1)}, bf16[128,1024]{1,0:T(8,128)(2,1)S(1)}, u32[]{:S(2)}, u32[]{:S(2)}) collective-permute-start(bf16[128,1024]{1,0:T(8,128)(2,1)S(1)} %get-tuple-element.174), channel_id=1, source_target_pairs={{0,24},{4,28},{8,16},{12,20},{16,8},{20,12},{24,0},{28,4},{1,25},{... | collective-permute-start | bytes 786440 | tf_op jit(solution)/shard_map/ppermute | solution.py:775
  197.3 27.3 %collective-permute-start.54 = (bf16[192,1024]{1,0:T(8,128)(2,1)S(1)}, bf16[192,1024]{1,0:T(8,128)(2,1)S(1)}, u32[]{:S(2)}, u32[]{:S(2)}) collective-permute-start(bf16[192,1024]{1,0:T(8,128)(2,1)S(1)} %shard_map.424.refs_0_), channel_id=1, source_target_pairs={{0,24},{4,28},{8,16},{12,20},{16,8},{20,12},{24,0},{28,4},{1,25},{... | collective-permute-start | bytes 1179656 | tf_op jit(solution)/shard_map/ppermute | solution.py:775
  199.8 24.8 %collective-permute-start.55 = (bf16[192,1024]{1,0:T(8,128)(2,1)S(1)}, bf16[192,1024]{1,0:T(8,128)(2,1)S(1)}, u32[]{:S(2)}, u32[]{:S(2)}) collective-permute-start(bf16[192,1024]{1,0:T(8,128)(2,1)S(1)} %shard_map.424.refs_0_), channel_id=1, source_target_pairs={{0,4},{4,0},{8,12},{12,8},{16,20},{20,16},{24,28},{28,24},{1,5},{5... | collective-permute-start | bytes 1179656 | tf_op jit(solution)/shard_map/ppermute | solution.py:775
  213.5 14.7 %collective-permute-start.41 = (bf16[128,1024]{1,0:T(8,128)(2,1)S(1)}, bf16[128,1024]{1,0:T(8,128)(2,1)S(1)}, u32[]{:S(2)}, u32[]{:S(2)}) collective-permute-start(bf16[128,1024]{1,0:T(8,128)(2,1)S(1)} %shard_map.420.refs_0_), channel_id=1, source_target_pairs={{0,8},{4,12},{8,0},{12,4},{16,24},{20,28},{24,16},{28,20},{1,9},{5... | collective-permute-start | bytes 786440 | tf_op jit(solution)/shard_map/ppermute | solution.py:775
  224.6 14.9 %collective-permute-start.31 = (bf16[128,1024]{1,0:T(8,128)(2,1)S(1)}, bf16[128,1024]{1,0:T(8,128)(2,1)S(1)}, u32[]{:S(2)}, u32[]{:S(2)}) collective-permute-start(bf16[128,1024]{1,0:T(8,128)(2,1)S(1)} %shard_map.416.refs_0_), channel_id=1, source_target_pairs={{0,8},{4,12},{8,0},{12,4},{16,24},{20,28},{24,16},{28,20},{1,9},{5... | collective-permute-start | bytes 786440 | tf_op jit(solution)/shard_map/ppermute | solution.py:775
  228.2 16.9 %collective-permute-start.56 = (bf16[192,1024]{1,0:T(8,128)(2,1)S(1)}, bf16[192,1024]{1,0:T(8,128)(2,1)S(1)}, u32[]{:S(2)}, u32[]{:S(2)}) collective-permute-start(bf16[192,1024]{1,0:T(8,128)(2,1)S(1)} %collective-permute-done.52.refs_1_), channel_id=1, source_target_pairs={{0,4},{4,0},{8,12},{12,8},{16,20},{20,16},{24,28},{28,24},{1,5},{5... | collective-permute-start | bytes 1179656 | tf_op jit(solution)/shard_map/ppermute | solution.py:775
  245.2 15.0 %collective-permute-start.22 = (bf16[128,1024]{1,0:T(8,128)(2,1)S(1)}, bf16[128,1024]{1,0:T(8,128)(2,1)S(1)}, u32[]{:S(2)}, u32[]{:S(2)}) collective-permute-start(bf16[128,1024]{1,0:T(8,128)(2,1)S(1)} %add_convert_fusion), channel_id=1, source_target_pairs={{0,2},{1,3},{2,0},{3,1},{4,6},{5,7},{6,4},{7,5},{8,10},{9,11},{10,... | collective-permute-start | bytes 786440 | tf_op jit(solution)/shard_map/ppermute | solution.py:775
  245.3 14.9 %collective-permute-start.30 = (bf16[128,1024]{1,0:T(8,128)(2,1)S(1)}, bf16[128,1024]{1,0:T(8,128)(2,1)S(1)}, u32[]{:S(2)}, u32[]{:S(2)}) collective-permute-start(bf16[128,1024]{1,0:T(8,128)(2,1)S(1)} %shard_map.416.refs_0_), channel_id=1, source_target_pairs={{0,4},{4,0},{8,12},{12,8},{16,20},{20,16},{24,28},{28,24},{1,5},{5... | collective-permute-start | bytes 786440 | tf_op jit(solution)/shard_map/ppermute | solution.py:775
  246.1 14.1 %collective-permute-start.32 = (bf16[128,1024]{1,0:T(8,128)(2,1)S(1)}, bf16[128,1024]{1,0:T(8,128)(2,1)S(1)}, u32[]{:S(2)}, u32[]{:S(2)}) collective-permute-start(bf16[128,1024]{1,0:T(8,128)(2,1)S(1)} %collective-permute-done.31.refs_1_), channel_id=1, source_target_pairs={{0,4},{4,0},{8,12},{12,8},{16,20},{20,16},{24,28},{28,24},{1,5},{5... | collective-permute-start | bytes 786440 | tf_op jit(solution)/shard_map/ppermute | solution.py:775
  246.5 13.7 %collective-permute-start.34 = (bf16[128,1024]{1,0:T(8,128)(2,1)S(1)}, bf16[128,1024]{1,0:T(8,128)(2,1)S(1)}, u32[]{:S(2)}, u32[]{:S(2)}) collective-permute-start(bf16[128,1024]{1,0:T(8,128)(2,1)S(1)} %collective-permute-done.33.refs_2_), channel_id=1, source_target_pairs={{0,4},{4,0},{8,12},{12,8},{16,20},{20,16},{24,28},{28,24},{1,5},{5... | collective-permute-start | bytes 786440 | tf_op jit(solution)/shard_map/ppermute | solution.py:775
  (48 other events, 506.9 us)

commit v3 on v2

--- a/solution.py
+++ b/solution.py
@@ -13,6 +13,7 @@
 HD = 64
 LANES = 128
 BLOCKS = 4
+FWD_BLOCKS = 2
 
 eps = 1e-05
 big_negative = -1e30
@@ -203,8 +204,8 @@
 
     lane_lo = lanes < HD
     scale = HD ** (-0.5)
-    half = length // BLOCKS
-    for block in range(BLOCKS):
+    half = length // FWD_BLOCKS
+    for block in range(FWD_BLOCKS):
         lo, hi = block * half, (block + 1) * half
         out = jnp.zeros((half, LANES), f32)
         stats = []
@@ -247,7 +248,7 @@
         uu = xc * pair_columns(dt, pair, lanes)
         u_lo = jnp.where(lane_lo, uu, 0.0).astype(bf16)
         u_hi = jnp.where(lane_lo, 0.0, uu).astype(bf16)
-        for block in range(BLOCKS):
+        for block in range(FWD_BLOCKS):
             lo, hi = block * half, (block + 1) * half
             total = jnp.zeros((half, LANES), f32)
             for side, masked in ((0, u_lo), (1, u_hi)):
@@ -1141,7 +1142,7 @@
     )
     grad_step = grad_step.T
     grad_oinput, grad_skip, grad_sbias, grad_dlog, mixers_grad, feedforward_grad, grad_ostate = (
-        value[0]
+        value.reshape(-1)
         for value in (
             grad_oinput, grad_skip, grad_sbias, grad_dlog, mixers_grad, feedforward_grad, grad_ostate
         )

time: 267 us -> 267 us (level)
  no operation moved by 1% of the time
where the time goes in v3:
time: 267 us; the launch traced here: 266 us
  waiting for transfers between devices  135 us (51%)
  starting transfers between devices  62.8 us (24%)
  Pallas kernels  51.6 us (19%)
  local copies, waits for them, and re-layouts  9.25 us (3%)
  other arithmetic  5.01 us (2%)
    ppermute x59, waiting for transfers between devices, swap(): return lax.ppermute(value, axis, xor_pairs(size, bit))  135 us
    ppermute x59, starting transfers between devices, swap(): return lax.ppermute(value, axis, xor_pairs(size, bit))  62.8 us
    pallas_call x19, Pallas kernels, call_kernel(): pl.pallas_call(body, in_specs=[pl.BlockSpec(memory_space=pltpu.SMEM)] + [...  51.6 us
  transfers between devices with their start and end apart: 59, of which 29 were waited for; matrix products, arithmetic and copies ran while one was open for 4% of the time, Pallas kernels for 14%

profile of v3, /device:TPU:0, one launch (start us, length us, event | category | flops | bytes accessed | tf_op | source)
XLA Modules:
  0.0 266.5 jit_solution(15381541786320238622)
XLA Ops:
  0.7 3.1 %collective-permute-start = (bf16[128,1024]{1,0:T(8,128)(2,1)}, bf16[128,1024]{1,0:T(8,128)(2,1)S(1)}, u32[]{:S(2)}, u32[]{:S(2)}) collective-permute-start(bf16[128,1024]{1,0:T(8,128)(2,1)} %refs_3_.3), channel_id=1, source_target_pairs={{0,1},{1,0},{2,3},{3,2},{4,5},{5,4},{6,7},{7,6},{8,9},{9,8},{10,11... | collective-permute-start | bytes 786440 | tf_op jit(solution)/shard_map/ppermute | solution.py:776
  3.8 2.6 collective-permute-start.1
  9.8 8.7 %collective-permute-done.1.refs_3_ = bf16[128,1024]{1,0:T(8,128)(2,1)} collective-permute-done((bf16[128,1024]{1,0:T(8,128)(2,1)}, bf16[128,1024]{1,0:T(8,128)(2,1)}, u32[]{:S(2)}, u32[]{:S(2)}) %collective-permute-start.1) | collective-permute-done | bytes 262176 | tf_op jit(solution)/shard_map/ppermute | solution.py:776
  26.2 10.3 %shard_map.408 = (bf16[512,1024]{1,0:T(8,128)(2,1)S(1)}, bf16[512,384]{1,0:T(8,128)(2,1)S(1)}, bf16[512,128]{1,0:T(8,128)(2,1)S(1)}, f32[512,128]{1,0:T(8,128)S(...) custom-call(s32[2]{0:T(128)S(1)} %compare_select_fusion.t_ref.refs_0, ...), custom_call_target="tpu_custom_call" | custom-call | tf_op jit(solution)/shard_map/pallas_call | solution.py:743
  40.5 10.9 %collective-permute-done.3 = bf16[128,1024]{1,0:T(8,128)(2,1)S(1)} collective-permute-done((bf16[128,1024]{1,0:T(8,128)(2,1)S(1)}, bf16[128,1024]{1,0:T(8,128)(2,1)S(1)}, u32[]{:S(2)}, u32[]{:S(2)}) %collective-permute-start.3) | collective-permute-done | bytes 262176 | tf_op jit(solution)/shard_map/ppermute | solution.py:776
  53.7 9.8 %collective-permute-done.5 = bf16[128,1024]{1,0:T(8,128)(2,1)S(1)} collective-permute-done((bf16[128,1024]{1,0:T(8,128)(2,1)S(1)}, bf16[128,1024]{1,0:T(8,128)(2,1)S(1)}, u32[]{:S(2)}, u32[]{:S(2)}) %collective-permute-start.5) | collective-permute-done | bytes 262176 | tf_op jit(solution)/shard_map/ppermute | solution.py:776
  65.2 6.8 %collective-permute-done.8 = bf16[128,1024]{1,0:T(8,128)(2,1)S(1)} collective-permute-done((bf16[128,1024]{1,0:T(8,128)(2,1)S(1)}, bf16[128,1024]{1,0:T(8,128)(2,1)S(1)}, u32[]{:S(2)}, u32[]{:S(2)}) %collective-permute-start.8) | collective-permute-done | bytes 262176 | tf_op jit(solution)/shard_map/ppermute | solution.py:776
  72.1 5.7 %collective-permute-done.7.refs_2_ = bf16[128,1024]{1,0:T(8,128)(2,1)S(1)} collective-permute-done((bf16[128,1024]{1,0:T(8,128)(2,1)S(1)}, bf16[128,1024]{1,0:T(8,128)(2,1)S(1)}, u32[]{:S(2)}, u32[]{:S(2)}) %collective-permute-start.7) | collective-permute-done | bytes 262176 | tf_op jit(solution)/shard_map/ppermute | solution.py:776
  80.3 5.9 %collective-permute-done.10.refs_0_ = bf16[128,1024]{1,0:T(8,128)(2,1)S(1)} collective-permute-done((bf16[128,1024]{1,0:T(8,128)(2,1)S(1)}, bf16[128,1024]{1,0:T(8,128)(2,1)S(1)}, u32[]{:S(2)}, u32[]{:S(2)}) %collective-permute-start.10) | collective-permute-done | bytes 262176 | tf_op jit(solution)/shard_map/ppermute | solution.py:776
  91.5 2.7 %shard_map.409 = (bf16[384,1024]{1,0:T(8,128)(2,1)S(1)}, bf16[384,512]{1,0:T(8,128)(2,1)S(1)}, bf16[384,1024]{1,0:T(8,128)(2,1)S(1)}, bf16[128,1024]{1,0:T(8,128...) custom-call(s32[2]{0:T(128)S(1)} %compare_select_fusion.t_ref.refs_0_.scalar.d_ref.u_ref, ...), custom_call_target="tpu_custom_call" | custom-call | tf_op jit(solution)/shard_map/pallas_call | solution.py:743
  95.3 3.6 %collective-permute-done.15 = bf16[128,1024]{1,0:T(8,128)(2,1)S(1)} collective-permute-done((bf16[128,1024]{1,0:T(8,128)(2,1)S(1)}, bf16[128,1024]{1,0:T(8,128)(2,1)S(1)}, u32[]{:S(2)}, u32[]{:S(2)}) %collective-permute-start.15) | collective-permute-done | bytes 262176 | tf_op jit(solution)/shard_map/ppermute | solution.py:776
  100.8 3.2 %shard_map.422 = (bf16[768,1024]{1,0:T(8,128)(2,1)S(1)}, bf16[768,1024]{1,0:T(8,128)(2,1)S(1)}) custom-call(s32[2]{0:T(128)S(1)} %compare_select_fusion.t_ref.refs_0_.scalar.d_ref.u_ref, bf16[384,1024]{1,0:T(8,128)(2,1)S(1)} %get-tuple-element.192.refs_0_, bf16[128,1024]{1,0:T(8,128)(2,1)S(1)} %get-tuple-element.193.refs_1_, ...), custom_call_target="tpu_custom_call" | custom-call | tf_op jit(solution)/shard_map/pallas_call | solution.py:743
  104.0 5.0 %collective-permute-done.16 = bf16[128,1024]{1,0:T(8,128)(2,1)S(1)} collective-permute-done((bf16[128,1024]{1,0:T(8,128)(2,1)S(1)}, bf16[128,1024]{1,0:T(8,128)(2,1)S(1)}, u32[]{:S(2)}, u32[]{:S(2)}) %collective-permute-start.16) | collective-permute-done | bytes 262176 | tf_op jit(solution)/shard_map/ppermute | solution.py:776
  110.4 6.7 %collective-permute-start.18 = (bf16[128,1024]{1,0:T(8,128)(2,1)S(1)}, bf16[128,1024]{1,0:T(8,128)(2,1)S(1)}, u32[]{:S(2)}, u32[]{:S(2)}) collective-permute-start(bf16[128,1024]{1,0:T(8,128)(2,1)S(1)} %get-tuple-element.207.refs_1_), channel_id=1, source_target_pairs={{0,1},{1,0},{2,3},{3,2},{4,5},{5,4},{6,7},{7,6},{8,9},{9,8},{10,11... | collective-permute-start | bytes 786440 | tf_op jit(solution)/shard_map/ppermute | solution.py:776
  117.8 6.0 %collective-permute-start.20 = (bf16[128,1024]{1,0:T(8,128)(2,1)S(1)}, bf16[128,1024]{1,0:T(8,128)(2,1)S(1)}, u32[]{:S(2)}, u32[]{:S(2)}) collective-permute-start(bf16[128,1024]{1,0:T(8,128)(2,1)S(1)} %collective-permute-done.19.refs_3_), channel_id=1, source_target_pairs={{0,1},{1,0},{2,3},{3,2},{4,5},{5,4},{6,7},{7,6},{8,9},{9,8},{10,11... | collective-permute-start | bytes 786440 | tf_op jit(solution)/shard_map/ppermute | solution.py:776
  123.9 3.1 %shard_map.411 = (f32[2,512,512]{2,1,0:T(8,128)S(1)}, f32[6,512,512]{2,1,0:T(8,128)S(1)}, bf16[6,512,512]{2,1,0:T(8,128)(2,1)S(1)}, f32[512,640]{1,0:T(8,128)S(1...) custom-call(s32[2]{0:T(128)S(1)} %compare_select_fusion.t_ref.refs_0, ...), custom_call_target="tpu_custom_call" | custom-call | tf_op jit(solution)/shard_map/pallas_call | solution.py:743
  128.2 5.0 %shard_map.412 = (bf16[512,640]{1,0:T(8,128)(2,1)S(1)}, f32[512,384]{1,0:T(8,128)S(1)}, bf16[512,1024]{1,0:T(8,128)(2,1)S(1)}, bf16[512,1024]{1,0:T(8,128)(2,1)S(1)}) custom-call(s32[2]{0:T(128)S(1)} %compare_select_fusion.t_ref.refs_0_.scalar.d_ref.u_ref, bf16[128,1024]{1,0:T(8,128)(2,1)S(1)} %get-tuple-element.207.refs_1_, ...), custom_call_target="tpu_custom_call" | custom-call | tf_op jit(solution)/shard_map/pallas_call | solution.py:743
  133.2 8.1 %shard_map.413 = (bf16[512,896]{1,0:T(8,128)(2,1)S(1)}, bf16[512,896]{1,0:T(8,128)(2,1)S(1)}, bf16[128,1024]{1,0:T(8,128)(2,1)S(1)}, bf16[128,1024]{1,0:T(8,128)...) custom-call(s32[2]{0:T(128)S(1)} %compare_select_fusion.t_ref.refs_0_.scalar.d_ref.u_ref, ...), custom_call_target="tpu_custom_call" | custom-call | tf_op jit(solution)/shard_map/pallas_call | solution.py:743
  145.0 6.5 %collective-permute-done.12 = bf16[128,1024]{1,0:T(8,128)(2,1)S(1)} collective-permute-done((bf16[128,1024]{1,0:T(8,128)(2,1)S(1)}, bf16[128,1024]{1,0:T(8,128)(2,1)S(1)}, u32[]{:S(2)}, u32[]{:S(2)}) %collective-permute-start.12) | collective-permute-done | bytes 262176 | tf_op jit(solution)/shard_map/ppermute | solution.py:776
  161.6 3.6 %collective-permute-done.13 = bf16[128,1024]{1,0:T(8,128)(2,1)S(1)} collective-permute-done((bf16[128,1024]{1,0:T(8,128)(2,1)S(1)}, bf16[128,1024]{1,0:T(8,128)(2,1)S(1)}, u32[]{:S(2)}, u32[]{:S(2)}) %collective-permute-start.13) | collective-permute-done | bytes 262176 | tf_op jit(solution)/shard_map/ppermute | solution.py:776
  169.7 15.3 %collective-permute-done.27.refs_3_ = bf16[128,896]{1,0:T(8,128)(2,1)S(1)} collective-permute-done((bf16[128,896]{1,0:T(8,128)(2,1)S(1)}, bf16[128,896]{1,0:T(8,128)(2,1)S(1)}, u32[]{:S(2)}, u32[]{:S(2)}) %collective-permute-start.27) | collective-permute-done | bytes 229408 | tf_op jit(solution)/shard_map/ppermute | solution.py:776
  199.5 10.6 %collective-permute-done.40.refs_3_ = bf16[128,1024]{1,0:T(8,128)(2,1)S(1)} collective-permute-done((bf16[128,1024]{1,0:T(8,128)(2,1)S(1)}, bf16[128,1024]{1,0:T(8,128)(2,1)S(1)}, u32[]{:S(2)}, u32[]{:S(2)}) %collective-permute-start.40) | collective-permute-done | bytes 262176 | tf_op jit(solution)/shard_map/ppermute | solution.py:776
  210.1 2.3 collective-permute-start.29
  215.1 8.4 %collective-permute-done.53.refs_2_ = bf16[192,1024]{1,0:T(8,128)(2,1)S(1)} collective-permute-done((bf16[192,1024]{1,0:T(8,128)(2,1)S(1)}, bf16[192,1024]{1,0:T(8,128)(2,1)S(1)}, u32[]{:S(2)}, u32[]{:S(2)}) %collective-permute-start.53) | collective-permute-done | bytes 393248 | tf_op jit(solution)/shard_map/ppermute | solution.py:776
  224.3 3.5 %collective-permute-start.31 = (bf16[128,1024]{1,0:T(8,128)(2,1)S(1)}, bf16[128,1024]{1,0:T(8,128)(2,1)S(1)}, u32[]{:S(2)}, u32[]{:S(2)}) collective-permute-start(bf16[128,1024]{1,0:T(8,128)(2,1)S(1)} %shard_map.416.refs_0_), channel_id=1, source_target_pairs={{0,8},{4,12},{8,0},{12,4},{16,24},{20,28},{24,16},{28,20},{1,9},{5... | collective-permute-start | bytes 786440 | tf_op jit(solution)/shard_map/ppermute | solution.py:776
  228.0 5.5 %collective-permute-done.42.refs_2_ = bf16[128,1024]{1,0:T(8,128)(2,1)S(1)} collective-permute-done((bf16[128,1024]{1,0:T(8,128)(2,1)S(1)}, bf16[128,1024]{1,0:T(8,128)(2,1)S(1)}, u32[]{:S(2)}, u32[]{:S(2)}) %collective-permute-start.42) | collective-permute-done | bytes 262176 | tf_op jit(solution)/shard_map/ppermute | solution.py:776
  233.6 5.6 %collective-permute-done.31.refs_1_ = bf16[128,1024]{1,0:T(8,128)(2,1)S(1)} collective-permute-done((bf16[128,1024]{1,0:T(8,128)(2,1)S(1)}, bf16[128,1024]{1,0:T(8,128)(2,1)S(1)}, u32[]{:S(2)}, u32[]{:S(2)}) %collective-permute-start.31) | collective-permute-done | bytes 262176 | tf_op jit(solution)/shard_map/ppermute | solution.py:776
  239.2 5.0 %collective-permute-done.33.refs_2_ = bf16[128,1024]{1,0:T(8,128)(2,1)S(1)} collective-permute-done((bf16[128,1024]{1,0:T(8,128)(2,1)S(1)}, bf16[128,1024]{1,0:T(8,128)(2,1)S(1)}, u32[]{:S(2)}, u32[]{:S(2)}) %collective-permute-start.33) | collective-permute-done | bytes 262176 | tf_op jit(solution)/shard_map/ppermute | solution.py:776
  247.5 3.4 %shard_map.425 = (f32[1024,512]{1,0:T(8,128)}, f32[1024,512]{1,0:T(8,128)}, f32[512,1024]{1,0:T(8,128)}) custom-call(s32[2]{0:T(128)S(1)} %compare_select_fusion.t_ref.refs_0_.scalar.d_ref.u_ref, bf16[192,1024]{1,0:T(8,128)(2,1)S(1)} %shard_map.424.refs_0_, bf16[192,1024]{1,0:T(8,128)(2,1)S(1)} %collective-permute-done.52.refs_1_, ...), custom_call_target="tpu_custom_call" | custom-call | tf_op jit(solution)/shard_map/pallas_call | solution.py:743
  250.9 3.1 %shard_map.421 = (f32[128,1024]{1,0:T(8,128)}, f32[384,1024]{1,0:T(8,128)}, f32[1024,384]{1,0:T(8,128)}, f32[1024,128]{1,0:T(8,128)}) custom-call(s32[2]{0:T(128)S(1)} %compare_select_fusion.t_ref.refs_0_.scalar.d_ref.u_ref, bf16[128,1024]{1,0:T(8,128)(2,1)S(1)} %shard_map.420.refs_0_, bf16[128,1024]{1,0:T(8,128)(2,1)S(1)} %collective-permute-done.41.refs_1_, ...), custom_call_target="tpu_custom_call" | custom-call | tf_op jit(solution)/shard_map/pallas_call | solution.py:743
  254.1 5.8 %collective-permute-done.22.refs_1_ = bf16[128,1024]{1,0:T(8,128)(2,1)S(1)} collective-permute-done((bf16[128,1024]{1,0:T(8,128)(2,1)S(1)}, bf16[128,1024]{1,0:T(8,128)(2,1)S(1)}, u32[]{:S(2)}, u32[]{:S(2)}) %collective-permute-start.22) | collective-permute-done | bytes 262176 | tf_op jit(solution)/shard_map/ppermute | solution.py:776
  259.9 3.3 %shard_map.418 = (f32[1024,128]{1,0:T(8,128)}, f32[1024,128]{1,0:T(8,128)}, f32[1024,256]{1,0:T(8,128)}, f32[1024,384]{1,0:T(8,128)}, f32[6,1024]{1,0:T(8,128)},...) custom-call(s32[2]{0:T(128)S(1)} %compare_select_fusion.t_ref.refs_0, ...), custom_call_target="tpu_custom_call" | custom-call | tf_op jit(solution)/shard_map/pallas_call | solution.py:743
  (181 shorter events, 76.0 us)
Async XLA Ops:
  0.7 23.6 %collective-permute-start = (bf16[128,1024]{1,0:T(8,128)(2,1)}, bf16[128,1024]{1,0:T(8,128)(2,1)S(1)}, u32[]{:S(2)}, u32[]{:S(2)}) collective-permute-start(bf16[128,1024]{1,0:T(8,128)(2,1)} %refs_3_.3), channel_id=1, source_target_pairs={{0,1},{1,0},{2,3},{3,2},{4,5},{5,4},{6,7},{7,6},{8,9},{9,8},{10,11... | collective-permute-start | bytes 786440 | tf_op jit(solution)/shard_map/ppermute | solution.py:776
  3.8 14.7 %collective-permute-start.1 = (bf16[128,1024]{1,0:T(8,128)(2,1)}, bf16[128,1024]{1,0:T(8,128)(2,1)}, u32[]{:S(2)}, u32[]{:S(2)}) collective-permute-start(bf16[128,1024]{1,0:T(8,128)(2,1)} %refs_3_.3), channel_id=1, source_target_pairs={{0,2},{1,3},{2,0},{3,1},{4,6},{5,7},{6,4},{7,5},{8,10},{9,11},{10,... | collective-permute-start | bytes 786440 | tf_op jit(solution)/shard_map/ppermute | solution.py:776
  36.6 14.9 %collective-permute-start.3 = (bf16[128,1024]{1,0:T(8,128)(2,1)S(1)}, bf16[128,1024]{1,0:T(8,128)(2,1)S(1)}, u32[]{:S(2)}, u32[]{:S(2)}) collective-permute-start(bf16[128,1024]{1,0:T(8,128)(2,1)S(1)} %get-tuple-element.119), channel_id=1, source_target_pairs={{0,1},{1,0},{2,3},{3,2},{4,5},{5,4},{6,7},{7,6},{8,9},{9,8},{10,11... | collective-permute-start | bytes 786440 | tf_op jit(solution)/shard_map/ppermute | solution.py:776
  37.8 15.7 %collective-permute-start.9 = (bf16[128,1024]{1,0:T(8,128)(2,1)S(1)}, bf16[128,1024]{1,0:T(8,128)(2,1)S(1)}, u32[]{:S(2)}, u32[]{:S(2)}) collective-permute-start(bf16[128,1024]{1,0:T(8,128)(2,1)S(1)} %copy-done.19), channel_id=1, source_target_pairs={{0,2},{1,3},{2,0},{3,1},{4,6},{5,7},{6,4},{7,5},{8,10},{9,11},{10,... | collective-permute-start | bytes 786440 | tf_op jit(solution)/shard_map/ppermute | solution.py:776
  39.7 23.8 %collective-permute-start.5 = (bf16[128,1024]{1,0:T(8,128)(2,1)S(1)}, bf16[128,1024]{1,0:T(8,128)(2,1)S(1)}, u32[]{:S(2)}, u32[]{:S(2)}) collective-permute-start(bf16[128,1024]{1,0:T(8,128)(2,1)S(1)} %get-tuple-element.120), channel_id=1, source_target_pairs={{0,1},{1,0},{2,3},{3,2},{4,5},{5,4},{6,7},{7,6},{8,9},{9,8},{10,11... | collective-permute-start | bytes 786440 | tf_op jit(solution)/shard_map/ppermute | solution.py:776
  51.6 20.4 %collective-permute-start.8 = (bf16[128,1024]{1,0:T(8,128)(2,1)S(1)}, bf16[128,1024]{1,0:T(8,128)(2,1)S(1)}, u32[]{:S(2)}, u32[]{:S(2)}) collective-permute-start(bf16[128,1024]{1,0:T(8,128)(2,1)S(1)} %copy-done.19), channel_id=1, source_target_pairs={{0,1},{1,0},{2,3},{3,2},{4,5},{5,4},{6,7},{7,6},{8,9},{9,8},{10,11... | collective-permute-start | bytes 786440 | tf_op jit(solution)/shard_map/ppermute | solution.py:776
  53.6 24.2 %collective-permute-start.11 = (bf16[128,1024]{1,0:T(8,128)(2,1)S(1)}, bf16[128,1024]{1,0:T(8,128)(2,1)S(1)}, u32[]{:S(2)}, u32[]{:S(2)}) collective-permute-start(bf16[128,1024]{1,0:T(8,128)(2,1)S(1)} %collective-permute-done.9), channel_id=1, source_target_pairs={{0,1},{1,0},{2,3},{3,2},{4,5},{5,4},{6,7},{7,6},{8,9},{9,8},{10,11... | collective-permute-start | bytes 786440 | tf_op jit(solution)/shard_map/ppermute | solution.py:776
  63.9 13.8 %collective-permute-start.7 = (bf16[128,1024]{1,0:T(8,128)(2,1)S(1)}, bf16[128,1024]{1,0:T(8,128)(2,1)S(1)}, u32[]{:S(2)}, u32[]{:S(2)}) collective-permute-start(bf16[128,1024]{1,0:T(8,128)(2,1)S(1)} %multiply_convert_fusion.refs_0_), channel_id=1, source_target_pairs={{0,2},{1,3},{2,0},{3,1},{4,6},{5,7},{6,4},{7,5},{8,10},{9,11},{10,... | collective-permute-start | bytes 786440 | tf_op jit(solution)/shard_map/ppermute | solution.py:776
  104.0 51.6 %collective-permute-start.48 = (bf16[768,1024]{1,0:T(8,128)(2,1)S(1)}, bf16[768,1024]{1,0:T(8,128)(2,1)S(1)}, u32[]{:S(2)}, u32[]{:S(2)}) collective-permute-start(bf16[768,1024]{1,0:T(8,128)(2,1)S(1)} %get-tuple-element.197), channel_id=1, source_target_pairs={{0,4},{4,0},{8,12},{12,8},{16,20},{20,16},{24,28},{28,24},{1,5},{5... | collective-permute-start | bytes 4718600 | tf_op jit(solution)/shard_map/ppermute | solution.py:776
  110.4 16.5 %collective-permute-start.18 = (bf16[128,1024]{1,0:T(8,128)(2,1)S(1)}, bf16[128,1024]{1,0:T(8,128)(2,1)S(1)}, u32[]{:S(2)}, u32[]{:S(2)}) collective-permute-start(bf16[128,1024]{1,0:T(8,128)(2,1)S(1)} %get-tuple-element.207.refs_1_), channel_id=1, source_target_pairs={{0,1},{1,0},{2,3},{3,2},{4,5},{5,4},{6,7},{7,6},{8,9},{9,8},{10,11... | collective-permute-start | bytes 786440 | tf_op jit(solution)/shard_map/ppermute | solution.py:776
  141.4 25.4 %collective-permute-start.37 = (bf16[512,1024]{1,0:T(8,128)(2,1)S(1)}, bf16[512,1024]{1,0:T(8,128)(2,1)S(1)}, u32[]{:S(2)}, u32[]{:S(2)}) collective-permute-start(bf16[512,1024]{1,0:T(8,128)(2,1)S(1)} %get-tuple-element.170), channel_id=1, source_target_pairs={{0,4},{4,0},{8,12},{12,8},{16,20},{20,16},{24,28},{28,24},{1,5},{5... | collective-permute-start | bytes 3145736 | tf_op jit(solution)/shard_map/ppermute | solution.py:776
  144.9 15.2 %collective-permute-start.14 = (bf16[128,1024]{1,0:T(8,128)(2,1)S(1)}, bf16[128,1024]{1,0:T(8,128)(2,1)S(1)}, u32[]{:S(2)}, u32[]{:S(2)}) collective-permute-start(bf16[128,1024]{1,0:T(8,128)(2,1)S(1)} %slice.14), channel_id=1, source_target_pairs={{0,1},{1,0},{2,3},{3,2},{4,5},{5,4},{6,7},{7,6},{8,9},{9,8},{10,11... | collective-permute-start | bytes 786440 | tf_op jit(solution)/shard_map/ppermute | solution.py:776
  151.5 13.7 %collective-permute-start.13 = (bf16[128,1024]{1,0:T(8,128)(2,1)S(1)}, bf16[128,1024]{1,0:T(8,128)(2,1)S(1)}, u32[]{:S(2)}, u32[]{:S(2)}) collective-permute-start(bf16[128,1024]{1,0:T(8,128)(2,1)S(1)} %add_convert_fusion.3), channel_id=1, source_target_pairs={{0,2},{1,3},{2,0},{3,1},{4,6},{5,7},{6,4},{7,5},{8,10},{9,11},{10,... | collective-permute-start | bytes 786440 | tf_op jit(solution)/shard_map/ppermute | solution.py:776
  154.0 14.1 %collective-permute-start.25 = (bf16[128,896]{1,0:T(8,128)(2,1)S(1)}, bf16[128,896]{1,0:T(8,128)(2,1)S(1)}, u32[]{:S(2)}, u32[]{:S(2)}) collective-permute-start(bf16[128,896]{1,0:T(8,128)(2,1)S(1)} %get-tuple-element.160), channel_id=1, source_target_pairs={{0,8},{4,12},{8,0},{12,4},{16,24},{20,28},{24,16},{28,20},{1,9},{5... | collective-permute-start | bytes 688136 | tf_op jit(solution)/shard_map/ppermute | solution.py:776
  155.6 14.1 %collective-permute-start.26 = (bf16[128,896]{1,0:T(8,128)(2,1)S(1)}, bf16[128,896]{1,0:T(8,128)(2,1)S(1)}, u32[]{:S(2)}, u32[]{:S(2)}) collective-permute-start(bf16[128,896]{1,0:T(8,128)(2,1)S(1)} %get-tuple-element.161), channel_id=1, source_target_pairs={{0,16},{4,20},{8,24},{12,28},{16,0},{20,4},{24,8},{28,12},{1,17},{... | collective-permute-start | bytes 688136 | tf_op jit(solution)/shard_map/ppermute | solution.py:776
  160.1 26.4 %collective-permute-start.49 = (bf16[192,1024]{1,0:T(8,128)(2,1)S(1)}, bf16[192,1024]{1,0:T(8,128)(2,1)S(1)}, u32[]{:S(2)}, u32[]{:S(2)}) collective-permute-start(bf16[192,1024]{1,0:T(8,128)(2,1)S(1)} %get-tuple-element.199), channel_id=1, source_target_pairs={{0,8},{4,12},{8,0},{12,4},{16,24},{20,28},{24,16},{28,20},{1,9},{5... | collective-permute-start | bytes 1179656 | tf_op jit(solution)/shard_map/ppermute | solution.py:776
  165.2 22.8 %collective-permute-start.50 = (bf16[192,1024]{1,0:T(8,128)(2,1)S(1)}, bf16[192,1024]{1,0:T(8,128)(2,1)S(1)}, u32[]{:S(2)}, u32[]{:S(2)}) collective-permute-start(bf16[192,1024]{1,0:T(8,128)(2,1)S(1)} %get-tuple-element.200), channel_id=1, source_target_pairs={{0,16},{4,20},{8,24},{12,28},{16,0},{20,4},{24,8},{28,12},{1,17},{... | collective-permute-start | bytes 1179656 | tf_op jit(solution)/shard_map/ppermute | solution.py:776
  166.8 23.3 %collective-permute-start.51 = (bf16[192,1024]{1,0:T(8,128)(2,1)S(1)}, bf16[192,1024]{1,0:T(8,128)(2,1)S(1)}, u32[]{:S(2)}, u32[]{:S(2)}) collective-permute-start(bf16[192,1024]{1,0:T(8,128)(2,1)S(1)} %get-tuple-element.201), channel_id=1, source_target_pairs={{0,24},{4,28},{8,16},{12,20},{16,8},{20,12},{24,0},{28,4},{1,25},{... | collective-permute-start | bytes 1179656 | tf_op jit(solution)/shard_map/ppermute | solution.py:776
  168.2 16.8 %collective-permute-start.27 = (bf16[128,896]{1,0:T(8,128)(2,1)S(1)}, bf16[128,896]{1,0:T(8,128)(2,1)S(1)}, u32[]{:S(2)}, u32[]{:S(2)}) collective-permute-start(bf16[128,896]{1,0:T(8,128)(2,1)S(1)} %get-tuple-element.162), channel_id=1, source_target_pairs={{0,24},{4,28},{8,16},{12,20},{16,8},{20,12},{24,0},{28,4},{1,25},{... | collective-permute-start | bytes 688136 | tf_op jit(solution)/shard_map/ppermute | solution.py:776
  169.7 21.6 %collective-permute-start.21 = (bf16[128,1024]{1,0:T(8,128)(2,1)S(1)}, bf16[128,1024]{1,0:T(8,128)(2,1)S(1)}, u32[]{:S(2)}, u32[]{:S(2)}) collective-permute-start(bf16[128,1024]{1,0:T(8,128)(2,1)S(1)} %get-tuple-element.155), channel_id=1, source_target_pairs={{0,1},{1,0},{2,3},{3,2},{4,5},{5,4},{6,7},{7,6},{8,9},{9,8},{10,11... | collective-permute-start | bytes 786440 | tf_op jit(solution)/shard_map/ppermute | solution.py:776
  191.3 21.7 %collective-permute-start.52 = (bf16[192,1024]{1,0:T(8,128)(2,1)S(1)}, bf16[192,1024]{1,0:T(8,128)(2,1)S(1)}, u32[]{:S(2)}, u32[]{:S(2)}) collective-permute-start(bf16[192,1024]{1,0:T(8,128)(2,1)S(1)} %shard_map.424.refs_0_), channel_id=1, source_target_pairs={{0,8},{4,12},{8,0},{12,4},{16,24},{20,28},{24,16},{28,20},{1,9},{5... | collective-permute-start | bytes 1179656 | tf_op jit(solution)/shard_map/ppermute | solution.py:776
  193.9 29.6 %collective-permute-start.53 = (bf16[192,1024]{1,0:T(8,128)(2,1)S(1)}, bf16[192,1024]{1,0:T(8,128)(2,1)S(1)}, u32[]{:S(2)}, u32[]{:S(2)}) collective-permute-start(bf16[192,1024]{1,0:T(8,128)(2,1)S(1)} %shard_map.424.refs_0_), channel_id=1, source_target_pairs={{0,16},{4,20},{8,24},{12,28},{16,0},{20,4},{24,8},{28,12},{1,17},{... | collective-permute-start | bytes 1179656 | tf_op jit(solution)/shard_map/ppermute | solution.py:776
  194.6 15.4 %collective-permute-start.40 = (bf16[128,1024]{1,0:T(8,128)(2,1)S(1)}, bf16[128,1024]{1,0:T(8,128)(2,1)S(1)}, u32[]{:S(2)}, u32[]{:S(2)}) collective-permute-start(bf16[128,1024]{1,0:T(8,128)(2,1)S(1)} %get-tuple-element.174), channel_id=1, source_target_pairs={{0,24},{4,28},{8,16},{12,20},{16,8},{20,12},{24,0},{28,4},{1,25},{... | collective-permute-start | bytes 786440 | tf_op jit(solution)/shard_map/ppermute | solution.py:776
  196.9 27.3 %collective-permute-start.54 = (bf16[192,1024]{1,0:T(8,128)(2,1)S(1)}, bf16[192,1024]{1,0:T(8,128)(2,1)S(1)}, u32[]{:S(2)}, u32[]{:S(2)}) collective-permute-start(bf16[192,1024]{1,0:T(8,128)(2,1)S(1)} %shard_map.424.refs_0_), channel_id=1, source_target_pairs={{0,24},{4,28},{8,16},{12,20},{16,8},{20,12},{24,0},{28,4},{1,25},{... | collective-permute-start | bytes 1179656 | tf_op jit(solution)/shard_map/ppermute | solution.py:776
  199.4 24.9 %collective-permute-start.55 = (bf16[192,1024]{1,0:T(8,128)(2,1)S(1)}, bf16[192,1024]{1,0:T(8,128)(2,1)S(1)}, u32[]{:S(2)}, u32[]{:S(2)}) collective-permute-start(bf16[192,1024]{1,0:T(8,128)(2,1)S(1)} %shard_map.424.refs_0_), channel_id=1, source_target_pairs={{0,4},{4,0},{8,12},{12,8},{16,20},{20,16},{24,28},{28,24},{1,5},{5... | collective-permute-start | bytes 1179656 | tf_op jit(solution)/shard_map/ppermute | solution.py:776
  213.1 14.7 %collective-permute-start.41 = (bf16[128,1024]{1,0:T(8,128)(2,1)S(1)}, bf16[128,1024]{1,0:T(8,128)(2,1)S(1)}, u32[]{:S(2)}, u32[]{:S(2)}) collective-permute-start(bf16[128,1024]{1,0:T(8,128)(2,1)S(1)} %shard_map.420.refs_0_), channel_id=1, source_target_pairs={{0,8},{4,12},{8,0},{12,4},{16,24},{20,28},{24,16},{28,20},{1,9},{5... | collective-permute-start | bytes 786440 | tf_op jit(solution)/shard_map/ppermute | solution.py:776
  224.3 14.9 %collective-permute-start.31 = (bf16[128,1024]{1,0:T(8,128)(2,1)S(1)}, bf16[128,1024]{1,0:T(8,128)(2,1)S(1)}, u32[]{:S(2)}, u32[]{:S(2)}) collective-permute-start(bf16[128,1024]{1,0:T(8,128)(2,1)S(1)} %shard_map.416.refs_0_), channel_id=1, source_target_pairs={{0,8},{4,12},{8,0},{12,4},{16,24},{20,28},{24,16},{28,20},{1,9},{5... | collective-permute-start | bytes 786440 | tf_op jit(solution)/shard_map/ppermute | solution.py:776
  227.8 16.9 %collective-permute-start.56 = (bf16[192,1024]{1,0:T(8,128)(2,1)S(1)}, bf16[192,1024]{1,0:T(8,128)(2,1)S(1)}, u32[]{:S(2)}, u32[]{:S(2)}) collective-permute-start(bf16[192,1024]{1,0:T(8,128)(2,1)S(1)} %collective-permute-done.52.refs_1_), channel_id=1, source_target_pairs={{0,4},{4,0},{8,12},{12,8},{16,20},{20,16},{24,28},{28,24},{1,5},{5... | collective-permute-start | bytes 1179656 | tf_op jit(solution)/shard_map/ppermute | solution.py:776
  244.9 15.0 %collective-permute-start.22 = (bf16[128,1024]{1,0:T(8,128)(2,1)S(1)}, bf16[128,1024]{1,0:T(8,128)(2,1)S(1)}, u32[]{:S(2)}, u32[]{:S(2)}) collective-permute-start(bf16[128,1024]{1,0:T(8,128)(2,1)S(1)} %add_convert_fusion), channel_id=1, source_target_pairs={{0,2},{1,3},{2,0},{3,1},{4,6},{5,7},{6,4},{7,5},{8,10},{9,11},{10,... | collective-permute-start | bytes 786440 | tf_op jit(solution)/shard_map/ppermute | solution.py:776
  244.9 14.9 %collective-permute-start.30 = (bf16[128,1024]{1,0:T(8,128)(2,1)S(1)}, bf16[128,1024]{1,0:T(8,128)(2,1)S(1)}, u32[]{:S(2)}, u32[]{:S(2)}) collective-permute-start(bf16[128,1024]{1,0:T(8,128)(2,1)S(1)} %shard_map.416.refs_0_), channel_id=1, source_target_pairs={{0,4},{4,0},{8,12},{12,8},{16,20},{20,16},{24,28},{28,24},{1,5},{5... | collective-permute-start | bytes 786440 | tf_op jit(solution)/shard_map/ppermute | solution.py:776
  245.7 14.2 %collective-permute-start.32 = (bf16[128,1024]{1,0:T(8,128)(2,1)S(1)}, bf16[128,1024]{1,0:T(8,128)(2,1)S(1)}, u32[]{:S(2)}, u32[]{:S(2)}) collective-permute-start(bf16[128,1024]{1,0:T(8,128)(2,1)S(1)} %collective-permute-done.31.refs_1_), channel_id=1, source_target_pairs={{0,4},{4,0},{8,12},{12,8},{16,20},{20,16},{24,28},{28,24},{1,5},{5... | collective-permute-start | bytes 786440 | tf_op jit(solution)/shard_map/ppermute | solution.py:776
  246.1 13.8 %collective-permute-start.34 = (bf16[128,1024]{1,0:T(8,128)(2,1)S(1)}, bf16[128,1024]{1,0:T(8,128)(2,1)S(1)}, u32[]{:S(2)}, u32[]{:S(2)}) collective-permute-start(bf16[128,1024]{1,0:T(8,128)(2,1)S(1)} %collective-permute-done.33.refs_2_), channel_id=1, source_target_pairs={{0,4},{4,0},{8,12},{12,8},{16,20},{20,16},{24,28},{28,24},{1,5},{5... | collective-permute-start | bytes 786440 | tf_op jit(solution)/shard_map/ppermute | solution.py:776
  (48 other events, 506.2 us)
